TPU v7x, 256 devices: a whole 4x4x8 slice. The times are simulated.
256 devices in a mesh: frame: 16 (over x_hi, z), head: 8 (over y, core), dp: 2 (over x_lo).
Axes of the slice: x: 4 (x_hi: 2, x_lo: 2; x = x_hi * 2 + x_lo), y: 4, z: 8, core: 2. Of those that a mesh axis runs over, the one named last changes fastest.
Arguments:
- clip: bfloat16 [2, 4096, 256], P('dp', 'frame'), may hold values from -40 to 40
- block_ids: int32 [2, 4096], P('dp'), may hold values from 0 to 63, never falling along the last dimension, each value on 1 to 128 neighbouring positions
- w_spatial: bfloat16 [9, 256, 256], replicated, may hold values from -0.125 to 0.125
- w_temporal: bfloat16 [3, 256, 256], replicated, may hold values from -0.21875 to 0.21875
- w_query: bfloat16 [256, 2048], P(None, 'head'), may hold values from -0.375 to 0.375
- w_key: bfloat16 [256, 2048], P(None, 'head'), may hold values from -0.375 to 0.375
- w_value: bfloat16 [256, 2048], P(None, 'head'), may hold values from -0.375 to 0.375
- w_out: bfloat16 [2048, 256], P('head'), may hold values from -0.125 to 0.125
- cotangent: bfloat16 [2, 4096, 256], P('dp', 'frame'), may hold values from -6 to 6
Outputs:
- grad_spatial: float32 [9, 256, 256], replicated
- grad_temporal: float32 [3, 256, 256], replicated
- grad_query: float32 [256, 2048], P(None, 'head')
- grad_key: float32 [256, 2048], P(None, 'head')
- grad_value: float32 [256, 2048], P(None, 'head')
- grad_out: float32 [2048, 256], P('head')
Inputs may be any that keep to these rules, and one draw needn't show every extreme that they name: `block_ids`: block numbers never fall along a clip's tokens; every block has 1 to (128) tokens.
All inputs are finite; a program needn't handle non-finite values.
Results may differ from a plain program's by a relative error of at most 0.04.
Values may be sent and summed in bfloat16 or wider, within the bound.
No kernel may reach another device: no remote copies, remote signals or barrier semaphores. Data moves between devices by JAX's collectives and lax.ppermute only.
A program may use at most 128 MiB of HBM per device.

v0:
```python
import jax
import jax.numpy as jnp
from jax import lax
from jax.sharding import PartitionSpec as P

HD = 128
SIDE = 8


NEG_FILL = -1e30


def with_halo(cells, sides, width):
    for axis, dim in sides:
        count = lax.axis_size(axis)
        ends = count - 1
        head = lax.slice_in_dim(cells, 0, width, axis=dim)
        tail = lax.slice_in_dim(cells, cells.shape[dim] - width, cells.shape[dim], axis=dim)
        cells = jnp.concatenate(
            [
                lax.ppermute(tail, axis, [(i, (i + 1) % count) for i in range(ends)]),
                cells,
                lax.ppermute(head, axis, [((i + 1) % count, i) for i in range(ends)]),
            ],
            axis=dim,
        )
    return cells


def spatial_taps(frame_grid, side):
    padded = jnp.pad(frame_grid, ((0, 0), (1, 1), (1, 1), (0, 0)))
    count = frame_grid.shape[0] * side * side
    width = frame_grid.shape[3]
    return [
        padded[:, row_off : row_off + side, col_off : col_off + side, :].reshape(count, width)
        for row_off in range(3)
        for col_off in range(3)
    ]


def silu_slope(pre_act):
    sigma = jax.nn.sigmoid(pre_act)
    return sigma * (1.0 + pre_act * (1.0 - sigma))


def frame_rims(field):
    return with_halo(field, (("frame", 0),), SIDE * SIDE)


def take_head(matrix, which_head):
    return matrix[:, which_head * HD : (which_head + 1) * HD]


def contract_rows(left, right):
    return lax.dot_general(
        left, right, (((0,), (0,)), ((), ())), preferred_element_type=jnp.float32
    )


def on_device(clip, block_ids, w_spatial, w_temporal, w_query, w_key, w_value, w_out, cotangent):
    frames_in = clip[0]
    upstream = cotangent[0]
    clip_blocks = block_ids[0]
    tok_local, channels = frames_in.shape
    frame_len = SIDE * SIDE
    scale = HD ** (-0.5)
    grid = frames_in.reshape(tok_local // frame_len, SIDE, SIDE, channels)
    taps = spatial_taps(grid, SIDE)
    pre_act = jnp.zeros((tok_local, channels), jnp.float32)
    for offset in range(9):
        pre_act = pre_act + jnp.dot(
            taps[offset], w_spatial[offset], preferred_element_type=jnp.float32
        )
    hidden = jax.nn.silu(pre_act).astype(jnp.bfloat16)
    hidden_rim = frame_rims(hidden)
    temporal = jnp.zeros((tok_local, channels), jnp.float32)
    for offset in range(3):
        temporal = temporal + jnp.dot(
            hidden_rim[offset * frame_len : offset * frame_len + tok_local],
            w_temporal[offset],
            preferred_element_type=jnp.float32,
        )
    features = temporal.astype(jnp.bfloat16)
    queries_local = jnp.dot(features, w_query, preferred_element_type=jnp.float32).astype(
        jnp.bfloat16
    )
    keys_local = jnp.dot(features, w_key, preferred_element_type=jnp.float32).astype(jnp.bfloat16)
    values_local = jnp.dot(features, w_value, preferred_element_type=jnp.float32).astype(
        jnp.bfloat16
    )
    keys_every, values_every = (
        lax.all_gather(keys_local, "frame", axis=0, tiled=True),
        lax.all_gather(values_local, "frame", axis=0, tiled=True),
    )
    first_row = lax.axis_index("frame") * tok_local
    grad_attended = jnp.dot(upstream, w_out.T, preferred_element_type=jnp.float32).astype(
        jnp.bfloat16
    )
    queries_held, grad_held = (queries_local, grad_attended)
    held_blocks = lax.dynamic_slice_in_dim(clip_blocks, first_row, tok_local)
    visible = clip_blocks[None, :] <= held_blocks[:, None]
    heads_here = queries_local.shape[1] // HD
    width_here = queries_local.shape[1]
    attended_parts, grad_query_parts, prob_list, score_grads, norm_list, delta_list = (
        [],
        [],
        [],
        [],
        [],
        [],
    )
    for which_head in range(heads_here):
        query_head = take_head(queries_held, which_head)
        key_head = take_head(keys_every, which_head)
        value_head = take_head(values_every, which_head)
        grad_head = take_head(grad_held, which_head)
        scores = jnp.dot(query_head, key_head.T, preferred_element_type=jnp.float32) * scale
        masked = jnp.where(visible, scores, NEG_FILL)
        top = jnp.max(masked, axis=1, keepdims=True)
        total = jnp.sum(jnp.where(visible, jnp.exp(masked - top), 0.0), axis=1, keepdims=True)
        log_norm = top + jnp.log(total)
        probs = jnp.where(visible, jnp.exp(masked - log_norm), 0.0)
        probs_low = probs.astype(jnp.bfloat16)
        attended = jnp.dot(probs_low, value_head, preferred_element_type=jnp.float32).astype(
            jnp.bfloat16
        )
        delta = jnp.sum(
            grad_head.astype(jnp.float32) * attended.astype(jnp.float32), axis=1, keepdims=True
        )
        grad_probs = jnp.dot(grad_head, value_head.T, preferred_element_type=jnp.float32)
        grad_scores = (probs * (grad_probs - delta) * scale).astype(jnp.bfloat16)
        grad_query_parts.append(
            jnp.dot(grad_scores, key_head, preferred_element_type=jnp.float32).astype(jnp.bfloat16)
        )
        attended_parts.append(attended)
        prob_list.append(probs_low)
        score_grads.append(grad_scores)
        norm_list.append(log_norm)
        delta_list.append(delta)
    attended_all = jnp.concatenate(attended_parts, axis=1)
    grad_queries = jnp.concatenate(grad_query_parts, axis=1)
    key_parts = []
    value_parts = []
    for which_head in range(heads_here):
        score_cols = score_grads[which_head]
        prob_cols = prob_list[which_head]
        key_parts.append(contract_rows(score_cols, take_head(queries_held, which_head)))
        value_parts.append(contract_rows(prob_cols, take_head(grad_held, which_head)))
    summed = lax.psum_scatter(
        jnp.concatenate(key_parts + value_parts, axis=1), "frame", scatter_dimension=0, tiled=True
    )
    grad_keys = summed[:, :width_here].astype(jnp.bfloat16)
    grad_values = summed[:, width_here:].astype(jnp.bfloat16)
    grad_wq_local = contract_rows(features, grad_queries)
    grad_wk_local = contract_rows(features, grad_keys)
    grad_wv_local = contract_rows(features, grad_values)
    grad_wo_local = contract_rows(attended_all, upstream)
    back_part = jnp.dot(grad_queries, w_query.T, preferred_element_type=jnp.float32)
    back_part = back_part + jnp.dot(grad_keys, w_key.T, preferred_element_type=jnp.float32)
    back_part = back_part + jnp.dot(grad_values, w_value.T, preferred_element_type=jnp.float32)
    head_sum = lax.psum(back_part, "head")
    grad_features = (head_sum + upstream.astype(jnp.float32)).astype(jnp.bfloat16)
    grad_rim = frame_rims(grad_features)
    grad_wt = jnp.stack(
        [
            contract_rows(
                hidden_rim[offset * frame_len : offset * frame_len + tok_local], grad_features
            )
            for offset in range(3)
        ]
    )
    grad_hidden = jnp.zeros((tok_local, channels), jnp.float32)
    for offset in range(3):
        grad_hidden = grad_hidden + jnp.dot(
            grad_rim[(2 - offset) * frame_len : (2 - offset) * frame_len + tok_local],
            w_temporal[offset].T,
            preferred_element_type=jnp.float32,
        )
    grad_pre = (grad_hidden * silu_slope(pre_act)).astype(jnp.bfloat16)
    grad_ws = jnp.stack([contract_rows(taps[offset], grad_pre) for offset in range(9)])
    totals = lax.psum(
        (grad_ws, grad_wt, grad_wq_local, grad_wk_local, grad_wv_local, grad_wo_local),
        ("frame", "dp"),
    )
    factor = float(lax.axis_size("dp") * lax.axis_size("frame") * tok_local) ** (-0.5)
    return (
        totals[0] * factor,
        totals[1] * factor,
        totals[2] * factor,
        totals[3] * factor,
        totals[4] * factor,
        totals[5] * factor,
    )


def solution(mesh):
    in_specs = (
        P("dp", "frame", None),
        P("dp", None),
        P(),
        P(),
        P(None, "head"),
        P(None, "head"),
        P(None, "head"),
        P("head", None),
        P("dp", "frame", None),
    )
    out_specs = (P(), P(), P(None, "head"), P(None, "head"), P(None, "head"), P("head", None))
    return jax.shard_map(
        on_device, mesh=mesh, in_specs=in_specs, out_specs=out_specs, check_vma=False
    )
```

profile of v0, /device:TPU:1, one launch (start us, length us, event | category | flops | bytes accessed | tf_op | source)
XLA Modules:
  0.0 699.3 jit_solution(11616659482293236148)
XLA Ops:
  7.2 1.9 pad_slice_fusion
  9.2 1.2 fusion.60
  10.4 1.1 convolution_add_fusion.11
  12.7 0.9 multiply_convert_fusion
  13.7 4.5 collective-permute-start
  18.2 1.3 collective-permute-start.1
  19.7 3.3 collective-permute-done.1
  23.4 0.8 convolution_convert_fusion.2
  24.3 1.7 convolution_convert_fusion
  26.2 0.9 convolution_convert_fusion.1
  27.3 83.1 %all-gather.3.cloned.1.call-done = bf16[4096,256]{1,0:T(8,128)(2,1)} async-done(((bf16[256,256]{1,0:T(8,128)(2,1)}), bf16[4096,256]{1,0:T(8,128)(2,1)}) %all-gather.3.cloned.1.call-update) | async-done | bytes 2097168 | tf_op jit(solution)/shard_map/all_gather | solution.py:92
  110.4 2.3 fusion.108
  112.7 0.9 fusion.109
  113.6 1.9 fusion.6
  115.6 0.4 copy-done.3
  116.0 2.4 fusion.9
  118.4 1.3 copy-done.1
  119.8 1.8 fusion.91
  121.5 1.8 fusion.94
  123.3 72.5 %all-gather.5.cloned.1.call-done = bf16[4096,256]{1,0:T(8,128)(2,1)} async-done(((bf16[256,256]{1,0:T(8,128)(2,1)}), bf16[4096,256]{1,0:T(8,128)(2,1)}) %all-gather.5.cloned.1.call-update) | async-done | bytes 2097168 | tf_op jit(solution)/shard_map/all_gather | solution.py:93
  195.8 2.8 convolution_convert_fusion.5
  198.6 2.9 multiply_reduce_fusion.1
  201.6 1.7 fusion.5
  203.3 0.5 fusion.85
  203.8 1.7 copy-done.4
  205.5 1.7 fusion.4
  207.2 1.3 copy-done.2
  208.5 0.5 fusion.88
  209.0 1.1 copy-done.7
  210.1 0.6 copy-done.8
  210.7 3.8 pad_maximum_fusion
  214.5 0.2 all-reduce.5.cloned.1.call-start
  214.8 2.8 convolution_convert_fusion.6
  217.6 0.9 convolution_convert_fusion.4
  218.5 0.9 fusion.83
  219.5 0.2 fusion.84
  219.7 0.9 fusion.35
  220.6 215.9 %reduce-scatter.2.cloned.1.call-done = f32[256,512]{0,1:T(8,128)} async-done(((f32[4096,512]{0,1:T(8,128)}), f32[256,512]{0,1:T(8,128)}) %reduce-scatter.2.cloned.1.call-update) | async-done | bytes 524304 | tf_op jit(solution)/shard_map/reduce_scatter | solution.py:149
  436.6 1.1 convert.4
  437.7 0.9 fusion.74
  438.6 0.2 convolution_add_fusion.2
  438.8 0.9 convolution_add_fusion.1
  439.8 0.9 fusion.71
  440.8 64.6 %all-reduce.5.cloned.1.call-done = f32[256,256]{1,0:T(8,128)} async-done(((f32[256,256]{1,0:T(8,128)}), f32[256,256]{1,0:T(8,128)}) %all-reduce.5.cloned.1.call-update) | async-done | bytes 262160 | tf_op jit(solution)/shard_map/psum | solution.py:161
  505.4 1.0 add_convert_fusion
  506.4 0.2 convolution_bitcast_fusion.1
  506.9 1.3 collective-permute-start.2
  508.2 4.0 collective-permute-start.3
  512.2 0.2 convolution_bitcast_fusion.2
  512.4 0.2 convolution_bitcast_fusion
  512.6 0.9 pad_maximum_fusion.1
  513.8 0.2 fusion.23
  514.1 0.2 fusion.21
  514.3 0.2 fusion.20
  515.0 0.2 fusion.17
  515.9 0.2 fusion.13
  516.2 1.4 copy-done.9
  517.6 167.9 %all-reduce.7.cloned.1.call-done = (f32[9,256,256]{2,1,0:T(8,128)}, f32[3,256,256]{2,1,0:T(8,128)}, f32[256,256]{1,0:T(8,128)}, f32[256,256]{1,0:T(8,128)}, f32[256,256]{1,0:T(8,128)}, /*index=5*/f32[256,256]{1,0:T(8,128)}) async-done(((f32[9,256,256]{2,1,0:T(8,128)}, f32[3,256,256]{2,1,0:T(8,128)}, f32[256,256]{1,0:T(8,128)}, f32[256,256]{1,0:T(8,128)}, f32[256,256]{1,0:T(8,128)}, ...) | async-done | bytes 4194320 | tf_op jit(solution)/shard_map/psum | solution.py:181
  685.5 3.4 broadcast_multiply_fusion
  688.9 0.7 broadcast_multiply_fusion.5
  689.6 0.7 broadcast_multiply_fusion.4
  690.3 0.7 broadcast_multiply_fusion.3
  691.1 0.7 broadcast_multiply_fusion.2
  691.8 0.9 broadcast_multiply_fusion.1
  (126 shorter events, 3.9 us)
Async XLA Ops:
  7.2 19.9 %copy-start = (bf16[256,256]{1,0:T(8,128)(2,1)S(1)}, bf16[256,256]{1,0:T(8,128)(2,1)}, u32[]{:S(2)}) copy-start(bf16[256,256]{1,0:T(8,128)(2,1)} %param.13) | copy-start | bytes 393220
  7.2 4.7 copy-start.14
  7.2 4.3 copy-start.19
  7.2 103.2 %all-gather.3.cloned.1.call-start = ((), (), s32[]{:S(2)}) async-start(), calls=%async_computation.1 | async-start | bytes 2228224 | tf_op jit(solution)/shard_map/all_gather | solution.py:92
  9.2 3.3 copy-start.15
  9.2 3.5 copy-start.30
  11.9 7.6 %copy-start.17 = (bf16[3,256,256]{2,1,0:T(8,128)(2,1)S(1)}, bf16[3,256,256]{2,1,0:T(8,128)(2,1)}, u32[]{:S(2)}) copy-start(bf16[3,256,256]{2,1,0:T(8,128)(2,1)} %param.12) | copy-start | bytes 1179652
  12.5 10.9 %copy-start.27 = (bf16[256,256]{1,0:T(8,128)(2,1)S(1)}, bf16[256,256]{1,0:T(8,128)(2,1)}, u32[]{:S(2)}) copy-start(bf16[256,256]{1,0:T(8,128)(2,1)} %param.14) | copy-start | bytes 393220
  12.7 13.4 %copy-start.42 = (s32[1,4096]{1,0:T(1,128)S(1)}, s32[1,4096]{1,0:T(1,128)}, u32[]{:S(2)}) copy-start(s32[1,4096]{1,0:T(1,128)} %param.10) | copy-start | bytes 49156
  12.7 13.5 %copy-start.13 = (bf16[1,256,256]{2,1,0:T(8,128)(2,1)S(1)}, bf16[1,256,256]{2,1,0:T(8,128)(2,1)}, u32[]{:S(2)}) copy-start(bf16[1,256,256]{2,1,0:T(8,128)(2,1)} %param.17) | copy-start | bytes 393220
  13.6 12.6 %copy-start.37 = (bf16[256,256]{1,0:T(8,128)(2,1)S(1)}, bf16[256,256]{1,0:T(8,128)(2,1)}, u32[]{:S(2)}) copy-start(bf16[256,256]{1,0:T(8,128)(2,1)} %param.16) | copy-start | bytes 393220
  13.7 9.5 %collective-permute-start = (bf16[64,256]{1,0:T(8,128)(2,1)S(1)}, bf16[64,256]{1,0:T(8,128)(2,1)S(1)}, u32[]{:S(2)}, u32[]{:S(2)}) collective-permute-start(bf16[64,256]{1,0:T(8,128)(2,1)S(1)} %get-tuple-element.18), channel_id=1, source_target_pairs={{0,16},{16,32},{32,48},{48,64},{64,80},{80,96},{96,112},{112,128},... | collective-permute-start | bytes 98312 | tf_op jit(solution)/shard_map/ppermute | solution.py:21
  18.2 4.8 collective-permute-start.1
  23.0 89.7 %copy-start.38 = (bf16[64,256]{1,0:T(8,128)(2,1)}, bf16[64,256]{1,0:T(8,128)(2,1)S(1)}, u32[]{:S(2)}) copy-start(bf16[64,256]{1,0:T(8,128)(2,1)S(1)} %collective-permute-done.1) | copy-start | bytes 98308
  23.2 89.5 %copy-start.40 = (bf16[64,256]{1,0:T(8,128)(2,1)}, bf16[64,256]{1,0:T(8,128)(2,1)S(1)}, u32[]{:S(2)}) copy-start(bf16[64,256]{1,0:T(8,128)(2,1)S(1)} %collective-permute-done) | copy-start | bytes 98308
  24.3 171.5 %all-gather.5.cloned.1.call-start = ((), (), s32[]{:S(2)}) async-start(), calls=%async_computation.2 | async-start | bytes 2228224 | tf_op jit(solution)/shard_map/all_gather | solution.py:93
  26.1 410.5 %reduce-scatter.2.cloned.1.call-start = ((), (), s32[]{:S(2)}) async-start(), calls=%async_computation.3 | async-start | bytes 8912896 | tf_op jit(solution)/shard_map/reduce_scatter | solution.py:149
  26.2 87.4 %copy-start.43 = (s32[1,256]{1,0:T(1,128)}, s32[1,256]{1,0:T(1,128)S(1)}, u32[]{:S(2)}) copy-start(s32[1,256]{1,0:T(1,128)S(1)} %constant_dynamic-slice_fusion) | copy-start | bytes 3076
  27.3 85.4 %copy-start.25 = (bf16[256,256]{1,0:T(8,128)(2,1)}, bf16[256,256]{1,0:T(8,128)(2,1)S(1)}, u32[]{:S(2)}) copy-start(bf16[256,256]{1,0:T(8,128)(2,1)S(1)} %convolution_convert_fusion.3) | copy-start | bytes 393220
  110.4 2.3 copy-start.10
  112.7 2.9 copy-start.5
  113.6 2.4 copy-start.3
  115.6 2.8 copy-start.45
  115.6 2.8 copy-start.47
  116.0 3.7 copy-start.20
  118.4 1.3 copy-start.1
  195.8 5.8 copy-start.6
  198.6 4.7 copy-start.23
  198.6 2.9 copy-start.12
  198.6 2.9 copy-start.21
  198.6 2.9 copy-start.44
  198.6 2.9 copy-start.48
  201.6 1.7 copy-start.26
  203.3 2.2 copy-start.4
  203.3 2.2 copy-start.46
  207.2 1.3 copy-start.2
  208.5 1.6 copy-start.7
  208.5 2.2 copy-start.8
  214.5 290.9 %all-reduce.5.cloned.1.call-start = ((), (), s32[]{:S(2)}) async-start(), calls=%async_computation.4 | async-start | bytes 524288 | tf_op jit(solution)/shard_map/psum | solution.py:161
  214.8 2.9 copy-start.11
  217.6 2.1 copy-start.24
  217.6 2.1 copy-start.36
  218.5 220.1 %copy-start.28 = (bf16[256,256]{1,0:T(8,128)(2,1)S(1)}, bf16[256,256]{1,0:T(8,128)(2,1)}, u32[]{:S(2)}) copy-start(bf16[256,256]{1,0:T(8,128)(2,1)} %param.14) | copy-start | bytes 393220
  218.5 220.3 %copy-start.29 = (bf16[256,256]{1,0:T(8,128)(2,1)S(1)}, bf16[256,256]{1,0:T(8,128)(2,1)}, u32[]{:S(2)}) copy-start(bf16[256,256]{1,0:T(8,128)(2,1)} %param.15) | copy-start | bytes 393220
  220.6 286.0 %copy-start.18 = (bf16[3,256,256]{2,1,0:T(8,128)(2,1)S(1)}, bf16[3,256,256]{2,1,0:T(8,128)(2,1)}, u32[]{:S(2)}) copy-start(bf16[3,256,256]{2,1,0:T(8,128)(2,1)} %param.12) | copy-start | bytes 1179652
  437.6 74.5 %copy-start.41 = (bf16[64,256]{1,0:T(8,128)(2,1)S(1)}, bf16[64,256]{1,0:T(8,128)(2,1)}, u32[]{:S(2)}) copy-start(bf16[64,256]{1,0:T(8,128)(2,1)} %copy-done.40) | copy-start | bytes 98308
  438.6 73.8 %copy-start.39 = (bf16[64,256]{1,0:T(8,128)(2,1)S(1)}, bf16[64,256]{1,0:T(8,128)(2,1)}, u32[]{:S(2)}) copy-start(bf16[64,256]{1,0:T(8,128)(2,1)} %copy-done.38) | copy-start | bytes 98308
  439.8 245.7 %all-reduce.7.cloned.1.call-start = ((), (), s32[]{:S(2)}) async-start(), calls=%async_computation.5 | async-start | bytes 8388608 | tf_op jit(solution)/shard_map/psum | solution.py:181
  440.8 73.1 %copy-start.49 = (f32[256,256]{1,0:T(8,128)S(1)}, f32[256,256]{1,0:T(8,128)}, u32[]{:S(2)}) copy-start(f32[256,256]{1,0:T(8,128)} %get-tuple-element.31) | copy-start | bytes 786436
  506.9 7.0 collective-permute-start.2
  508.2 5.4 collective-permute-start.3
  512.4 1.7 copy-start.16
  514.1 1.8 copy-start.31
  516.1 1.4 copy-start.9
  685.5 3.4 copy-start.35
  685.5 4.2 copy-start.34
  685.5 4.9 copy-start.33
  685.5 5.6 copy-start.32
  685.5 6.3 copy-start.22
Sparse Core Ops, SparseCore 0:
  24.4 85.9 all-gather.2
  113.6 82.1 all-gather.4
  214.7 221.8 reduce-scatter.1
  439.9 65.4 all-reduce.4
  517.7 167.7 all-reduce.6
where the time goes:
time: 700 us; the launch traced here: 699 us
  waiting for transfers between devices  607 us (87%)
  matrix products  37.3 us (5%)
  other arithmetic  18.4 us (3%)
  between operations  14.7 us (2%)
  starting transfers between devices  11.5 us (2%)
  local copies, waits for them, and re-layouts  9.96 us (1%)
    reduce_scatter x1, waiting for transfers between devices, on_device(): lax.psum_scatter(jnp.concatenate(key_parts + value_parts, axis=1), 'frame...  216 us
    psum x1, waiting for transfers between devices, on_device(): lax.psum((grad_ws, grad_wt, grad_wq_local, grad_wk_local, grad_wv_local,...  168 us
    all_gather x1, waiting for transfers between devices, on_device(): lax.all_gather(keys_local, 'frame', axis=0, tiled=True)  83.1 us
    all_gather x1, waiting for transfers between devices, on_device(): lax.all_gather(values_local, 'frame', axis=0, tiled=True)  72.5 us
    psum x1, waiting for transfers between devices, on_device(): head_sum = lax.psum(back_part, 'head')  64.6 us
  transfers between devices with their start and end apart: 9, of which 6 were waited for; matrix products, arithmetic and copies ran while one was open for 3% of the time, Pallas kernels for 0%

commit v1 on v0

v1 whole, which is shorter than its diff:
```python
import jax
import jax.numpy as jnp
from jax import lax
from jax.sharding import Mesh, PartitionSpec as P

HD = 128
SIDE = 8
FRAME = SIDE * SIDE
NEG_FILL = -1e30
BF = jnp.bfloat16
F32 = jnp.float32


def dot(left, right):
    return jnp.dot(left, right, preferred_element_type=F32)


def contract_rows(left, right):
    return lax.dot_general(left, right, (((0,), (0,)), ((), ())), preferred_element_type=F32)


def dot_t(left, right):
    return lax.dot_general(left, right, (((1,), (1,)), ((), ())), preferred_element_type=F32)


def xor_perm(count, step):
    return [(i, i ^ step) for i in range(count)]


def unxor(parts, index):
    parts = list(parts)
    bit = 1
    while bit < len(parts):
        odd = (index & bit) != 0
        parts = [jnp.where(odd, parts[s ^ bit], parts[s]) for s in range(len(parts))]
        bit *= 2
    return parts


def gather_xor(block, axis, count, index):
    parts = [block] + [lax.ppermute(block, axis, xor_perm(count, s)) for s in range(1, count)]
    return unxor(parts, index)


def scatter_xor(total, axis, count, index):
    rows = total.shape[0] // count
    low = total.astype(BF)
    got = [
        lax.ppermute(
            lax.dynamic_slice_in_dim(low, (index ^ s) * rows, rows), axis, xor_perm(count, s)
        )
        for s in range(1, count)
    ]
    own = lax.dynamic_slice_in_dim(total, index * rows, rows)
    for part in got:
        own = own + part.astype(F32)
    return own


def spread(block, axis, count):
    return lax.all_to_all(
        jnp.broadcast_to(block[None], (count,) + block.shape), axis, 0, 0
    )


def shift_rows(field, step):
    if step == 0:
        return field
    pad = jnp.zeros_like(field[:, :1])
    if step > 0:
        return jnp.concatenate([field[:, 1:], pad], axis=1)
    return jnp.concatenate([pad, field[:, :-1]], axis=1)


def shift_cols(field, step):
    if step == 0:
        return field
    pad = jnp.zeros_like(field[:, :, :1])
    if step > 0:
        return jnp.concatenate([field[:, :, 1:], pad], axis=2)
    return jnp.concatenate([pad, field[:, :, :-1]], axis=2)


def shift_frames(tokens, step):
    if step == 0:
        return tokens
    pad = jnp.zeros_like(tokens[:FRAME])
    if step > 0:
        return jnp.concatenate([tokens[FRAME:], pad], axis=0)
    return jnp.concatenate([pad, tokens[:-FRAME]], axis=0)


def on_device(sizes, clip, block_ids, w_spatial, w_temporal, w_query, w_key, w_value, w_out, cotangent):
    n_xh, n_z, n_y, n_c, n_dp = sizes
    i_xh, i_y, i_c, i_dp = (lax.axis_index(a) for a in ("xh", "y", "c", "dp"))
    i_x = i_xh * n_dp + i_dp
    n_head = n_y * n_c
    n_frame = n_xh * n_z
    own_clip = clip[0]
    upstream = cotangent[0]
    ids = block_ids[0]
    local, ch = own_clip.shape
    tokens = local * n_frame
    frames = tokens // FRAME
    scale = HD ** (-0.5)

    piece = local // n_head
    mine = lax.dynamic_slice_in_dim(own_clip, lax.axis_index(("y", "c")) * piece, piece)
    part = spread(mine, "z", n_z)
    part = jnp.stack(gather_xor(part, "xh", n_xh, i_xh))
    part = jnp.stack(gather_xor(part, "y", n_y, i_y))
    part = jnp.stack(gather_xor(part, "c", n_c, i_c))
    whole = part.transpose(2, 3, 1, 0, 4, 5).reshape(frames, SIDE, SIDE, ch)

    cols = jnp.concatenate([shift_cols(whole, b - 1) for b in range(3)], axis=3)
    cols = cols.reshape(tokens, 3 * ch)
    w_sp = w_spatial.reshape(3, 3 * ch, ch).transpose(1, 0, 2).reshape(3 * ch, 3 * ch)
    mixed = dot(cols, w_sp).reshape(frames, SIDE, SIDE, 3 * ch)
    pre = sum(shift_rows(mixed[..., a * ch : (a + 1) * ch], a - 1) for a in range(3))
    pre = pre.reshape(tokens, ch)
    sigma = jax.nn.sigmoid(pre)
    slope = sigma * (1.0 + pre * (1.0 - sigma))
    hidden = (pre * sigma).astype(BF)
    around = jnp.concatenate([shift_frames(hidden, d - 1) for d in range(3)], axis=1)
    features = dot(around, w_temporal.reshape(3 * ch, ch)).astype(BF)

    keys = dot(features, w_key).astype(BF)
    values = dot(features, w_value).astype(BF)
    first = lax.axis_index(("xh", "z")) * local
    own_feat = lax.dynamic_slice_in_dim(features, first, local)
    queries = dot(own_feat, w_query).astype(BF)
    grad_att = dot_t(upstream, w_out).astype(BF)
    visible = ids[None, :] <= lax.dynamic_slice_in_dim(ids, first, local)[:, None]
    att_parts, gq_parts, gk_parts, gv_parts = [], [], [], []
    for h in range(queries.shape[1] // HD):
        sel = slice(h * HD, (h + 1) * HD)
        q_h, k_h, v_h, g_h = queries[:, sel], keys[:, sel], values[:, sel], grad_att[:, sel]
        scores = jnp.where(visible, dot_t(q_h, k_h) * scale, NEG_FILL)
        top = jnp.max(scores, axis=1, keepdims=True)
        total = jnp.sum(jnp.where(visible, jnp.exp(scores - top), 0.0), axis=1, keepdims=True)
        log_norm = top + jnp.log(total)
        probs = jnp.where(visible, jnp.exp(scores - log_norm), 0.0)
        probs_low = probs.astype(BF)
        att = dot(probs_low, v_h).astype(BF)
        delta = jnp.sum(g_h.astype(F32) * att.astype(F32), axis=1, keepdims=True)
        grad_scores = (probs * (dot_t(g_h, v_h) - delta) * scale).astype(BF)
        att_parts.append(att)
        gq_parts.append(dot(grad_scores, k_h).astype(BF))
        gk_parts.append(contract_rows(grad_scores, q_h).astype(BF))
        gv_parts.append(contract_rows(probs_low, g_h).astype(BF))
    att = jnp.concatenate(att_parts, axis=1)
    gq = jnp.concatenate(gq_parts, axis=1)
    gk = jnp.concatenate(gk_parts, axis=1)
    gv = jnp.concatenate(gv_parts, axis=1)

    gf = dot_t(gk, w_key) + dot_t(gv, w_value)
    own_gf = dot_t(gq, w_query) + upstream.astype(F32) * (1.0 / n_head)
    own_gf = own_gf + lax.dynamic_slice_in_dim(gf, first, local)
    gf = lax.dynamic_update_slice_in_dim(gf, own_gf, first, 0).astype(BF)
    g_wt = contract_rows(around, gf)
    back = jnp.concatenate([shift_frames(gf, 1 - d) for d in range(3)], axis=1)
    w_tt = w_temporal.transpose(0, 2, 1).reshape(3 * ch, ch)
    grad_pre = dot(back, w_tt) * slope
    grad_pre = grad_pre.reshape(frames, SIDE, SIDE, ch)
    rows = jnp.concatenate([shift_rows(grad_pre, 1 - a).astype(BF) for a in range(3)], axis=3)
    g_ws = contract_rows(cols, rows.reshape(tokens, 3 * ch))
    g_ws = g_ws.reshape(3, ch, 3, ch).transpose(2, 0, 1, 3).reshape(9 * ch, ch)
    g_head = jnp.concatenate(
        [
            contract_rows(own_feat, gq),
            contract_rows(features, gk),
            contract_rows(features, gv),
            contract_rows(att, upstream),
        ]
    )

    shared = jnp.concatenate([g_ws, g_wt])
    shared = scatter_xor(shared, "c", n_c, i_c)
    shared = scatter_xor(shared, "y", n_y, i_y)
    block = jnp.concatenate([shared, g_head])
    n_x = n_xh * n_dp
    block = scatter_xor(block, ("xh", "dp"), n_x, i_x)
    rows = block.shape[0] // n_z
    got = lax.all_to_all(block.astype(BF).reshape(n_z, rows, ch), "z", 0, 0)
    factor = float(n_dp * tokens) ** (-0.5)
    done = (jnp.sum(got.astype(F32), axis=0) * factor).astype(BF)
    done = spread(done, "z", n_z).reshape(n_z * rows, ch)
    done = jnp.concatenate(gather_xor(done, ("xh", "dp"), n_x, i_x))
    cut = shared.shape[0]
    heads = done[cut:].astype(F32).reshape(4, ch, -1)
    done = jnp.concatenate(gather_xor(done[:cut], "y", n_y, i_y))
    done = jnp.concatenate(gather_xor(done, "c", n_c, i_c)).astype(F32)
    return (
        done[: 9 * ch].reshape(9, ch, ch),
        done[9 * ch :].reshape(3, ch, ch),
        heads[0],
        heads[1],
        heads[2],
        heads[3],
    )


def solution(mesh):
    frame, head, dp = (mesh.shape[a] for a in ("frame", "head", "dp"))
    sizes = (2, frame // 2, head // 2, 2, dp)
    names = ("xh", "z", "y", "c", "dp")
    fine = Mesh(mesh.devices.reshape(sizes), names)
    rows, head_axes = ("xh", "z"), ("y", "c")
    in_specs = (
        P("dp", rows, None),
        P("dp", None),
        P(),
        P(),
        P(None, head_axes),
        P(None, head_axes),
        P(None, head_axes),
        P(head_axes, None),
        P("dp", rows, None),
    )
    out_specs = (
        P(),
        P(),
        P(None, head_axes),
        P(None, head_axes),
        P(None, head_axes),
        P(head_axes, None),
    )

    def body(*args):
        return on_device(sizes, *args)

    return jax.shard_map(
        body, mesh=fine, in_specs=in_specs, out_specs=out_specs, check_vma=False
    )
```

time: 700 us -> 239 us (0.34)
  waiting for transfers between devices: 607 us -> 46.7 us
  blocking collectives: 0 us -> 39 us
  local copies, waits for them, and re-layouts: 9.96 us -> 37.6 us
  starting transfers between devices: 11.5 us -> 31.2 us
  other arithmetic: 18.4 us -> 32.9 us
  between operations: 14.7 us -> 1.52 us
  matrix products: 37.3 us -> 46.2 us
    psum x2 -> x0, waiting for transfers between devices: 233 us -> none  [the longest x1 168 us: on_device(): lax.psum((grad_ws, grad_wt, grad_wq_local, grad_wk_local, grad_wv_local,...]
    reduce_scatter x1 -> x0, waiting for transfers between devices: 216 us -> none  [on_device(): lax.psum_scatter(jnp.concatenate(key_parts + value_parts, axis=1), 'frame...]
    all_gather x2 -> x0, waiting for transfers between devices: 156 us -> none  [the longest x1 83.1 us: on_device(): lax.all_gather(keys_local, 'frame', axis=0, tiled=True)]
    ppermute x4 -> x19, waiting for transfers between devices: 3.35 us -> 46.7 us  [the longest x12 28.3 us: gather_xor(): lax.ppermute(block, axis, xor_perm(count, s))]
    all_to_all x0 -> x3, blocking collectives: none -> 39 us  [the longest x2 27.8 us: spread(): lax.all_to_all(jnp.broadcast_to(block[None], (count,) + block.shape), axi...]
    ppermute x4 -> x19, starting transfers between devices: 11.1 us -> 31.2 us  [the longest x12 23.7 us: gather_xor(): lax.ppermute(block, axis, xor_perm(count, s))]
    convert_element_type x2 -> x10, other arithmetic: 3.36 us -> 12.2 us  [the longest x3 5.07 us: scatter_xor(): low = total.astype(BF)]
    reshape x0 -> x3, local copies, waits for them, and re-layouts: none -> 8.8 us  [the longest x1 8.72 us: on_device(): g_ws = contract_rows(cols, rows.reshape(tokens, 3 * ch))]
  transfers between devices with their start and end apart: 9 -> 19, of which waited for: 6 -> 17; matrix products, arithmetic and copies ran while one was open for 3% -> 2% of each run, Pallas kernels for 0% -> 0%
where the time goes in v1:
time: 239 us; the launch traced here: 235 us
  waiting for transfers between devices  46.7 us (20%)
  matrix products  46.2 us (19%)
  blocking collectives  39 us (16%)
  local copies, waits for them, and re-layouts  37.6 us (16%)
  other arithmetic  32.9 us (14%)
  starting transfers between devices  31.2 us (13%)
    ppermute x12, waiting for transfers between devices, gather_xor(): lax.ppermute(block, axis, xor_perm(count, s))  28.3 us
    all_to_all x2, blocking collectives, spread(): lax.all_to_all(jnp.broadcast_to(block[None], (count,) + block.shape), axi...  27.8 us
    ppermute x12, starting transfers between devices, gather_xor(): lax.ppermute(block, axis, xor_perm(count, s))  23.7 us
    dot_general x10, matrix products, dot(): return jnp.dot(left, right, preferred_element_type=F32)  22 us
    ppermute x7, waiting for transfers between devices, scatter_xor(): lax.ppermute(lax.dynamic_slice_in_dim(low, (index ^ s) * rows, rows), axi...  18.4 us
    dot_general x10, matrix products, contract_rows(): lax.dot_general(left, right, (((0,), (0,)), ((), ())), preferred_element_...  17 us
    all_to_all x1, blocking collectives, on_device(): got = lax.all_to_all(block.astype(BF).reshape(n_z, rows, ch), 'z', 0, 0)  11.1 us
    reshape x1, local copies, waits for them, and re-layouts, on_device(): g_ws = contract_rows(cols, rows.reshape(tokens, 3 * ch))  8.72 us
  transfers between devices with their start and end apart: 19, of which 17 were waited for; matrix products, arithmetic and copies ran while one was open for 2% of the time, Pallas kernels for 0%

profile of v1, /device:TPU:1, one launch (start us, length us, event | category | flops | bytes accessed | tf_op | source)
XLA Modules:
  0.0 235.1 jit_solution(6348850290847643487)
XLA Ops:
  1.5 16.7 %all_to_all.15 = bf16[8,32,256]{2,1,0:T(8,128)(2,1)S(1)} all-to-all(bf16[8,32,256]{2,1,0:T(8,128)(2,1)S(1)} %broadcast_in_dim.33), channel_id=1, replica_groups=mesh['xh'=2,'z'=8,'y'=4,'c'=2,'dp'=2] {'z'}, dimensions={0} | all-to-all | bytes 262144 | tf_op jit(solution)/shard_map/all_to_all | solution.py:61
  18.2 2.7 %collective-permute-start = (bf16[8,32,256]{2,1,0:T(8,128)(2,1)S(1)}, bf16[8,32,256]{2,1,0:T(8,128)(2,1)S(1)}, u32[]{:S(2)}, u32[]{:S(2)}) collective-permute-start(bf16[8,32,256]{2,1,0:T(8,128)(2,1)S(1)} %all_to_all.15), channel_id=1, source_target_pairs={{0,128},{128,0},{1,129},{129,1},{2,130},{130,2},{3,131},{131,3},{4... | collective-permute-start | bytes 393224 | tf_op jit(solution)/shard_map/ppermute | solution.py:41
  20.9 2.6 %collective-permute-done = bf16[8,32,256]{2,1,0:T(8,128)(2,1)S(1)} collective-permute-done((bf16[8,32,256]{2,1,0:T(8,128)(2,1)S(1)}, bf16[8,32,256]{2,1,0:T(8,128)(2,1)S(1)}, u32[]{:S(2)}, u32[]{:S(2)}) %collective-permute-start) | collective-permute-done | bytes 131104 | tf_op jit(solution)/shard_map/ppermute | solution.py:41
  23.6 1.4 collective-permute-start.3
  25.0 2.6 %collective-permute-start.2 = (bf16[2,8,32,256]{3,2,1,0:T(8,128)(2,1)S(1)}, bf16[2,8,32,256]{3,2,1,0:T(8,128)(2,1)S(1)}, u32[]{:S(2)}, u32[]{:S(2)}) collective-permute-start(bf16[2,8,32,256]{3,2,1,0:T(8,128)(2,1)S(1)} %pad_maximum_fusion.15), channel_id=1, source_target_pairs={{0,8},{4,12},{8,0},{12,4},{1,9},{5,13},{9,1},{13,5},{2,10},{6,14},... | collective-permute-start | bytes 786440 | tf_op jit(solution)/shard_map/ppermute | solution.py:41
  27.6 1.3 collective-permute-done.3
  28.9 7.0 %collective-permute-done.2 = bf16[2,8,32,256]{3,2,1,0:T(8,128)(2,1)S(1)} collective-permute-done((bf16[2,8,32,256]{3,2,1,0:T(8,128)(2,1)S(1)}, bf16[2,8,32,256]{3,2,1,0:T(8,128)(2,1)S(1)}, u32[]{:S(2)}, u32[]{:S(2)}) %collective-permute-start.2) | collective-permute-done | bytes 262176 | tf_op jit(solution)/shard_map/ppermute | solution.py:41
  35.9 5.1 %collective-permute-done.1 = bf16[2,8,32,256]{3,2,1,0:T(8,128)(2,1)} collective-permute-done((bf16[2,8,32,256]{3,2,1,0:T(8,128)(2,1)S(1)}, bf16[2,8,32,256]{3,2,1,0:T(8,128)(2,1)}, u32[]{:S(2)}, u32[]{:S(2)}) %collective-permute-start.1) | collective-permute-done | bytes 262176 | tf_op jit(solution)/shard_map/ppermute | solution.py:41
  41.0 1.0 select_bitcast_fusion.5
  42.1 1.1 pad_maximum_fusion.11
  43.2 2.4 %collective-permute-start.4 = (bf16[4,2,8,32,256]{4,3,0,2,1:T(8,128)(2,1)}, bf16[4,2,8,32,256]{4,3,0,2,1:T(8,128)(2,1)}, u32[]{:S(2)}, u32[]{:S(2)}) collective-permute-start(bf16[4,2,8,32,256]{4,3,0,2,1:T(8,128)(2,1)} %pad_maximum_fusion.11), channel_id=1, source_target_pairs={{0,2},{2,0},{1,3},{3,1},{4,6},{6,4},{5,7},{7,5},{8,10},{10,8},{9,1... | collective-permute-start | bytes 3145736 | tf_op jit(solution)/shard_map/ppermute | solution.py:41
  46.5 1.6 copy.36
  48.3 1.4 select_bitcast_fusion.1
  50.0 1.0 fusion.108
  53.0 8.1 %fusion.19 = f32[64,8,8,768]{3,2,1,0:T(8,128)} fusion(bf16[768,768,1,1]{0,1,3,2:T(8,128)(2,1)S(1)} %bitcast.129, bf16[64,8,8,256]{3,2,1,0:T(8,128)(2,1)S(1)} %concatenate.86, bf16[64,8,8,256]{3,2,1,0:T(8,128)(2,1)S(1)} %bitcast.116, bf16[64,8,8,256]{3,2,1,0:T(8,128)(2,1)S(1)} %concatenate.83), kind=kOutput, calls=%fused_computation.28 | convolution fusion | flops 4850712576 | bytes 20054016 | tf_op jit(solution)/shard_map/dot_general | solution.py:15
  61.1 3.7 %fusion.104 = (f32[64,7,8,256]{3,2,1,0:T(8,128)S(1)}, f32[64,7,8,256]{3,2,1,0:T(8,128)S(1)}) fusion(f32[64,8,8,768]{3,2,1,0:T(8,128)} %fusion.19), kind=kLoop, calls=%fused_computation.194 | loop fusion | bytes 14680064 | tf_op jit(solution)/shard_map/slice | solution.py:72
  64.8 3.4 %fusion.40 = f32[64,8,8,256]{3,2,1,0:T(8,128)S(1)} fusion(f32[64,8,8,768]{3,2,1,0:T(8,128)} %fusion.19, f32[64,7,8,256]{3,2,1,0:T(8,128)S(1)} %get-tuple-element.13, f32[64,7,8,256]{3,2,1,0:T(8,128)S(1)} %get-tuple-element.12), kind=kLoop, calls=%fused_computation.58 | loop fusion | flops 2097152 | bytes 15728640 | tf_op jit(solution)/shard_map/add | solution.py:119
  68.2 3.8 %fusion.44 = (bf16[4096,256]{1,0:T(8,128)(2,1)S(1)}, f32[4096,256]{1,0:T(8,128)}) fusion(f32[64,8,8,256]{3,2,1,0:T(8,128)S(1)} %fusion.40), kind=kLoop, calls=%fused_computation.65 | loop fusion | flops 9437184 | bytes 10485760 | tf_op jit(solution)/shard_map/convert_element_type | solution.py:123
  72.3 3.0 %convolution_convert_fusion.2 = bf16[4096,256]{1,0:T(8,128)(2,1)S(1)} fusion(bf16[768,256]{1,0:T(8,128)(2,1)S(1)} %bitcast.131, bf16[4032,256]{1,0:T(8,128)(2,1)S(1)} %get-tuple-element.21, bf16[4032,256]{1,0:T(8,128)(2,1)S(1)} %get-tuple-element.20, bf16[4096,256]{1,0:T(8,128)(2,1)S(1)} %get-tuple-element.14), kind=kOutput, calls=%fused_computation.50 | convolution fusion | flops 1643118592 | bytes 8716288 | tf_op jit(solution)/shard_map/dot_general | solution.py:15
  78.8 1.9 fusion.38
  80.7 1.7 fusion.48
  84.2 1.5 multiply_reduce_fusion.1
  85.7 1.7 fusion.34
  88.8 1.7 fusion.33
  91.8 1.0 copy-done.4
  94.8 2.7 %fusion.99 = f32[768,256]{1,0:T(8,128)} fusion(bf16[4096,256]{1,0:T(8,128)(2,1)S(1)} %convert_element_type.147, bf16[4032,256]{1,0:T(8,128)(2,1)S(1)} %get-tuple-element.21, bf16[4032,256]{1,0:T(8,128)(2,1)S(1)} %get-tuple-element.20, bf16[4096,256]{1,0:T(8,128)(2,1)S(1)} %get-tuple-element.14), kind=kOutput, calls=%fused_computation.192 | convolution fusion | flops 1642070016 | bytes 9109504 | tf_op jit(solution)/shard_map/dot_general | solution.py:19
  97.6 2.2 fusion.106
  100.0 3.1 %maximum_bitcast_fusion = bf16[768,4096]{0,1:T(8,128)(2,1)} fusion(bf16[4096,256]{1,0:T(8,128)(2,1)S(1)} %bitcast.124, bf16[4096,256]{1,0:T(8,128)(2,1)S(1)} %bitcast.117, bf16[4096,256]{1,0:T(8,128)(2,1)S(1)} %bitcast.123), kind=kLoop, calls=%fused_computation.27 | loop fusion | flops 18874368 | bytes 12582912 | tf_op jit(solution)/shard_map/dot_general | solution.py:19
  103.1 8.5 %copy.35 = bf16[768,4096]{1,0:T(8,128)(2,1)} copy(bf16[768,4096]{0,1:T(8,128)(2,1)} %maximum_bitcast_fusion) | data formatting | bytes 12582912 | tf_op jit(solution)/shard_map/dot_general | solution.py:19
  111.6 5.4 %fusion.35 = bf16[4096,256]{1,0:T(8,128)(2,1)S(1)} fusion(f32[4096,256]{1,0:T(8,128)} %get-tuple-element.15, bf16[768,256]{1,0:T(8,128)(2,1)} %bitcast.132, bf16[4032,256]{1,0:T(8,128)(2,1)} %get-tuple-element.19, bf16[4032,256]{1,0:T(8,128)(2,1)} %get-tuple-element.18, bf16[4096,256]{1,0:T(8,128)(2,1)} %copy-done.3), kind=kOutput, calls=%fused_computation.49 | convolution fusion | flops 1644167168 | bytes 12910592 | tf_op jit(solution)/shard_map/dot_general | solution.py:15
  117.3 5.6 %fusion.6 = bf16[64,8,8,768]{3,2,1,0:T(8,128)(2,1)} fusion(bf16[64,7,8,256]{3,2,1,0:T(8,128)(2,1)S(1)} %get-tuple-element.17, bf16[64,7,8,256]{3,2,1,0:T(8,128)(2,1)S(1)} %get-tuple-element.16, bf16[64,8,8,256]{3,2,1,0:T(8,128)(2,1)S(1)} %bitcast.122), kind=kLoop, calls=%fused_computation.16 | loop fusion | flops 31457280 | bytes 12058624 | tf_op jit(solution)/shard_map/concatenate | solution.py:165
  122.9 8.7 %copy.39 = bf16[4096,768]{0,1:T(8,128)(2,1)} copy(bf16[4096,768]{1,0:T(8,128)(2,1)} %bitcast.118) | data formatting | bytes 12582912 | tf_op jit(solution)/shard_map/reshape | solution.py:166
  131.6 9.1 %convolution_bitcast_fusion = f32[3,3,256,256]{3,2,0,1:T(8,128)S(1)} fusion(bf16[3,256,4096,1]{2,1,3,0:T(8,128)(2,1)} %bitcast.125, bf16[3,256,4096,1]{2,1,0,3:T(8,128)(2,1)} %bitcast.126), kind=kOutput, calls=%fused_computation.78 | convolution fusion | flops 4831838208 | bytes 14942208 | tf_op jit(solution)/shard_map/dot_general | solution.py:19
  140.9 1.4 copy-done.2
  142.3 1.8 fusion.51
  144.4 2.3 collective-permute-done.5
  146.7 3.2 %fusion.102 = (bf16[1536,256]{1,0:T(8,128)(2,1)S(1)}, f32[1536,256]{1,0:T(8,128)}) fusion(bf16[1536,256]{1,0:T(8,128)(2,1)} %collective-permute-done.5, s32[]{:T(128)S(6)} %select_n.237, f32[768,256]{1,0:T(8,128)} %fusion.99, f32[2304,256]{1,0:T(8,128)} %bitcast.120), kind=kLoop, calls=%fused_computation.193 | loop fusion | flops 1572864 | bytes 6291460 | tf_op jit(solution)/shard_map/convert_element_type | solution.py:47
  150.8 3.2 %collective-permute-start.7 = (bf16[384,256]{1,0:T(8,128)(2,1)}, bf16[384,256]{1,0:T(8,128)(2,1)}, u32[]{:S(2)}, u32[]{:S(2)}) collective-permute-start(bf16[384,256]{1,0:T(8,128)(2,1)} %get-tuple-element.42), channel_id=1, source_target_pairs={{0,8},{4,12},{8,0},{12,4},{1,9},{5,13},{9,1},{13,5},{2,10},{6,14},... | collective-permute-start | bytes 589832 | tf_op jit(solution)/shard_map/ppermute | solution.py:49
  154.0 3.2 %collective-permute-done.6 = bf16[384,256]{1,0:T(8,128)(2,1)} collective-permute-done((bf16[384,256]{1,0:T(8,128)(2,1)}, bf16[384,256]{1,0:T(8,128)(2,1)}, u32[]{:S(2)}, u32[]{:S(2)}) %collective-permute-start.6) | collective-permute-done | bytes 196640 | tf_op jit(solution)/shard_map/ppermute | solution.py:49
  157.3 5.4 %collective-permute-done.8 = bf16[384,256]{1,0:T(8,128)(2,1)} collective-permute-done((bf16[384,256]{1,0:T(8,128)(2,1)}, bf16[384,256]{1,0:T(8,128)(2,1)}, u32[]{:S(2)}, u32[]{:S(2)}) %collective-permute-start.8) | collective-permute-done | bytes 196640 | tf_op jit(solution)/shard_map/ppermute | solution.py:49
  162.7 1.4 add_dynamic-update-slice_fusion
  164.3 2.1 fusion.57
  167.6 1.1 copy-done.11
  168.8 1.3 collective-permute-start.9
  170.1 1.8 collective-permute-start.11
  172.7 1.0 collective-permute-done.9
  173.7 1.9 collective-permute-done.11
  175.6 4.5 %collective-permute-done.10 = bf16[352,256]{1,0:T(8,128)(2,1)S(1)} collective-permute-done((bf16[352,256]{1,0:T(8,128)(2,1)S(1)}, bf16[352,256]{1,0:T(8,128)(2,1)S(1)}, u32[]{:S(2)}, u32[]{:S(2)}) %collective-permute-start.10) | collective-permute-done | bytes 180256 | tf_op jit(solution)/shard_map/ppermute | solution.py:49
  180.2 1.1 add_convert_fusion
  181.3 11.1 %all_to_all.16 = bf16[8,44,256]{2,1,0:T(8,128)(2,1)S(1)} all-to-all(bf16[8,44,256]{2,1,0:T(8,128)(2,1)S(1)} %reshape.114), channel_id=1, replica_groups=mesh['xh'=2,'z'=8,'y'=4,'c'=2,'dp'=2] {'z'}, dimensions={0} | all-to-all | bytes 360448 | tf_op jit(solution)/shard_map/all_to_all | solution.py:184
  192.5 11.1 %all_to_all.17 = bf16[8,44,256]{2,1,0:T(8,128)(2,1)S(1)} all-to-all(bf16[8,44,256]{2,1,0:T(8,128)(2,1)S(1)} %broadcast_in_dim.36), channel_id=1, replica_groups=mesh['xh'=2,'z'=8,'y'=4,'c'=2,'dp'=2] {'z'}, dimensions={0} | all-to-all | bytes 360448 | tf_op jit(solution)/shard_map/all_to_all | solution.py:61
  203.7 2.7 %collective-permute-start.13 = (bf16[352,256]{1,0:T(8,128)(2,1)S(1)}, bf16[352,256]{1,0:T(8,128)(2,1)S(1)}, u32[]{:S(2)}, u32[]{:S(2)}) collective-permute-start(bf16[352,256]{1,0:T(8,128)(2,1)S(1)} %reshape.115), channel_id=1, source_target_pairs={{0,128},{1,129},{128,0},{129,1},{2,130},{3,131},{130,2},{131,3},{4... | collective-permute-start | bytes 540680 | tf_op jit(solution)/shard_map/ppermute | solution.py:41
  206.4 1.1 collective-permute-start.12
  208.1 3.3 %collective-permute-done.13 = bf16[352,256]{1,0:T(8,128)(2,1)S(1)} collective-permute-done((bf16[352,256]{1,0:T(8,128)(2,1)S(1)}, bf16[352,256]{1,0:T(8,128)(2,1)S(1)}, u32[]{:S(2)}, u32[]{:S(2)}) %collective-permute-start.13) | collective-permute-done | bytes 180256 | tf_op jit(solution)/shard_map/ppermute | solution.py:41
  211.3 1.8 collective-permute-done.12
  213.4 2.4 %collective-permute-start.16 = (bf16[384,256]{1,0:T(8,128)(2,1)S(1)}, bf16[384,256]{1,0:T(8,128)(2,1)S(1)}, u32[]{:S(2)}, u32[]{:S(2)}) collective-permute-start(bf16[384,256]{1,0:T(8,128)(2,1)S(1)} %pad_maximum_fusion.16), channel_id=1, source_target_pairs={{0,8},{4,12},{8,0},{12,4},{1,9},{5,13},{9,1},{13,5},{2,10},{6,14},... | collective-permute-start | bytes 589832 | tf_op jit(solution)/shard_map/ppermute | solution.py:41
  215.8 1.4 collective-permute-start.15
  217.2 1.0 collective-permute-done.17
  218.2 2.9 %collective-permute-done.16 = bf16[384,256]{1,0:T(8,128)(2,1)S(1)} collective-permute-done((bf16[384,256]{1,0:T(8,128)(2,1)S(1)}, bf16[384,256]{1,0:T(8,128)(2,1)S(1)}, u32[]{:S(2)}, u32[]{:S(2)}) %collective-permute-start.16) | collective-permute-done | bytes 196640 | tf_op jit(solution)/shard_map/ppermute | solution.py:41
  221.1 2.0 collective-permute-done.15
  223.2 6.6 %collective-permute-start.18 = (bf16[1536,256]{1,0:T(8,128)(2,1)S(1)}, bf16[1536,256]{1,0:T(8,128)(2,1)S(1)}, u32[]{:S(2)}, u32[]{:S(2)}) collective-permute-start(bf16[1536,256]{1,0:T(8,128)(2,1)S(1)} %pad_maximum_fusion.12), channel_id=1, source_target_pairs={{0,2},{2,0},{1,3},{3,1},{4,6},{6,4},{5,7},{7,5},{8,10},{10,8},{9,1... | collective-permute-start | bytes 2359304 | tf_op jit(solution)/shard_map/ppermute | solution.py:41
  229.9 1.0 fusion.109
  232.1 0.9 maximum_convert_fusion.1
  233.3 1.6 slice.139
  (104 shorter events, 20.9 us)
Async XLA Ops:
  0.6 74.9 %copy-start = (bf16[256,256]{1,0:T(8,128)(2,1)S(1)}, bf16[256,256]{1,0:T(8,128)(2,1)}, u32[]{:S(2)}) copy-start(bf16[256,256]{1,0:T(8,128)(2,1)} %param.14) | copy-start | bytes 393220
  0.6 45.0 %copy-start.20 = (bf16[3,256,256]{2,1,0:T(8,128)(2,1)S(1)}, bf16[3,256,256]{2,1,0:T(8,128)(2,1)}, u32[]{:S(2)}) copy-start(bf16[3,256,256]{2,1,0:T(8,128)(2,1)} %param.12) | copy-start | bytes 1179652
  1.5 45.1 %copy-start.14 = (bf16[9,256,256]{2,1,0:T(8,128)(2,1)S(1)}, bf16[9,256,256]{2,1,0:T(8,128)(2,1)}, u32[]{:S(2)}) copy-start(bf16[9,256,256]{2,1,0:T(8,128)(2,1)} %param.11) | copy-start | bytes 3538948
  18.2 5.3 %collective-permute-start = (bf16[8,32,256]{2,1,0:T(8,128)(2,1)S(1)}, bf16[8,32,256]{2,1,0:T(8,128)(2,1)S(1)}, u32[]{:S(2)}, u32[]{:S(2)}) collective-permute-start(bf16[8,32,256]{2,1,0:T(8,128)(2,1)S(1)} %all_to_all.15), channel_id=1, source_target_pairs={{0,128},{128,0},{1,129},{129,1},{2,130},{130,2},{3,131},{131,3},{4... | collective-permute-start | bytes 393224 | tf_op jit(solution)/shard_map/ppermute | solution.py:41
  23.6 5.3 %collective-permute-start.3 = (bf16[2,8,32,256]{3,2,1,0:T(8,128)(2,1)S(1)}, bf16[2,8,32,256]{3,2,1,0:T(8,128)(2,1)S(1)}, u32[]{:S(2)}, u32[]{:S(2)}) collective-permute-start(bf16[2,8,32,256]{3,2,1,0:T(8,128)(2,1)S(1)} %pad_maximum_fusion.15), channel_id=1, source_target_pairs={{0,4},{4,0},{8,12},{12,8},{1,5},{5,1},{9,13},{13,9},{2,6},{6,2},{1... | collective-permute-start | bytes 786440 | tf_op jit(solution)/shard_map/ppermute | solution.py:41
  25.0 10.9 %collective-permute-start.2 = (bf16[2,8,32,256]{3,2,1,0:T(8,128)(2,1)S(1)}, bf16[2,8,32,256]{3,2,1,0:T(8,128)(2,1)S(1)}, u32[]{:S(2)}, u32[]{:S(2)}) collective-permute-start(bf16[2,8,32,256]{3,2,1,0:T(8,128)(2,1)S(1)} %pad_maximum_fusion.15), channel_id=1, source_target_pairs={{0,8},{4,12},{8,0},{12,4},{1,9},{5,13},{9,1},{13,5},{2,10},{6,14},... | collective-permute-start | bytes 786440 | tf_op jit(solution)/shard_map/ppermute | solution.py:41
  27.6 13.4 %collective-permute-start.1 = (bf16[2,8,32,256]{3,2,1,0:T(8,128)(2,1)S(1)}, bf16[2,8,32,256]{3,2,1,0:T(8,128)(2,1)}, u32[]{:S(2)}, u32[]{:S(2)}) collective-permute-start(bf16[2,8,32,256]{3,2,1,0:T(8,128)(2,1)S(1)} %pad_maximum_fusion.15), channel_id=1, source_target_pairs={{0,12},{4,8},{8,4},{12,0},{1,13},{5,9},{9,5},{13,1},{2,14},{6,10},... | collective-permute-start | bytes 786440 | tf_op jit(solution)/shard_map/ppermute | solution.py:41
  42.1 6.0 %copy-start.23 = (s32[1,4096]{1,0:T(1,128)S(1)}, s32[1,4096]{1,0:T(1,128)}, u32[]{:S(2)}) copy-start(s32[1,4096]{1,0:T(1,128)} %param.10) | copy-start | bytes 49156
  42.1 6.0 %copy-start.13 = (bf16[1,256,256]{2,1,0:T(8,128)(2,1)S(1)}, bf16[1,256,256]{2,1,0:T(8,128)(2,1)}, u32[]{:S(2)}) copy-start(bf16[1,256,256]{2,1,0:T(8,128)(2,1)} %param.17) | copy-start | bytes 393220
  42.1 6.0 %copy-start.22 = (bf16[256,256]{1,0:T(8,128)(2,1)S(1)}, bf16[256,256]{1,0:T(8,128)(2,1)}, u32[]{:S(2)}) copy-start(bf16[256,256]{1,0:T(8,128)(2,1)} %param.16) | copy-start | bytes 393220
  43.2 5.1 %collective-permute-start.4 = (bf16[4,2,8,32,256]{4,3,0,2,1:T(8,128)(2,1)}, bf16[4,2,8,32,256]{4,3,0,2,1:T(8,128)(2,1)}, u32[]{:S(2)}, u32[]{:S(2)}) collective-permute-start(bf16[4,2,8,32,256]{4,3,0,2,1:T(8,128)(2,1)} %pad_maximum_fusion.11), channel_id=1, source_target_pairs={{0,2},{2,0},{1,3},{3,1},{4,6},{6,4},{5,7},{7,5},{8,10},{10,8},{9,1... | collective-permute-start | bytes 3145736 | tf_op jit(solution)/shard_map/ppermute | solution.py:41
  51.7 1.3 copy-start.15
  52.3 8.8 %copy-start.5 = (bf16[64,8,8,256]{3,2,1,0:T(8,128)(2,1)}, bf16[64,8,8,256]{3,2,1,0:T(8,128)(2,1)S(1)}, u32[]{:S(2)}) copy-start(bf16[64,8,8,256]{3,2,1,0:T(8,128)(2,1)S(1)} %concatenate.86) | copy-start | bytes 6291460
  72.3 3.0 %copy-start.19 = (bf16[256,256]{1,0:T(8,128)(2,1)S(1)}, bf16[256,256]{1,0:T(8,128)(2,1)}, u32[]{:S(2)}) copy-start(bf16[256,256]{1,0:T(8,128)(2,1)} %param.13) | copy-start | bytes 393220
  77.1 0.9 copy-start.18
  83.3 0.9 copy-start.16
  83.8 9.8 %copy-start.7 = (bf16[4096,128]{0,1:T(8,128)(2,1)}, bf16[4096,128]{0,1:T(8,128)(2,1)S(1)}, u32[]{:S(2)}) copy-start(bf16[4096,128]{0,1:T(8,128)(2,1)S(1)} %convolution_convert_fusion.3) | copy-start | bytes 3145732
  84.2 9.3 %copy-start.9 = (bf16[4096,128]{0,1:T(8,128)(2,1)}, bf16[4096,128]{0,1:T(8,128)(2,1)S(1)}, u32[]{:S(2)}) copy-start(bf16[4096,128]{0,1:T(8,128)(2,1)S(1)} %convolution_convert_fusion.4) | copy-start | bytes 3145732
  91.8 1.0 copy-start.4
  94.8 2.7 %copy-start.3 = (bf16[4096,256]{1,0:T(8,128)(2,1)}, bf16[4096,256]{1,0:T(8,128)(2,1)S(1)}, u32[]{:S(2)}) copy-start(bf16[4096,256]{1,0:T(8,128)(2,1)S(1)} %convert_element_type.147) | copy-start | bytes 6291460
  97.6 2.5 %copy-start.6 = (bf16[64,8,8,256]{3,2,1,0:T(8,128)(2,1)S(1)}, bf16[64,8,8,256]{3,2,1,0:T(8,128)(2,1)}, u32[]{:S(2)}) copy-start(bf16[64,8,8,256]{3,2,1,0:T(8,128)(2,1)} %copy-done.5) | copy-start | bytes 6291460
  140.7 1.7 copy-start.12
  140.9 1.4 copy-start.2
  144.1 2.6 %collective-permute-start.5 = (bf16[1536,256]{1,0:T(8,128)(2,1)}, bf16[1536,256]{1,0:T(8,128)(2,1)}, u32[]{:S(2)}, u32[]{:S(2)}) collective-permute-start(bf16[1536,256]{1,0:T(8,128)(2,1)} %fusion.51), channel_id=1, source_target_pairs={{0,2},{2,0},{1,3},{3,1},{4,6},{6,4},{5,7},{7,5},{8,10},{10,8},{9,1... | collective-permute-start | bytes 2359304 | tf_op jit(solution)/shard_map/ppermute | solution.py:49
  150.8 6.5 %collective-permute-start.6 = (bf16[384,256]{1,0:T(8,128)(2,1)}, bf16[384,256]{1,0:T(8,128)(2,1)}, u32[]{:S(2)}, u32[]{:S(2)}) collective-permute-start(bf16[384,256]{1,0:T(8,128)(2,1)} %get-tuple-element.40), channel_id=1, source_target_pairs={{0,4},{4,0},{8,12},{12,8},{1,5},{5,1},{9,13},{13,9},{2,6},{6,2},{1... | collective-permute-start | bytes 589832 | tf_op jit(solution)/shard_map/ppermute | solution.py:49
  150.8 11.9 %collective-permute-start.8 = (bf16[384,256]{1,0:T(8,128)(2,1)}, bf16[384,256]{1,0:T(8,128)(2,1)}, u32[]{:S(2)}, u32[]{:S(2)}) collective-permute-start(bf16[384,256]{1,0:T(8,128)(2,1)} %get-tuple-element.41), channel_id=1, source_target_pairs={{0,12},{4,8},{8,4},{12,0},{1,13},{5,9},{9,5},{13,1},{2,14},{6,10},... | collective-permute-start | bytes 589832 | tf_op jit(solution)/shard_map/ppermute | solution.py:49
  150.8 11.9 %collective-permute-start.7 = (bf16[384,256]{1,0:T(8,128)(2,1)}, bf16[384,256]{1,0:T(8,128)(2,1)}, u32[]{:S(2)}, u32[]{:S(2)}) collective-permute-start(bf16[384,256]{1,0:T(8,128)(2,1)} %get-tuple-element.42), channel_id=1, source_target_pairs={{0,8},{4,12},{8,0},{12,4},{1,9},{5,13},{9,1},{13,5},{2,10},{6,14},... | collective-permute-start | bytes 589832 | tf_op jit(solution)/shard_map/ppermute | solution.py:49
  164.3 2.2 copy-start.8
  164.3 2.2 copy-start.10
  166.5 0.8 copy-start.17
  166.5 0.9 copy-start.21
  167.5 1.1 copy-start.11
  168.8 5.0 %collective-permute-start.9 = (bf16[352,256]{1,0:T(8,128)(2,1)S(1)}, bf16[352,256]{1,0:T(8,128)(2,1)S(1)}, u32[]{:S(2)}, u32[]{:S(2)}) collective-permute-start(bf16[352,256]{1,0:T(8,128)(2,1)S(1)} %get-tuple-element.47), channel_id=1, source_target_pairs={{0,1},{1,0},{128,129},{129,128},{2,3},{3,2},{130,131},{131,130},{4... | collective-permute-start | bytes 540680 | tf_op jit(solution)/shard_map/ppermute | solution.py:49
  170.1 5.6 %collective-permute-start.11 = (bf16[352,256]{1,0:T(8,128)(2,1)S(1)}, bf16[352,256]{1,0:T(8,128)(2,1)S(1)}, u32[]{:S(2)}, u32[]{:S(2)}) collective-permute-start(bf16[352,256]{1,0:T(8,128)(2,1)S(1)} %get-tuple-element.48), channel_id=1, source_target_pairs={{0,129},{1,128},{128,1},{129,0},{2,131},{3,130},{130,3},{131,2},{4... | collective-permute-start | bytes 540680 | tf_op jit(solution)/shard_map/ppermute | solution.py:49
  171.9 8.3 %collective-permute-start.10 = (bf16[352,256]{1,0:T(8,128)(2,1)S(1)}, bf16[352,256]{1,0:T(8,128)(2,1)S(1)}, u32[]{:S(2)}, u32[]{:S(2)}) collective-permute-start(bf16[352,256]{1,0:T(8,128)(2,1)S(1)} %get-tuple-element.49), channel_id=1, source_target_pairs={{0,128},{1,129},{128,0},{129,1},{2,130},{3,131},{130,2},{131,3},{4... | collective-permute-start | bytes 540680 | tf_op jit(solution)/shard_map/ppermute | solution.py:49
  203.6 4.4 %collective-permute-start.14 = (bf16[352,256]{1,0:T(8,128)(2,1)S(1)}, bf16[352,256]{1,0:T(8,128)(2,1)S(1)}, u32[]{:S(2)}, u32[]{:S(2)}) collective-permute-start(bf16[352,256]{1,0:T(8,128)(2,1)S(1)} %reshape.115), channel_id=1, source_target_pairs={{0,1},{1,0},{128,129},{129,128},{2,3},{3,2},{130,131},{131,130},{4... | collective-permute-start | bytes 540680 | tf_op jit(solution)/shard_map/ppermute | solution.py:41
  203.7 7.6 %collective-permute-start.13 = (bf16[352,256]{1,0:T(8,128)(2,1)S(1)}, bf16[352,256]{1,0:T(8,128)(2,1)S(1)}, u32[]{:S(2)}, u32[]{:S(2)}) collective-permute-start(bf16[352,256]{1,0:T(8,128)(2,1)S(1)} %reshape.115), channel_id=1, source_target_pairs={{0,128},{1,129},{128,0},{129,1},{2,130},{3,131},{130,2},{131,3},{4... | collective-permute-start | bytes 540680 | tf_op jit(solution)/shard_map/ppermute | solution.py:41
  206.4 6.7 %collective-permute-start.12 = (bf16[352,256]{1,0:T(8,128)(2,1)S(1)}, bf16[352,256]{1,0:T(8,128)(2,1)S(1)}, u32[]{:S(2)}, u32[]{:S(2)}) collective-permute-start(bf16[352,256]{1,0:T(8,128)(2,1)S(1)} %reshape.115), channel_id=1, source_target_pairs={{0,129},{1,128},{128,1},{129,0},{2,131},{3,130},{130,3},{131,2},{4... | collective-permute-start | bytes 540680 | tf_op jit(solution)/shard_map/ppermute | solution.py:41
  213.3 4.9 %collective-permute-start.17 = (bf16[384,256]{1,0:T(8,128)(2,1)S(1)}, bf16[384,256]{1,0:T(8,128)(2,1)S(1)}, u32[]{:S(2)}, u32[]{:S(2)}) collective-permute-start(bf16[384,256]{1,0:T(8,128)(2,1)S(1)} %pad_maximum_fusion.16), channel_id=1, source_target_pairs={{0,4},{4,0},{8,12},{12,8},{1,5},{5,1},{9,13},{13,9},{2,6},{6,2},{1... | collective-permute-start | bytes 589832 | tf_op jit(solution)/shard_map/ppermute | solution.py:41
  213.4 7.7 %collective-permute-start.16 = (bf16[384,256]{1,0:T(8,128)(2,1)S(1)}, bf16[384,256]{1,0:T(8,128)(2,1)S(1)}, u32[]{:S(2)}, u32[]{:S(2)}) collective-permute-start(bf16[384,256]{1,0:T(8,128)(2,1)S(1)} %pad_maximum_fusion.16), channel_id=1, source_target_pairs={{0,8},{4,12},{8,0},{12,4},{1,9},{5,13},{9,1},{13,5},{2,10},{6,14},... | collective-permute-start | bytes 589832 | tf_op jit(solution)/shard_map/ppermute | solution.py:41
  215.8 7.3 %collective-permute-start.15 = (bf16[384,256]{1,0:T(8,128)(2,1)S(1)}, bf16[384,256]{1,0:T(8,128)(2,1)S(1)}, u32[]{:S(2)}, u32[]{:S(2)}) collective-permute-start(bf16[384,256]{1,0:T(8,128)(2,1)S(1)} %pad_maximum_fusion.16), channel_id=1, source_target_pairs={{0,12},{4,8},{8,4},{12,0},{1,13},{5,9},{9,5},{13,1},{2,14},{6,10},... | collective-permute-start | bytes 589832 | tf_op jit(solution)/shard_map/ppermute | solution.py:41
  223.2 8.6 %collective-permute-start.18 = (bf16[1536,256]{1,0:T(8,128)(2,1)S(1)}, bf16[1536,256]{1,0:T(8,128)(2,1)S(1)}, u32[]{:S(2)}, u32[]{:S(2)}) collective-permute-start(bf16[1536,256]{1,0:T(8,128)(2,1)S(1)} %pad_maximum_fusion.12), channel_id=1, source_target_pairs={{0,2},{2,0},{1,3},{3,1},{4,6},{6,4},{5,7},{7,5},{8,10},{10,8},{9,1... | collective-permute-start | bytes 2359304 | tf_op jit(solution)/shard_map/ppermute | solution.py:41
  233.1 1.8 copy-start.1

commit v2 on v1

v2 whole, which is shorter than its diff:
```python
import functools

import jax
import jax.numpy as jnp
from jax import lax
from jax.experimental import pallas as pl
from jax.experimental.pallas import tpu as pltpu
from jax.sharding import Mesh, PartitionSpec as P

HD = 128
SIDE = 8
FRAME = SIDE * SIDE
NEG_FILL = -1e30
LOG2E = 1.4426950408889634
BF = jnp.bfloat16
F32 = jnp.float32


def dot(left, right):
    return jnp.dot(left, right, preferred_element_type=F32)


def contract_rows(left, right):
    return lax.dot_general(left, right, (((0,), (0,)), ((), ())), preferred_element_type=F32)


def dot_t(left, right):
    return lax.dot_general(left, right, (((1,), (1,)), ((), ())), preferred_element_type=F32)


def xor_perm(count, step):
    return [(i, i ^ step) for i in range(count)]


def unxor(parts, index):
    parts = list(parts)
    bit = 1
    while bit < len(parts):
        odd = (index & bit) != 0
        parts = [jnp.where(odd, parts[s ^ bit], parts[s]) for s in range(len(parts))]
        bit *= 2
    return parts


def gather_xor(block, axis, count, index):
    parts = [block] + [lax.ppermute(block, axis, xor_perm(count, s)) for s in range(1, count)]
    return unxor(parts, index)


def scatter_xor(total, axis, count, index):
    rows = total.shape[0] // count
    low = total.astype(BF)
    got = [
        lax.ppermute(
            lax.dynamic_slice_in_dim(low, (index ^ s) * rows, rows), axis, xor_perm(count, s)
        )
        for s in range(1, count)
    ]
    own = lax.dynamic_slice_in_dim(total, index * rows, rows)
    for part in got:
        own = own + part.astype(F32)
    return own


def spread(block, axis, count):
    return lax.all_to_all(
        jnp.broadcast_to(block[None], (count,) + block.shape), axis, 0, 0
    )


def roll_cols(block, step):
    groups = block.reshape(-1, SIDE, block.shape[1])
    place = lax.broadcasted_iota(jnp.int32, groups.shape, 1)
    if step < 0:
        moved = jnp.where(place == 0, 0.0, pltpu.roll(groups, 1, 1))
    else:
        moved = jnp.where(place == SIDE - 1, 0.0, pltpu.roll(groups, SIDE - 1, 1))
    return moved.reshape(block.shape)


def move_rows(field, step):
    pad = jnp.zeros((field.shape[0], SIDE, field.shape[2]), field.dtype)
    if step > 0:
        return jnp.concatenate([field[:, SIDE:], pad], axis=1)
    return jnp.concatenate([pad, field[:, :-SIDE]], axis=1)


def local_kernel(
    dims,
    pos,
    ids_ref,
    own_ids_ref,
    *refs,
):
    n_xh, n_z, n_y, n_c, chunk = dims
    n_parts = n_y * n_c
    parts = refs[:n_parts]
    w_sp, w_t, w_q, w_k, w_v, w_o, up_ref = refs[n_parts : n_parts + 7]
    send_ref, keep_ref, head_ref = refs[n_parts + 7 : n_parts + 10]
    (
        cols,
        slope,
        hid,
        feat,
        keys,
        values,
        gkey,
        gval,
        gf,
        e_ref,
        acc,
        q_ref,
        g_ref,
        att_ref,
        gq_ref,
    ) = refs[n_parts + 10 :]
    my_xh, my_y, my_c = pos[0], pos[1], pos[2]
    first = pl.multiple_of(pos[3], 256)
    tokens, ch = feat.shape
    local = up_ref.shape[0]
    half = parts[0].shape[2]
    n_chunk = tokens // chunk
    frames = chunk // FRAME
    scale = HD ** (-0.5)
    n_head = n_y * n_c

    @pl.loop(0, n_z)
    def _(z):
        for s in range(n_y):
            for t in range(n_c):
                for u in range(n_xh):
                    frame = ((my_xh ^ u) * n_z + z) * n_y + (my_y ^ s)
                    row = pl.multiple_of(frame * FRAME + (my_c ^ t) * half, half)
                    low = parts[s * n_c + t][u, z]
                    wide = low.astype(F32)
                    cols[pl.ds(row, half), 0:ch] = roll_cols(wide, -1).astype(BF)
                    cols[pl.ds(row, half), ch : 2 * ch] = low
                    cols[pl.ds(row, half), 2 * ch : 3 * ch] = roll_cols(wide, 1).astype(BF)

    edge = jnp.zeros((FRAME, ch), BF)
    hid[0:FRAME, :] = edge
    hid[tokens + FRAME : tokens + 2 * FRAME, :] = edge
    gf[0:FRAME, :] = edge
    gf[tokens + FRAME : tokens + 2 * FRAME, :] = edge
    acc[...] = jnp.zeros_like(acc)
    head_ref[...] = jnp.zeros_like(head_ref)

    @pl.loop(0, n_chunk)
    def _(i):
        row = pl.multiple_of(i * chunk, chunk)
        x = cols[pl.ds(row, chunk), :]
        mix = [
            dot(x, w_sp[a * 3 * ch : (a + 1) * 3 * ch, :]).reshape(frames, FRAME, ch)
            for a in range(3)
        ]
        pre = mix[1] + move_rows(mix[0], -1) + move_rows(mix[2], 1)
        pre = pre.reshape(chunk, ch)
        sigma = jax.nn.sigmoid(pre)
        slope[pl.ds(row, chunk), :] = sigma * (1.0 + pre * (1.0 - sigma))
        hid[pl.ds(pl.multiple_of(row + FRAME, FRAME), chunk), :] = (pre * sigma).astype(BF)

    @pl.loop(0, n_chunk)
    def _(i):
        row = pl.multiple_of(i * chunk, chunk)
        total = dot(hid[pl.ds(row, chunk), :], w_t[0:ch, :])
        for d in range(1, 3):
            at = pl.multiple_of(row + d * FRAME, FRAME)
            total = total + dot(hid[pl.ds(at, chunk), :], w_t[d * ch : (d + 1) * ch, :])
        low = total.astype(BF)
        feat[pl.ds(row, chunk), :] = low
        keys[pl.ds(row, chunk), :] = dot(low, w_k[...]).astype(BF)
        values[pl.ds(row, chunk), :] = dot(low, w_v[...]).astype(BF)

    q_ref[...] = dot(feat[pl.ds(first, local), :], w_q[...]).astype(BF)
    g_ref[...] = dot_t(up_ref[...], w_o[...]).astype(BF)

    def fold(block, join):
        out = block[:, 0:HD]
        for k in range(1, block.shape[1] // HD):
            out = join(out, block[:, k * HD : (k + 1) * HD])
        return out

    for h in range(q_ref.shape[1] // HD):
        sel = slice(h * HD, (h + 1) * HD)

        def raw(i, top):
            row = pl.multiple_of(i * chunk, chunk)
            s = dot_t(q_ref[:, sel], keys[pl.ds(row, chunk), sel])
            s = jnp.where(ids_ref[:, pl.ds(row, chunk)] <= own_ids_ref[...], s, NEG_FILL)
            e_ref[:, pl.ds(row, chunk)] = s
            return jnp.maximum(top, fold(s, jnp.maximum))

        top = lax.fori_loop(0, n_chunk, raw, jnp.full((local, HD), NEG_FILL, F32))
        top = jnp.max(top, axis=1, keepdims=True)

        def forward(i, carry):
            total, out = carry
            row = pl.multiple_of(i * chunk, chunk)
            e = jnp.exp2((e_ref[:, pl.ds(row, chunk)] - top) * (scale * LOG2E))
            e_ref[:, pl.ds(row, chunk)] = e
            total = total + fold(e, jnp.add)
            return total, out + dot(e.astype(BF), values[pl.ds(row, chunk), sel])

        zero = jnp.zeros((local, HD), F32)
        total, out = lax.fori_loop(0, n_chunk, forward, (zero, zero))
        inv = 1.0 / jnp.sum(total, axis=1, keepdims=True)
        att = (out * inv).astype(BF)
        att_ref[:, sel] = att
        delta = jnp.sum(g_ref[:, sel].astype(F32) * att.astype(F32), axis=1, keepdims=True)

        def backward(i, gq):
            row = pl.multiple_of(i * chunk, chunk)
            p = e_ref[:, pl.ds(row, chunk)] * inv
            g = g_ref[:, sel]
            k = keys[pl.ds(row, chunk), sel]
            ds = (p * (dot_t(g, values[pl.ds(row, chunk), sel]) - delta)).astype(BF)
            gkey[pl.ds(row, chunk), sel] = (contract_rows(ds, q_ref[:, sel]) * scale).astype(BF)
            gval[pl.ds(row, chunk), sel] = contract_rows(p.astype(BF), g).astype(BF)
            return gq + dot(ds, k)

        gq = lax.fori_loop(0, n_chunk, backward, zero)
        gq_ref[:, sel] = (gq * scale).astype(BF)

    @pl.loop(0, n_chunk)
    def _(i):
        row = pl.multiple_of(i * chunk, chunk)
        gk, gv = gkey[pl.ds(row, chunk), :], gval[pl.ds(row, chunk), :]
        f = feat[pl.ds(row, chunk), :]
        at = pl.multiple_of(row + FRAME, FRAME)
        gf[pl.ds(at, chunk), :] = (dot_t(gk, w_k[...]) + dot_t(gv, w_v[...])).astype(BF)
        head_ref[ch : 2 * ch, :] += contract_rows(f, gk)
        head_ref[2 * ch : 3 * ch, :] += contract_rows(f, gv)

    own = pl.ds(first, local)
    up = up_ref[...]
    total = dot_t(gkey[own, :], w_k[...]) + dot_t(gval[own, :], w_v[...])
    total = total + dot_t(gq_ref[...], w_q[...]) + up.astype(F32) * (1.0 / n_head)
    gf[pl.ds(pl.multiple_of(first + FRAME, FRAME), local), :] = total.astype(BF)
    head_ref[0:ch, :] = contract_rows(feat[own, :], gq_ref[...])
    head_ref[3 * ch : 4 * ch, :] = contract_rows(att_ref[...], up)

    @pl.loop(0, n_chunk)
    def _(i):
        row = pl.multiple_of(i * chunk, chunk)
        here = gf[pl.ds(pl.multiple_of(row + FRAME, FRAME), chunk), :]
        back = jnp.zeros((chunk, ch), F32)
        for d in range(3):
            at = pl.multiple_of(row + d * FRAME, FRAME)
            acc[(9 + d) * ch : (10 + d) * ch, :] += contract_rows(hid[pl.ds(at, chunk), :], here)
            at = pl.multiple_of(row + (2 - d) * FRAME, FRAME)
            back = back + dot_t(gf[pl.ds(at, chunk), :], w_t[d * ch : (d + 1) * ch, :])
        gp = (back * slope[pl.ds(row, chunk), :]).reshape(frames, FRAME, ch)
        x = cols[pl.ds(row, chunk), :]
        for a in range(3):
            moved = gp if a == 1 else move_rows(gp, 1 - a)
            moved = moved.reshape(chunk, ch).astype(BF)
            acc[a * 3 * ch : (a + 1) * 3 * ch, :] += contract_rows(x, moved)

    half_rows = keep_ref.shape[0]
    send_ref[...] = acc[pl.ds(pl.multiple_of((1 - my_c) * half_rows, half_rows), half_rows), :].astype(BF)
    keep_ref[...] = acc[pl.ds(pl.multiple_of(my_c * half_rows, half_rows), half_rows), :]


def local_terms(sizes, pos, ids, own_ids, parts, weights, up, chunk=512):
    n_xh, n_z, n_y, n_c, _ = sizes
    local, ch = up.shape
    tokens = local * n_xh * n_z
    wide = weights[2].shape[1]
    dims = (n_xh, n_z, n_y, n_c, chunk)
    vm = pl.BlockSpec(memory_space=pltpu.VMEM)
    n_in = 2 + len(parts) + len(weights) + 1
    return pl.pallas_call(
        functools.partial(local_kernel, dims),
        name="local_terms",
        out_shape=(
            jax.ShapeDtypeStruct((6 * ch, ch), BF),
            jax.ShapeDtypeStruct((6 * ch, ch), F32),
            jax.ShapeDtypeStruct((4 * ch, ch), F32),
        ),
        in_specs=[pl.BlockSpec(memory_space=pltpu.SMEM)] + [vm] * n_in,
        out_specs=(vm, vm, vm),
        scratch_shapes=[
            pltpu.VMEM((tokens, 3 * ch), BF),
            pltpu.VMEM((tokens, ch), F32),
            pltpu.VMEM((tokens + 2 * FRAME, ch), BF),
            pltpu.VMEM((tokens, ch), BF),
            pltpu.VMEM((tokens, wide), BF),
            pltpu.VMEM((tokens, wide), BF),
            pltpu.VMEM((tokens, wide), BF),
            pltpu.VMEM((tokens, wide), BF),
            pltpu.VMEM((tokens + 2 * FRAME, ch), BF),
            pltpu.VMEM((local, tokens), F32),
            pltpu.VMEM((12 * ch, ch), F32),
            pltpu.VMEM((local, wide), BF),
            pltpu.VMEM((local, wide), BF),
            pltpu.VMEM((local, wide), BF),
            pltpu.VMEM((local, wide), BF),
        ],
        compiler_params=pltpu.CompilerParams(vmem_limit_bytes=58 * 2**20),
        cost_estimate=pl.CostEstimate(
            flops=24 * 10**9, transcendentals=2 * local * tokens, bytes_accessed=12 * 2**20
        ),
    )(pos, ids, own_ids, *parts, *weights, up)


def on_device(sizes, clip, block_ids, w_spatial, w_temporal, w_query, w_key, w_value, w_out, cotangent):
    n_xh, n_z, n_y, n_c, n_dp = sizes
    i_xh, i_y, i_c, i_dp = (lax.axis_index(a) for a in ("xh", "y", "c", "dp"))
    i_x = i_xh * n_dp + i_dp
    n_head = n_y * n_c
    n_frame = n_xh * n_z
    own_clip = clip[0]
    upstream = cotangent[0]
    ids = block_ids[0]
    local, ch = own_clip.shape
    tokens = local * n_frame

    piece = local // n_head
    mine = lax.dynamic_slice_in_dim(own_clip, lax.axis_index(("y", "c")) * piece, piece)
    part = spread(mine, "z", n_z)
    part = jnp.stack([part, lax.ppermute(part, "xh", xor_perm(n_xh, 1))])
    parts = []
    for s in range(n_y):
        block = part if s == 0 else lax.ppermute(part, "y", xor_perm(n_y, s))
        parts += [block, lax.ppermute(block, "c", xor_perm(n_c, 1))]

    first = lax.axis_index(("xh", "z")) * local
    pos = jnp.stack([i_xh, i_y, i_c, first]).astype(jnp.int32)
    own_ids = lax.dynamic_slice_in_dim(ids, first, local)[:, None]
    weights = (
        w_spatial.reshape(9 * ch, ch),
        w_temporal.reshape(3 * ch, ch),
        w_query,
        w_key,
        w_value,
        w_out,
    )
    send, keep, g_head = local_terms(sizes, pos, ids[None], own_ids, parts, weights, upstream)

    shared = keep + lax.ppermute(send, "c", xor_perm(n_c, 1)).astype(F32)
    shared = scatter_xor(shared, "y", n_y, i_y)
    block = jnp.concatenate([shared, g_head])
    n_x = n_xh * n_dp
    block = scatter_xor(block, ("xh", "dp"), n_x, i_x)
    rows = block.shape[0] // n_z
    got = lax.all_to_all(block.astype(BF).reshape(n_z, rows, ch), "z", 0, 0)
    factor = float(n_dp * tokens) ** (-0.5)
    done = (jnp.sum(got.astype(F32), axis=0) * factor).astype(BF)
    done = spread(done, "z", n_z).reshape(n_z * rows, ch)
    done = jnp.concatenate(gather_xor(done, ("xh", "dp"), n_x, i_x))
    cut = shared.shape[0]
    heads = done[cut:].astype(F32).reshape(4, ch, -1)
    done = jnp.concatenate(gather_xor(done[:cut], "y", n_y, i_y))
    done = jnp.concatenate(gather_xor(done, "c", n_c, i_c)).astype(F32)
    return (
        done[: 9 * ch].reshape(9, ch, ch),
        done[9 * ch :].reshape(3, ch, ch),
        heads[0],
        heads[1],
        heads[2],
        heads[3],
    )


def solution(mesh):
    frame, head, dp = (mesh.shape[a] for a in ("frame", "head", "dp"))
    sizes = (2, frame // 2, head // 2, 2, dp)
    names = ("xh", "z", "y", "c", "dp")
    fine = Mesh(mesh.devices.reshape(sizes), names)
    rows, head_axes = ("xh", "z"), ("y", "c")
    in_specs = (
        P("dp", rows, None),
        P("dp", None),
        P(),
        P(),
        P(None, head_axes),
        P(None, head_axes),
        P(None, head_axes),
        P(head_axes, None),
        P("dp", rows, None),
    )
    out_specs = (
        P(),
        P(),
        P(None, head_axes),
        P(None, head_axes),
        P(None, head_axes),
        P(head_axes, None),
    )

    def body(*args):
        return on_device(sizes, *args)

    return jax.shard_map(
        body, mesh=fine, in_specs=in_specs, out_specs=out_specs, check_vma=False
    )
```

time: 239 us -> 182 us (0.76); the launches traced: 235 us -> 182 us
  Pallas kernels: 0 us -> 54.3 us
  matrix products: 46.2 us -> 0 us
  local copies, waits for them, and re-layouts: 37.6 us -> 6.68 us
  other arithmetic: 32.9 us -> 5.23 us
  waiting for transfers between devices: 46.7 us -> 40.3 us
  starting transfers between devices: 31.2 us -> 35.5 us
    pallas_call x0 -> x1, Pallas kernels: none -> 54.3 us  [local_terms(): pl.pallas_call(functools.partial(local_kernel, dims), name='local_terms',...]
    dot_general x28 -> x0, matrix products: 46.2 us -> none  [the longest x10 22 us: dot(): return jnp.dot(left, right, preferred_element_type=F32)]
    ppermute x12 -> x7, waiting for transfers between devices: 28.3 us -> 12.7 us  [gather_xor(): lax.ppermute(block, axis, xor_perm(count, s))]
    ppermute x0 -> x9, starting transfers between devices: none -> 13.5 us  [the longest x4 7.29 us: on_device(): parts += [block, lax.ppermute(block, 'c', xor_perm(n_c, 1))]]
    ppermute x0 -> x9, waiting for transfers between devices: none -> 10.7 us  [the longest x3 5.66 us: on_device(): block = part if s == 0 else lax.ppermute(part, 'y', xor_perm(n_y, s))]
    ppermute x12 -> x7, starting transfers between devices: 23.7 us -> 14.5 us  [gather_xor(): lax.ppermute(block, axis, xor_perm(count, s))]
    reshape x1 -> x0, local copies, waits for them, and re-layouts: 8.72 us -> none  [on_device(): g_ws = contract_rows(cols, rows.reshape(tokens, 3 * ch))]
    dot_general x1 -> x0, local copies, waits for them, and re-layouts: 8.54 us -> none  [contract_rows(): lax.dot_general(left, right, (((0,), (0,)), ((), ())), preferred_element_...]
  transfers between devices with their start and end apart: 19 -> 22, of which waited for: 17 -> 16; matrix products, arithmetic and copies ran while one was open for 2% -> 2% of each run, Pallas kernels for 0% -> 0%
where the time goes in v2:
time: 182 us
  Pallas kernels  54.3 us (30%)
  waiting for transfers between devices  40.3 us (22%)
  blocking collectives  38.8 us (21%)
  starting transfers between devices  35.5 us (20%)
  local copies, waits for them, and re-layouts  6.68 us (4%)
  other arithmetic  5.23 us (3%)
    pallas_call x1, Pallas kernels, local_terms(): pl.pallas_call(functools.partial(local_kernel, dims), name='local_terms',...  54.3 us
    all_to_all x2, blocking collectives, spread(): lax.all_to_all(jnp.broadcast_to(block[None], (count,) + block.shape), axi...  27.7 us
    ppermute x6, waiting for transfers between devices, scatter_xor(): lax.ppermute(lax.dynamic_slice_in_dim(low, (index ^ s) * rows, rows), axi...  16.9 us
    ppermute x7, starting transfers between devices, gather_xor(): lax.ppermute(block, axis, xor_perm(count, s))  14.5 us
    ppermute x7, waiting for transfers between devices, gather_xor(): lax.ppermute(block, axis, xor_perm(count, s))  12.7 us
    all_to_all x1, blocking collectives, on_device(): got = lax.all_to_all(block.astype(BF).reshape(n_z, rows, ch), 'z', 0, 0)  11.1 us
    ppermute x6, starting transfers between devices, scatter_xor(): lax.ppermute(lax.dynamic_slice_in_dim(low, (index ^ s) * rows, rows), axi...  7.47 us
    ppermute x4, starting transfers between devices, on_device(): parts += [block, lax.ppermute(block, 'c', xor_perm(n_c, 1))]  7.29 us
  transfers between devices with their start and end apart: 22, of which 16 were waited for; matrix products, arithmetic and copies ran while one was open for 2% of the time, Pallas kernels for 0%

profile of v2, /device:TPU:1, one launch (start us, length us, event | category | flops | bytes accessed | tf_op | source)
XLA Modules:
  0.0 181.7 jit_solution(15597473863659726719)
XLA Ops:
  0.7 0.9 copy-done
  1.6 16.6 %all_to_all.15 = bf16[8,32,256]{2,1,0:T(8,128)(2,1)S(1)} all-to-all(bf16[8,32,256]{2,1,0:T(8,128)(2,1)S(1)} %broadcast_in_dim.19), channel_id=1, replica_groups=mesh['xh'=2,'z'=8,'y'=4,'c'=2,'dp'=2] {'z'}, dimensions={0} | all-to-all | bytes 262144 | tf_op jit(solution)/shard_map/all_to_all | solution.py:66
  18.1 2.7 %collective-permute-start = (bf16[8,32,256]{2,1,0:T(8,128)(2,1)S(1)}, bf16[8,32,256]{2,1,0:T(8,128)(2,1)S(1)}, u32[]{:S(2)}, u32[]{:S(2)}) collective-permute-start(bf16[8,32,256]{2,1,0:T(8,128)(2,1)S(1)} %all_to_all.15), channel_id=1, source_target_pairs={{0,128},{128,0},{1,129},{129,1},{2,130},{130,2},{3,131},{131,3},{4... | collective-permute-start | bytes 393224 | tf_op jit(solution)/shard_map/ppermute | solution.py:321
  20.9 2.6 %collective-permute-done = bf16[8,32,256]{2,1,0:T(8,128)(2,1)S(1)} collective-permute-done((bf16[8,32,256]{2,1,0:T(8,128)(2,1)S(1)}, bf16[8,32,256]{2,1,0:T(8,128)(2,1)S(1)}, u32[]{:S(2)}, u32[]{:S(2)}) %collective-permute-start) | collective-permute-done | bytes 131104 | tf_op jit(solution)/shard_map/ppermute | solution.py:321
  23.5 2.8 %collective-permute-start.6 = (bf16[2,8,32,256]{3,2,1,0:T(8,128)(2,1)S(1)}, bf16[2,8,32,256]{3,2,1,0:T(8,128)(2,1)S(1)}, u32[]{:S(2)}, u32[]{:S(2)}) collective-permute-start(bf16[2,8,32,256]{3,2,1,0:T(8,128)(2,1)S(1)} %pad_maximum_fusion.4.refs_0_), channel_id=1, source_target_pairs={{0,12},{4,8},{8,4},{12,0},{1,13},{5,9},{9,5},{13,1},{2,14},{6,10},... | collective-permute-start | bytes 786440 | tf_op jit(solution)/shard_map/ppermute | solution.py:324
  26.3 0.3 collective-permute-start.4
  26.7 0.3 collective-permute-start.2
  27.0 4.1 %collective-permute-start.1 = (bf16[2,8,32,256]{3,2,1,0:T(8,128)(2,1)S(1)}, bf16[2,8,32,256]{3,2,1,0:T(8,128)(2,1)S(1)}, u32[]{:S(2)}, u32[]{:S(2)}) collective-permute-start(bf16[2,8,32,256]{3,2,1,0:T(8,128)(2,1)S(1)} %pad_maximum_fusion.4.refs_0_), channel_id=1, source_target_pairs={{0,2},{2,0},{1,3},{3,1},{4,6},{6,4},{5,7},{7,5},{8,10},{10,8},{9,1... | collective-permute-start | bytes 786440 | tf_op jit(solution)/shard_map/ppermute | solution.py:325
  31.1 5.7 %collective-permute-done.6.refs_6_ = bf16[2,8,32,256]{3,2,1,0:T(8,128)(2,1)S(1)} collective-permute-done((bf16[2,8,32,256]{3,2,1,0:T(8,128)(2,1)S(1)}, bf16[2,8,32,256]{3,2,1,0:T(8,128)(2,1)S(1)}, u32[]{:S(2)}, u32[]{:S(2)}) %collective-permute-start.6) | collective-permute-done | bytes 262176 | tf_op jit(solution)/shard_map/ppermute | solution.py:324
  36.8 1.7 collective-permute-start.7
  38.5 0.9 collective-permute-start.5
  39.4 0.6 collective-permute-start.3
  40.0 0.7 fusion.7
  40.6 0.8 copy.15.own_ids_ref
  41.4 0.6 pad_add_fusion.pos
  42.1 0.6 copy-done.6
  42.7 0.1 copy-done.7
  42.8 0.1 copy-done.8
  42.9 0.1 copy-done.9
  43.0 54.3 %local_terms.1 = (bf16[1536,256]{1,0:T(8,128)(2,1)}, f32[1536,256]{1,0:T(8,128)}, f32[1024,256]{1,0:T(8,128)}) custom-call(s32[4]{0:T(128)} %pad_add_fusion.pos, s32[1,4096]{1,0:T(1,128)} %ids_ref.1, s32[256,1]{1,0:T(8,128)} %copy.15.own_ids_ref, bf16[2,8,32,256]{3,2,1,0:T(8,128)(2,1)} %copy-done.2, bf16[2,8,32,256]{3,2,1,0:T(8,128)(2,1)} %copy-done.6, ...), custom_call_target="tpu_custom_call" | custom-call | flops 24000000000 | bytes 12582912 | tf_op jit(solution)/shard_map/local_terms/pallas_call | solution.py:272
  97.3 0.0 collective-permute-start.8
  97.3 2.5 %collective-permute-done.8 = bf16[1536,256]{1,0:T(8,128)(2,1)S(1)} collective-permute-done((bf16[1536,256]{1,0:T(8,128)(2,1)}, bf16[1536,256]{1,0:T(8,128)(2,1)S(1)}, u32[]{:S(2)}, u32[]{:S(2)}) %collective-permute-start.8) | collective-permute-done | bytes 786464 | tf_op jit(solution)/shard_map/ppermute | solution.py:340
  99.8 1.6 fusion.8
  101.4 0.7 constant_dynamic-slice_fusion.5
  102.1 1.1 collective-permute-start.9
  103.3 1.8 %collective-permute-start.11 = (bf16[384,256]{1,0:T(8,128)(2,1)S(1)}, bf16[384,256]{1,0:T(8,128)(2,1)S(1)}, u32[]{:S(2)}, u32[]{:S(2)}) collective-permute-start(bf16[384,256]{1,0:T(8,128)(2,1)S(1)} %get-tuple-element.25), channel_id=1, source_target_pairs={{0,12},{4,8},{8,4},{12,0},{1,13},{5,9},{9,5},{13,1},{2,14},{6,10},... | collective-permute-start | bytes 589832 | tf_op jit(solution)/shard_map/ppermute | solution.py:54
  105.1 0.7 collective-permute-start.10
  105.9 2.9 %collective-permute-done.9 = bf16[384,256]{1,0:T(8,128)(2,1)S(1)} collective-permute-done((bf16[384,256]{1,0:T(8,128)(2,1)}, bf16[384,256]{1,0:T(8,128)(2,1)S(1)}, u32[]{:S(2)}, u32[]{:S(2)}) %collective-permute-start.9) | collective-permute-done | bytes 196640 | tf_op jit(solution)/shard_map/ppermute | solution.py:54
  108.7 4.3 %collective-permute-done.11 = bf16[384,256]{1,0:T(8,128)(2,1)S(1)} collective-permute-done((bf16[384,256]{1,0:T(8,128)(2,1)S(1)}, bf16[384,256]{1,0:T(8,128)(2,1)S(1)}, u32[]{:S(2)}, u32[]{:S(2)}) %collective-permute-start.11) | collective-permute-done | bytes 196640 | tf_op jit(solution)/shard_map/ppermute | solution.py:54
  113.0 2.2 %collective-permute-done.10 = bf16[384,256]{1,0:T(8,128)(2,1)} collective-permute-done((bf16[384,256]{1,0:T(8,128)(2,1)S(1)}, bf16[384,256]{1,0:T(8,128)(2,1)}, u32[]{:S(2)}, u32[]{:S(2)}) %collective-permute-start.10) | collective-permute-done | bytes 196640 | tf_op jit(solution)/shard_map/ppermute | solution.py:54
  115.3 1.0 convert_add_fusion.1
  116.3 0.1 fusion
  116.4 1.3 collective-permute-start.12
  117.7 1.8 collective-permute-start.14
  119.5 0.6 collective-permute-start.13
  120.2 1.4 collective-permute-done.12
  121.6 2.1 %collective-permute-done.14 = bf16[352,256]{1,0:T(8,128)(2,1)S(1)} collective-permute-done((bf16[352,256]{1,0:T(8,128)(2,1)S(1)}, bf16[352,256]{1,0:T(8,128)(2,1)S(1)}, u32[]{:S(2)}, u32[]{:S(2)}) %collective-permute-start.14) | collective-permute-done | bytes 180256 | tf_op jit(solution)/shard_map/ppermute | solution.py:54
  123.8 3.9 %collective-permute-done.13 = bf16[352,256]{1,0:T(8,128)(2,1)S(1)} collective-permute-done((bf16[352,256]{1,0:T(8,128)(2,1)S(1)}, bf16[352,256]{1,0:T(8,128)(2,1)S(1)}, u32[]{:S(2)}, u32[]{:S(2)}) %collective-permute-start.13) | collective-permute-done | bytes 180256 | tf_op jit(solution)/shard_map/ppermute | solution.py:54
  127.7 0.2 fusion.6
  127.9 11.1 %all_to_all.16 = bf16[8,44,256]{2,1,0:T(8,128)(2,1)S(1)} all-to-all(bf16[8,44,256]{2,1,0:T(8,128)(2,1)S(1)} %reshape.49), channel_id=1, replica_groups=mesh['xh'=2,'z'=8,'y'=4,'c'=2,'dp'=2] {'z'}, dimensions={0} | all-to-all | bytes 360448 | tf_op jit(solution)/shard_map/all_to_all | solution.py:346
  139.0 11.1 %all_to_all.17 = bf16[8,44,256]{2,1,0:T(8,128)(2,1)S(1)} all-to-all(bf16[8,44,256]{2,1,0:T(8,128)(2,1)S(1)} %broadcast_in_dim.20), channel_id=1, replica_groups=mesh['xh'=2,'z'=8,'y'=4,'c'=2,'dp'=2] {'z'}, dimensions={0} | all-to-all | bytes 360448 | tf_op jit(solution)/shard_map/all_to_all | solution.py:66
  150.2 0.2 collective-permute-start.17
  150.4 3.1 %collective-permute-start.16 = (bf16[352,256]{1,0:T(8,128)(2,1)S(1)}, bf16[352,256]{1,0:T(8,128)(2,1)S(1)}, u32[]{:S(2)}, u32[]{:S(2)}) collective-permute-start(bf16[352,256]{1,0:T(8,128)(2,1)S(1)} %reshape.50), channel_id=1, source_target_pairs={{0,128},{1,129},{128,0},{129,1},{2,130},{3,131},{130,2},{131,3},{4... | collective-permute-start | bytes 540680 | tf_op jit(solution)/shard_map/ppermute | solution.py:46
  153.5 0.6 collective-permute-start.15
  154.2 0.5 collective-permute-done.17
  154.6 3.8 %collective-permute-done.16 = bf16[352,256]{1,0:T(8,128)(2,1)S(1)} collective-permute-done((bf16[352,256]{1,0:T(8,128)(2,1)S(1)}, bf16[352,256]{1,0:T(8,128)(2,1)S(1)}, u32[]{:S(2)}, u32[]{:S(2)}) %collective-permute-start.16) | collective-permute-done | bytes 180256 | tf_op jit(solution)/shard_map/ppermute | solution.py:46
  158.4 1.8 %collective-permute-done.15 = bf16[352,256]{1,0:T(8,128)(2,1)S(1)} collective-permute-done((bf16[352,256]{1,0:T(8,128)(2,1)S(1)}, bf16[352,256]{1,0:T(8,128)(2,1)S(1)}, u32[]{:S(2)}, u32[]{:S(2)}) %collective-permute-start.15) | collective-permute-done | bytes 180256 | tf_op jit(solution)/shard_map/ppermute | solution.py:46
  160.3 0.1 broadcast_select_fusion.15
  160.4 0.1 collective-permute-start.20
  160.5 2.3 %collective-permute-start.19 = (bf16[384,256]{1,0:T(8,128)(2,1)S(1)}, bf16[384,256]{1,0:T(8,128)(2,1)S(1)}, u32[]{:S(2)}, u32[]{:S(2)}) collective-permute-start(bf16[384,256]{1,0:T(8,128)(2,1)S(1)} %pad_maximum_fusion.5), channel_id=1, source_target_pairs={{0,8},{4,12},{8,0},{12,4},{1,9},{5,13},{9,1},{13,5},{2,10},{6,14},... | collective-permute-start | bytes 589832 | tf_op jit(solution)/shard_map/ppermute | solution.py:46
  162.8 1.5 collective-permute-start.18
  164.3 0.7 collective-permute-done.20
  165.0 3.0 %collective-permute-done.19 = bf16[384,256]{1,0:T(8,128)(2,1)S(1)} collective-permute-done((bf16[384,256]{1,0:T(8,128)(2,1)S(1)}, bf16[384,256]{1,0:T(8,128)(2,1)S(1)}, u32[]{:S(2)}, u32[]{:S(2)}) %collective-permute-start.19) | collective-permute-done | bytes 196640 | tf_op jit(solution)/shard_map/ppermute | solution.py:46
  168.0 2.0 %collective-permute-done.18 = bf16[384,256]{1,0:T(8,128)(2,1)S(1)} collective-permute-done((bf16[384,256]{1,0:T(8,128)(2,1)S(1)}, bf16[384,256]{1,0:T(8,128)(2,1)S(1)}, u32[]{:S(2)}, u32[]{:S(2)}) %collective-permute-start.18) | collective-permute-done | bytes 196640 | tf_op jit(solution)/shard_map/ppermute | solution.py:46
  170.0 0.1 broadcast_select_fusion.9
  170.1 0.1 pad_maximum_fusion.1
  170.2 6.6 %collective-permute-start.21 = (bf16[1536,256]{1,0:T(8,128)(2,1)S(1)}, bf16[1536,256]{1,0:T(8,128)(2,1)S(1)}, u32[]{:S(2)}, u32[]{:S(2)}) collective-permute-start(bf16[1536,256]{1,0:T(8,128)(2,1)S(1)} %pad_maximum_fusion.1), channel_id=1, source_target_pairs={{0,2},{2,0},{1,3},{3,1},{4,6},{6,4},{5,7},{7,5},{8,10},{10,8},{9,1... | collective-permute-start | bytes 2359304 | tf_op jit(solution)/shard_map/ppermute | solution.py:46
  176.8 0.1 fusion.1
  176.8 1.0 fusion.9
  177.8 0.9 collective-permute-done.21
  178.7 0.3 broadcast_select_fusion.1
  178.9 0.9 maximum_convert_fusion.1
  179.9 0.2 maximum_convert_fusion
  180.1 1.6 slice.38
  (31 shorter events, 0.3 us)
Async XLA Ops:
  0.6 0.9 copy-start
  18.1 5.3 %collective-permute-start = (bf16[8,32,256]{2,1,0:T(8,128)(2,1)S(1)}, bf16[8,32,256]{2,1,0:T(8,128)(2,1)S(1)}, u32[]{:S(2)}, u32[]{:S(2)}) collective-permute-start(bf16[8,32,256]{2,1,0:T(8,128)(2,1)S(1)} %all_to_all.15), channel_id=1, source_target_pairs={{0,128},{128,0},{1,129},{129,1},{2,130},{130,2},{3,131},{131,3},{4... | collective-permute-start | bytes 393224 | tf_op jit(solution)/shard_map/ppermute | solution.py:321
  23.5 18.6 %copy-start.2 = (bf16[2,8,32,256]{3,2,1,0:T(8,128)(2,1)}, bf16[2,8,32,256]{3,2,1,0:T(8,128)(2,1)S(1)}, u32[]{:S(2)}) copy-start(bf16[2,8,32,256]{3,2,1,0:T(8,128)(2,1)S(1)} %pad_maximum_fusion.4.refs_0_) | copy-start | bytes 786436
  23.5 13.3 %collective-permute-start.6 = (bf16[2,8,32,256]{3,2,1,0:T(8,128)(2,1)S(1)}, bf16[2,8,32,256]{3,2,1,0:T(8,128)(2,1)S(1)}, u32[]{:S(2)}, u32[]{:S(2)}) collective-permute-start(bf16[2,8,32,256]{3,2,1,0:T(8,128)(2,1)S(1)} %pad_maximum_fusion.4.refs_0_), channel_id=1, source_target_pairs={{0,12},{4,8},{8,4},{12,0},{1,13},{5,9},{9,5},{13,1},{2,14},{6,10},... | collective-permute-start | bytes 786440 | tf_op jit(solution)/shard_map/ppermute | solution.py:324
  26.3 12.1 %collective-permute-start.4 = (bf16[2,8,32,256]{3,2,1,0:T(8,128)(2,1)S(1)}, bf16[2,8,32,256]{3,2,1,0:T(8,128)(2,1)S(1)}, u32[]{:S(2)}, u32[]{:S(2)}) collective-permute-start(bf16[2,8,32,256]{3,2,1,0:T(8,128)(2,1)S(1)} %pad_maximum_fusion.4.refs_0_), channel_id=1, source_target_pairs={{0,8},{4,12},{8,0},{12,4},{1,9},{5,13},{9,1},{13,5},{2,10},{6,14},... | collective-permute-start | bytes 786440 | tf_op jit(solution)/shard_map/ppermute | solution.py:324
  26.7 12.7 %collective-permute-start.2 = (bf16[2,8,32,256]{3,2,1,0:T(8,128)(2,1)S(1)}, bf16[2,8,32,256]{3,2,1,0:T(8,128)(2,1)S(1)}, u32[]{:S(2)}, u32[]{:S(2)}) collective-permute-start(bf16[2,8,32,256]{3,2,1,0:T(8,128)(2,1)S(1)} %pad_maximum_fusion.4.refs_0_), channel_id=1, source_target_pairs={{0,4},{4,0},{8,12},{12,8},{1,5},{5,1},{9,13},{13,9},{2,6},{6,2},{1... | collective-permute-start | bytes 786440 | tf_op jit(solution)/shard_map/ppermute | solution.py:324
  27.0 15.0 %collective-permute-start.1 = (bf16[2,8,32,256]{3,2,1,0:T(8,128)(2,1)S(1)}, bf16[2,8,32,256]{3,2,1,0:T(8,128)(2,1)S(1)}, u32[]{:S(2)}, u32[]{:S(2)}) collective-permute-start(bf16[2,8,32,256]{3,2,1,0:T(8,128)(2,1)S(1)} %pad_maximum_fusion.4.refs_0_), channel_id=1, source_target_pairs={{0,2},{2,0},{1,3},{3,1},{4,6},{6,4},{5,7},{7,5},{8,10},{10,8},{9,1... | collective-permute-start | bytes 786440 | tf_op jit(solution)/shard_map/ppermute | solution.py:325
  36.8 5.3 %copy-start.3 = (bf16[2,8,32,256]{3,2,1,0:T(8,128)(2,1)}, bf16[2,8,32,256]{3,2,1,0:T(8,128)(2,1)S(1)}, u32[]{:S(2)}) copy-start(bf16[2,8,32,256]{3,2,1,0:T(8,128)(2,1)S(1)} %collective-permute-done.6.refs_6_) | copy-start | bytes 786436
  36.8 5.3 %collective-permute-start.7 = (bf16[2,8,32,256]{3,2,1,0:T(8,128)(2,1)S(1)}, bf16[2,8,32,256]{3,2,1,0:T(8,128)(2,1)S(1)}, u32[]{:S(2)}, u32[]{:S(2)}) collective-permute-start(bf16[2,8,32,256]{3,2,1,0:T(8,128)(2,1)S(1)} %collective-permute-done.6.refs_6_), channel_id=1, source_target_pairs={{0,2},{2,0},{1,3},{3,1},{4,6},{6,4},{5,7},{7,5},{8,10},{10,8},{9,1... | collective-permute-start | bytes 786440 | tf_op jit(solution)/shard_map/ppermute | solution.py:325
  38.5 3.6 %copy-start.4 = (bf16[2,8,32,256]{3,2,1,0:T(8,128)(2,1)}, bf16[2,8,32,256]{3,2,1,0:T(8,128)(2,1)S(1)}, u32[]{:S(2)}) copy-start(bf16[2,8,32,256]{3,2,1,0:T(8,128)(2,1)S(1)} %collective-permute-done.4.refs_4_) | copy-start | bytes 786436
  38.5 3.6 %collective-permute-start.5 = (bf16[2,8,32,256]{3,2,1,0:T(8,128)(2,1)S(1)}, bf16[2,8,32,256]{3,2,1,0:T(8,128)(2,1)S(1)}, u32[]{:S(2)}, u32[]{:S(2)}) collective-permute-start(bf16[2,8,32,256]{3,2,1,0:T(8,128)(2,1)S(1)} %collective-permute-done.4.refs_4_), channel_id=1, source_target_pairs={{0,2},{2,0},{1,3},{3,1},{4,6},{6,4},{5,7},{7,5},{8,10},{10,8},{9,1... | collective-permute-start | bytes 786440 | tf_op jit(solution)/shard_map/ppermute | solution.py:325
  39.4 2.7 %copy-start.5 = (bf16[2,8,32,256]{3,2,1,0:T(8,128)(2,1)}, bf16[2,8,32,256]{3,2,1,0:T(8,128)(2,1)S(1)}, u32[]{:S(2)}) copy-start(bf16[2,8,32,256]{3,2,1,0:T(8,128)(2,1)S(1)} %collective-permute-done.2.refs_2_) | copy-start | bytes 786436
  39.4 2.7 %collective-permute-start.3 = (bf16[2,8,32,256]{3,2,1,0:T(8,128)(2,1)S(1)}, bf16[2,8,32,256]{3,2,1,0:T(8,128)(2,1)S(1)}, u32[]{:S(2)}, u32[]{:S(2)}) collective-permute-start(bf16[2,8,32,256]{3,2,1,0:T(8,128)(2,1)S(1)} %collective-permute-done.2.refs_2_), channel_id=1, source_target_pairs={{0,2},{2,0},{1,3},{3,1},{4,6},{6,4},{5,7},{7,5},{8,10},{10,8},{9,1... | collective-permute-start | bytes 786440 | tf_op jit(solution)/shard_map/ppermute | solution.py:325
  42.0 0.7 copy-start.6
  42.0 0.8 copy-start.7
  42.1 0.9 copy-start.8
  42.1 0.9 copy-start.9
  97.3 2.5 %collective-permute-start.8 = (bf16[1536,256]{1,0:T(8,128)(2,1)}, bf16[1536,256]{1,0:T(8,128)(2,1)S(1)}, u32[]{:S(2)}, u32[]{:S(2)}) collective-permute-start(bf16[1536,256]{1,0:T(8,128)(2,1)} %get-tuple-element.10), channel_id=1, source_target_pairs={{0,2},{2,0},{1,3},{3,1},{4,6},{6,4},{5,7},{7,5},{8,10},{10,8},{9,1... | collective-permute-start | bytes 2359304 | tf_op jit(solution)/shard_map/ppermute | solution.py:340
  101.4 14.9 %copy-start.1 = (f32[1024,256]{1,0:T(8,128)S(1)}, f32[1024,256]{1,0:T(8,128)}, u32[]{:S(2)}) copy-start(f32[1024,256]{1,0:T(8,128)} %get-tuple-element.11) | copy-start | bytes 3145732
  102.1 6.6 %collective-permute-start.9 = (bf16[384,256]{1,0:T(8,128)(2,1)}, bf16[384,256]{1,0:T(8,128)(2,1)S(1)}, u32[]{:S(2)}, u32[]{:S(2)}) collective-permute-start(bf16[384,256]{1,0:T(8,128)(2,1)} %get-tuple-element.24), channel_id=1, source_target_pairs={{0,4},{4,0},{8,12},{12,8},{1,5},{5,1},{9,13},{13,9},{2,6},{6,2},{1... | collective-permute-start | bytes 589832 | tf_op jit(solution)/shard_map/ppermute | solution.py:54
  103.3 9.8 %collective-permute-start.11 = (bf16[384,256]{1,0:T(8,128)(2,1)S(1)}, bf16[384,256]{1,0:T(8,128)(2,1)S(1)}, u32[]{:S(2)}, u32[]{:S(2)}) collective-permute-start(bf16[384,256]{1,0:T(8,128)(2,1)S(1)} %get-tuple-element.25), channel_id=1, source_target_pairs={{0,12},{4,8},{8,4},{12,0},{1,13},{5,9},{9,5},{13,1},{2,14},{6,10},... | collective-permute-start | bytes 589832 | tf_op jit(solution)/shard_map/ppermute | solution.py:54
  105.1 10.2 %collective-permute-start.10 = (bf16[384,256]{1,0:T(8,128)(2,1)S(1)}, bf16[384,256]{1,0:T(8,128)(2,1)}, u32[]{:S(2)}, u32[]{:S(2)}) collective-permute-start(bf16[384,256]{1,0:T(8,128)(2,1)S(1)} %get-tuple-element.26), channel_id=1, source_target_pairs={{0,8},{4,12},{8,0},{12,4},{1,9},{5,13},{9,1},{13,5},{2,10},{6,14},... | collective-permute-start | bytes 589832 | tf_op jit(solution)/shard_map/ppermute | solution.py:54
  116.4 5.2 %collective-permute-start.12 = (bf16[352,256]{1,0:T(8,128)(2,1)S(1)}, bf16[352,256]{1,0:T(8,128)(2,1)S(1)}, u32[]{:S(2)}, u32[]{:S(2)}) collective-permute-start(bf16[352,256]{1,0:T(8,128)(2,1)S(1)} %get-tuple-element.31), channel_id=1, source_target_pairs={{0,1},{1,0},{128,129},{129,128},{2,3},{3,2},{130,131},{131,130},{4... | collective-permute-start | bytes 540680 | tf_op jit(solution)/shard_map/ppermute | solution.py:54
  117.7 6.0 %collective-permute-start.14 = (bf16[352,256]{1,0:T(8,128)(2,1)S(1)}, bf16[352,256]{1,0:T(8,128)(2,1)S(1)}, u32[]{:S(2)}, u32[]{:S(2)}) collective-permute-start(bf16[352,256]{1,0:T(8,128)(2,1)S(1)} %get-tuple-element.32), channel_id=1, source_target_pairs={{0,129},{1,128},{128,1},{129,0},{2,131},{3,130},{130,3},{131,2},{4... | collective-permute-start | bytes 540680 | tf_op jit(solution)/shard_map/ppermute | solution.py:54
  119.5 8.1 %collective-permute-start.13 = (bf16[352,256]{1,0:T(8,128)(2,1)S(1)}, bf16[352,256]{1,0:T(8,128)(2,1)S(1)}, u32[]{:S(2)}, u32[]{:S(2)}) collective-permute-start(bf16[352,256]{1,0:T(8,128)(2,1)S(1)} %get-tuple-element.33), channel_id=1, source_target_pairs={{0,128},{1,129},{128,0},{129,1},{2,130},{3,131},{130,2},{131,3},{4... | collective-permute-start | bytes 540680 | tf_op jit(solution)/shard_map/ppermute | solution.py:54
  150.2 4.4 %collective-permute-start.17 = (bf16[352,256]{1,0:T(8,128)(2,1)S(1)}, bf16[352,256]{1,0:T(8,128)(2,1)S(1)}, u32[]{:S(2)}, u32[]{:S(2)}) collective-permute-start(bf16[352,256]{1,0:T(8,128)(2,1)S(1)} %reshape.50), channel_id=1, source_target_pairs={{0,1},{1,0},{128,129},{129,128},{2,3},{3,2},{130,131},{131,130},{4... | collective-permute-start | bytes 540680 | tf_op jit(solution)/shard_map/ppermute | solution.py:46
  150.4 8.1 %collective-permute-start.16 = (bf16[352,256]{1,0:T(8,128)(2,1)S(1)}, bf16[352,256]{1,0:T(8,128)(2,1)S(1)}, u32[]{:S(2)}, u32[]{:S(2)}) collective-permute-start(bf16[352,256]{1,0:T(8,128)(2,1)S(1)} %reshape.50), channel_id=1, source_target_pairs={{0,128},{1,129},{128,0},{129,1},{2,130},{3,131},{130,2},{131,3},{4... | collective-permute-start | bytes 540680 | tf_op jit(solution)/shard_map/ppermute | solution.py:46
  153.5 6.7 %collective-permute-start.15 = (bf16[352,256]{1,0:T(8,128)(2,1)S(1)}, bf16[352,256]{1,0:T(8,128)(2,1)S(1)}, u32[]{:S(2)}, u32[]{:S(2)}) collective-permute-start(bf16[352,256]{1,0:T(8,128)(2,1)S(1)} %reshape.50), channel_id=1, source_target_pairs={{0,129},{1,128},{128,1},{129,0},{2,131},{3,130},{130,3},{131,2},{4... | collective-permute-start | bytes 540680 | tf_op jit(solution)/shard_map/ppermute | solution.py:46
  160.4 4.7 %collective-permute-start.20 = (bf16[384,256]{1,0:T(8,128)(2,1)S(1)}, bf16[384,256]{1,0:T(8,128)(2,1)S(1)}, u32[]{:S(2)}, u32[]{:S(2)}) collective-permute-start(bf16[384,256]{1,0:T(8,128)(2,1)S(1)} %pad_maximum_fusion.5), channel_id=1, source_target_pairs={{0,4},{4,0},{8,12},{12,8},{1,5},{5,1},{9,13},{13,9},{2,6},{6,2},{1... | collective-permute-start | bytes 589832 | tf_op jit(solution)/shard_map/ppermute | solution.py:46
  160.5 7.6 %collective-permute-start.19 = (bf16[384,256]{1,0:T(8,128)(2,1)S(1)}, bf16[384,256]{1,0:T(8,128)(2,1)S(1)}, u32[]{:S(2)}, u32[]{:S(2)}) collective-permute-start(bf16[384,256]{1,0:T(8,128)(2,1)S(1)} %pad_maximum_fusion.5), channel_id=1, source_target_pairs={{0,8},{4,12},{8,0},{12,4},{1,9},{5,13},{9,1},{13,5},{2,10},{6,14},... | collective-permute-start | bytes 589832 | tf_op jit(solution)/shard_map/ppermute | solution.py:46
  162.8 7.3 %collective-permute-start.18 = (bf16[384,256]{1,0:T(8,128)(2,1)S(1)}, bf16[384,256]{1,0:T(8,128)(2,1)S(1)}, u32[]{:S(2)}, u32[]{:S(2)}) collective-permute-start(bf16[384,256]{1,0:T(8,128)(2,1)S(1)} %pad_maximum_fusion.5), channel_id=1, source_target_pairs={{0,12},{4,8},{8,4},{12,0},{1,13},{5,9},{9,5},{13,1},{2,14},{6,10},... | collective-permute-start | bytes 589832 | tf_op jit(solution)/shard_map/ppermute | solution.py:46
  170.2 8.5 %collective-permute-start.21 = (bf16[1536,256]{1,0:T(8,128)(2,1)S(1)}, bf16[1536,256]{1,0:T(8,128)(2,1)S(1)}, u32[]{:S(2)}, u32[]{:S(2)}) collective-permute-start(bf16[1536,256]{1,0:T(8,128)(2,1)S(1)} %pad_maximum_fusion.1), channel_id=1, source_target_pairs={{0,2},{2,0},{1,3},{3,1},{4,6},{6,4},{5,7},{7,5},{8,10},{10,8},{9,1... | collective-permute-start | bytes 2359304 | tf_op jit(solution)/shard_map/ppermute | solution.py:46

commit v3 on v2

--- a/solution.py
+++ b/solution.py
@@ -47,21 +47,6 @@
     return unxor(parts, index)
 
 
-def scatter_xor(total, axis, count, index):
-    rows = total.shape[0] // count
-    low = total.astype(BF)
-    got = [
-        lax.ppermute(
-            lax.dynamic_slice_in_dim(low, (index ^ s) * rows, rows), axis, xor_perm(count, s)
-        )
-        for s in range(1, count)
-    ]
-    own = lax.dynamic_slice_in_dim(total, index * rows, rows)
-    for part in got:
-        own = own + part.astype(F32)
-    return own
-
-
 def spread(block, axis, count):
     return lax.all_to_all(
         jnp.broadcast_to(block[None], (count,) + block.shape), axis, 0, 0
@@ -89,14 +74,15 @@
     dims,
     pos,
     ids_ref,
-    own_ids_ref,
     *refs,
 ):
-    n_xh, n_z, n_y, n_c, chunk = dims
-    n_parts = n_y * n_c
+    n_xh, n_z, n_y, n_c, n_dp = dims
+    n_x = n_xh * n_dp
+    n_parts = n_xh * n_y * n_c
     parts = refs[:n_parts]
     w_sp, w_t, w_q, w_k, w_v, w_o, up_ref = refs[n_parts : n_parts + 7]
-    send_ref, keep_ref, head_ref = refs[n_parts + 7 : n_parts + 10]
+    outs = refs[n_parts + 7 : n_parts + 7 + 2 * n_y + n_x]
+    send_refs, keep_refs, head_refs = outs[:n_y], outs[n_y : 2 * n_y], outs[2 * n_y :]
     (
         cols,
         slope,
@@ -109,29 +95,30 @@
         gf,
         e_ref,
         acc,
+        heads,
         q_ref,
         g_ref,
         att_ref,
         gq_ref,
-    ) = refs[n_parts + 10 :]
-    my_xh, my_y, my_c = pos[0], pos[1], pos[2]
-    first = pl.multiple_of(pos[3], 256)
+    ) = refs[n_parts + 7 + 2 * n_y + n_x :]
+    my_xh, my_y, my_c, my_x = pos[0], pos[1], pos[2], pos[4]
+    first = pl.multiple_of(pos[3], up_ref.shape[0])
     tokens, ch = feat.shape
     local = up_ref.shape[0]
-    half = parts[0].shape[2]
-    n_chunk = tokens // chunk
-    frames = chunk // FRAME
+    half = parts[0].shape[1]
     scale = HD ** (-0.5)
     n_head = n_y * n_c
+    own_ids = jnp.broadcast_to(ids_ref[:, pl.ds(first, local)].astype(F32), (SIDE, local))
+    own_ids = jnp.transpose(own_ids)[:, 0:1].astype(jnp.int32)
 
     @pl.loop(0, n_z)
     def _(z):
-        for s in range(n_y):
-            for t in range(n_c):
-                for u in range(n_xh):
+        for u in range(n_xh):
+            for s in range(n_y):
+                for t in range(n_c):
                     frame = ((my_xh ^ u) * n_z + z) * n_y + (my_y ^ s)
                     row = pl.multiple_of(frame * FRAME + (my_c ^ t) * half, half)
-                    low = parts[s * n_c + t][u, z]
+                    low = parts[(u * n_y + s) * n_c + t][z]
                     wide = low.astype(F32)
                     cols[pl.ds(row, half), 0:ch] = roll_cols(wide, -1).astype(BF)
                     cols[pl.ds(row, half), ch : 2 * ch] = low
@@ -143,8 +130,11 @@
     gf[0:FRAME, :] = edge
     gf[tokens + FRAME : tokens + 2 * FRAME, :] = edge
     acc[...] = jnp.zeros_like(acc)
-    head_ref[...] = jnp.zeros_like(head_ref)
-
+    heads[...] = jnp.zeros_like(heads)
+
+    chunk = min(tokens, 1024)
+    n_chunk = tokens // chunk
+    frames = chunk // FRAME
     @pl.loop(0, n_chunk)
     def _(i):
         row = pl.multiple_of(i * chunk, chunk)
@@ -159,6 +149,8 @@
         slope[pl.ds(row, chunk), :] = sigma * (1.0 + pre * (1.0 - sigma))
         hid[pl.ds(pl.multiple_of(row + FRAME, FRAME), chunk), :] = (pre * sigma).astype(BF)
 
+    chunk = min(tokens, 1024)
+    n_chunk = tokens // chunk
     @pl.loop(0, n_chunk)
     def _(i):
         row = pl.multiple_of(i * chunk, chunk)
@@ -174,6 +166,8 @@
     q_ref[...] = dot(feat[pl.ds(first, local), :], w_q[...]).astype(BF)
     g_ref[...] = dot_t(up_ref[...], w_o[...]).astype(BF)
 
+    chunk = min(tokens, 2048)
+    n_chunk = tokens // chunk
     def fold(block, join):
         out = block[:, 0:HD]
         for k in range(1, block.shape[1] // HD):
@@ -186,7 +180,7 @@
         def raw(i, top):
             row = pl.multiple_of(i * chunk, chunk)
             s = dot_t(q_ref[:, sel], keys[pl.ds(row, chunk), sel])
-            s = jnp.where(ids_ref[:, pl.ds(row, chunk)] <= own_ids_ref[...], s, NEG_FILL)
+            s = jnp.where(ids_ref[:, pl.ds(row, chunk)] <= own_ids, s, NEG_FILL)
             e_ref[:, pl.ds(row, chunk)] = s
             return jnp.maximum(top, fold(s, jnp.maximum))
 
@@ -221,6 +215,8 @@
         gq = lax.fori_loop(0, n_chunk, backward, zero)
         gq_ref[:, sel] = (gq * scale).astype(BF)
 
+    chunk = min(tokens, 1024)
+    n_chunk = tokens // chunk
     @pl.loop(0, n_chunk)
     def _(i):
         row = pl.multiple_of(i * chunk, chunk)
@@ -228,17 +224,20 @@
         f = feat[pl.ds(row, chunk), :]
         at = pl.multiple_of(row + FRAME, FRAME)
         gf[pl.ds(at, chunk), :] = (dot_t(gk, w_k[...]) + dot_t(gv, w_v[...])).astype(BF)
-        head_ref[ch : 2 * ch, :] += contract_rows(f, gk)
-        head_ref[2 * ch : 3 * ch, :] += contract_rows(f, gv)
+        heads[ch : 2 * ch, :] += contract_rows(f, gk)
+        heads[2 * ch : 3 * ch, :] += contract_rows(f, gv)
 
     own = pl.ds(first, local)
     up = up_ref[...]
     total = dot_t(gkey[own, :], w_k[...]) + dot_t(gval[own, :], w_v[...])
     total = total + dot_t(gq_ref[...], w_q[...]) + up.astype(F32) * (1.0 / n_head)
     gf[pl.ds(pl.multiple_of(first + FRAME, FRAME), local), :] = total.astype(BF)
-    head_ref[0:ch, :] = contract_rows(feat[own, :], gq_ref[...])
-    head_ref[3 * ch : 4 * ch, :] = contract_rows(att_ref[...], up)
-
+    heads[0:ch, :] = contract_rows(feat[own, :], gq_ref[...])
+    heads[3 * ch : 4 * ch, :] = contract_rows(att_ref[...], up)
+
+    chunk = min(tokens, 1024)
+    n_chunk = tokens // chunk
+    frames = chunk // FRAME
     @pl.loop(0, n_chunk)
     def _(i):
         row = pl.multiple_of(i * chunk, chunk)
@@ -256,29 +255,35 @@
             moved = moved.reshape(chunk, ch).astype(BF)
             acc[a * 3 * ch : (a + 1) * 3 * ch, :] += contract_rows(x, moved)
 
-    half_rows = keep_ref.shape[0]
-    send_ref[...] = acc[pl.ds(pl.multiple_of((1 - my_c) * half_rows, half_rows), half_rows), :].astype(BF)
-    keep_ref[...] = acc[pl.ds(pl.multiple_of(my_c * half_rows, half_rows), half_rows), :]
-
-
-def local_terms(sizes, pos, ids, own_ids, parts, weights, up, chunk=512):
-    n_xh, n_z, n_y, n_c, _ = sizes
+    rows = keep_refs[0].shape[0]
+    sub = rows // n_x
+    for s in range(n_y):
+        for r in range(n_x):
+            at = (my_y ^ s) * rows + (my_x ^ r) * sub
+            here = slice(r * sub, (r + 1) * sub)
+            for ref, which in ((send_refs[s], 1 - my_c), (keep_refs[s], my_c)):
+                row = pl.multiple_of(which * (n_y * rows) + at, SIDE)
+                ref[here, :] = acc[pl.ds(row, sub), :].astype(BF)
+    for r in range(n_x):
+        head_refs[r][...] = heads[pl.ds(pl.multiple_of((my_x ^ r) * ch, ch), ch), :].astype(BF)
+
+
+def local_terms(sizes, pos, ids, parts, weights, up):
+    n_xh, n_z, n_y, n_c, n_dp = sizes
+    n_x = n_xh * n_dp
     local, ch = up.shape
     tokens = local * n_xh * n_z
     wide = weights[2].shape[1]
-    dims = (n_xh, n_z, n_y, n_c, chunk)
+    block = 12 * ch // (n_c * n_y)
     vm = pl.BlockSpec(memory_space=pltpu.VMEM)
-    n_in = 2 + len(parts) + len(weights) + 1
-    return pl.pallas_call(
-        functools.partial(local_kernel, dims),
+    n_in = 1 + len(parts) + len(weights) + 1
+    shapes = [(block, ch)] * (2 * n_y) + [(4 * ch // n_x, ch)] * n_x
+    out = pl.pallas_call(
+        functools.partial(local_kernel, sizes),
         name="local_terms",
-        out_shape=(
-            jax.ShapeDtypeStruct((6 * ch, ch), BF),
-            jax.ShapeDtypeStruct((6 * ch, ch), F32),
-            jax.ShapeDtypeStruct((4 * ch, ch), F32),
-        ),
+        out_shape=[jax.ShapeDtypeStruct(s, BF) for s in shapes],
         in_specs=[pl.BlockSpec(memory_space=pltpu.SMEM)] + [vm] * n_in,
-        out_specs=(vm, vm, vm),
+        out_specs=[vm] * len(shapes),
         scratch_shapes=[
             pltpu.VMEM((tokens, 3 * ch), BF),
             pltpu.VMEM((tokens, ch), F32),
@@ -291,6 +296,7 @@
             pltpu.VMEM((tokens + 2 * FRAME, ch), BF),
             pltpu.VMEM((local, tokens), F32),
             pltpu.VMEM((12 * ch, ch), F32),
+            pltpu.VMEM((4 * ch, ch), F32),
             pltpu.VMEM((local, wide), BF),
             pltpu.VMEM((local, wide), BF),
             pltpu.VMEM((local, wide), BF),
@@ -300,7 +306,8 @@
         cost_estimate=pl.CostEstimate(
             flops=24 * 10**9, transcendentals=2 * local * tokens, bytes_accessed=12 * 2**20
         ),
-    )(pos, ids, own_ids, *parts, *weights, up)
+    )(pos, ids, *parts, *weights, up)
+    return out[:n_y], out[n_y : 2 * n_y], out[2 * n_y :]
 
 
 def on_device(sizes, clip, block_ids, w_spatial, w_temporal, w_query, w_key, w_value, w_out, cotangent):
@@ -318,15 +325,15 @@
     piece = local // n_head
     mine = lax.dynamic_slice_in_dim(own_clip, lax.axis_index(("y", "c")) * piece, piece)
     part = spread(mine, "z", n_z)
-    part = jnp.stack([part, lax.ppermute(part, "xh", xor_perm(n_xh, 1))])
     parts = []
-    for s in range(n_y):
-        block = part if s == 0 else lax.ppermute(part, "y", xor_perm(n_y, s))
-        parts += [block, lax.ppermute(block, "c", xor_perm(n_c, 1))]
+    for u in range(n_xh):
+        held = part if u == 0 else lax.ppermute(part, "xh", xor_perm(n_xh, u))
+        for s in range(n_y):
+            block = held if s == 0 else lax.ppermute(held, "y", xor_perm(n_y, s))
+            parts += [block, lax.ppermute(block, "c", xor_perm(n_c, 1))]
 
     first = lax.axis_index(("xh", "z")) * local
-    pos = jnp.stack([i_xh, i_y, i_c, first]).astype(jnp.int32)
-    own_ids = lax.dynamic_slice_in_dim(ids, first, local)[:, None]
+    pos = jnp.stack([i_xh, i_y, i_c, first, i_x]).astype(jnp.int32)
     weights = (
         w_spatial.reshape(9 * ch, ch),
         w_temporal.reshape(3 * ch, ch),
@@ -335,30 +342,45 @@
         w_value,
         w_out,
     )
-    send, keep, g_head = local_terms(sizes, pos, ids[None], own_ids, parts, weights, upstream)
-
-    shared = keep + lax.ppermute(send, "c", xor_perm(n_c, 1)).astype(F32)
-    shared = scatter_xor(shared, "y", n_y, i_y)
-    block = jnp.concatenate([shared, g_head])
+    send, keep, heads = local_terms(sizes, pos, ids[None], parts, weights, upstream)
+
     n_x = n_xh * n_dp
-    block = scatter_xor(block, ("xh", "dp"), n_x, i_x)
+    x_axes = ("xh", "dp")
+    other = [lax.ppermute(send[s], "c", xor_perm(n_c, 1)) for s in range(n_y)]
+    both = [keep[s].astype(F32) + other[s].astype(F32) for s in range(n_y)]
+    shared = both[0]
+    for s in range(1, n_y):
+        shared = shared + lax.ppermute(both[s].astype(BF), "y", xor_perm(n_y, s)).astype(F32)
+    own_head = heads[0].astype(F32)
+    for r in range(1, n_x):
+        own_head = own_head + lax.ppermute(heads[r], x_axes, xor_perm(n_x, r)).astype(F32)
+    cut = shared.shape[0] // n_x
+    low = shared.astype(BF)
+    total = shared[:cut]
+    for r in range(1, n_x):
+        got = lax.ppermute(low[r * cut : (r + 1) * cut], x_axes, xor_perm(n_x, r))
+        total = total + got.astype(F32)
+    block = jnp.concatenate([total, own_head])
     rows = block.shape[0] // n_z
     got = lax.all_to_all(block.astype(BF).reshape(n_z, rows, ch), "z", 0, 0)
     factor = float(n_dp * tokens) ** (-0.5)
     done = (jnp.sum(got.astype(F32), axis=0) * factor).astype(BF)
+
     done = spread(done, "z", n_z).reshape(n_z * rows, ch)
-    done = jnp.concatenate(gather_xor(done, ("xh", "dp"), n_x, i_x))
-    cut = shared.shape[0]
-    heads = done[cut:].astype(F32).reshape(4, ch, -1)
-    done = jnp.concatenate(gather_xor(done[:cut], "y", n_y, i_y))
-    done = jnp.concatenate(gather_xor(done, "c", n_c, i_c)).astype(F32)
+    piece = jnp.concatenate(gather_xor(done[:cut], x_axes, n_x, i_x))
+    own_head, piece = lax.optimization_barrier((done[cut:], piece))
+    g_heads = [part.astype(F32) for part in gather_xor(own_head, x_axes, n_x, i_x)]
+    pieces = [piece] + [lax.ppermute(piece, "y", xor_perm(n_y, s)) for s in range(1, n_y)]
+    others = [lax.ppermute(p, "c", xor_perm(n_c, 1)) for p in pieces]
+    pieces, others = unxor(pieces, i_y), unxor(others, i_y)
+    halves = []
+    for c in range(n_c):
+        halves += [jnp.where(i_c == c, p, o).astype(F32) for p, o in zip(pieces, others)]
+    n_ws = 9 * ch // halves[0].shape[0]
     return (
-        done[: 9 * ch].reshape(9, ch, ch),
-        done[9 * ch :].reshape(3, ch, ch),
-        heads[0],
-        heads[1],
-        heads[2],
-        heads[3],
+        jnp.concatenate(halves[:n_ws]).reshape(9, ch, ch),
+        jnp.concatenate(halves[n_ws:]).reshape(3, ch, ch),
+        *g_heads,
     )
 
 

time: 182 us -> 160 us (0.88)
  waiting for transfers between devices: 40.3 us -> 21.3 us
  starting transfers between devices: 35.5 us -> 49.2 us
  Pallas kernels: 54.3 us -> 40.6 us
  local copies, waits for them, and re-layouts: 6.68 us -> 2.26 us
    ppermute x11 -> x27, starting transfers between devices: 13.7 us -> 34.2 us  [the longest x4 9.79 us: on_device(): others = [lax.ppermute(p, 'c', xor_perm(n_c, 1)) for p in pieces]]
    pallas_call x1, Pallas kernels: 54.3 us -> 40.6 us  [local_terms(): pl.pallas_call(functools.partial(local_kernel, sizes), name='local_terms'...]
    ppermute x11 -> x27, waiting for transfers between devices: 27.6 us -> 15.1 us  [the longest x6 5.82 us: on_device(): block = held if s == 0 else lax.ppermute(held, 'y', xor_perm(n_y, s))]
    ppermute x7 -> x6, starting transfers between devices: 14.5 us -> 6.4 us  [gather_xor(): lax.ppermute(block, axis, xor_perm(count, s))]
    ppermute x7 -> x6, waiting for transfers between devices: 12.7 us -> 5.87 us  [gather_xor(): lax.ppermute(block, axis, xor_perm(count, s))]
    reshape x0 -> x2, other arithmetic: none -> 2.57 us  [the longest x1 1.63 us: on_device(): jnp.concatenate(halves[:n_ws]).reshape(9, ch, ch)]
    slice x2 -> x3, local copies, waits for them, and re-layouts: 2.54 us -> 0.03 us  [the longest x1 0.01 us: on_device(): got = lax.ppermute(low[r * cut:(r + 1) * cut], x_axes, xor_perm(n_x, r))]
    ppermute x4 -> x8, starting transfers between devices: 7.29 us -> 8.64 us  [on_device(): parts += [block, lax.ppermute(block, 'c', xor_perm(n_c, 1))]]
  transfers between devices with their start and end apart: 22 -> 41, of which waited for: 16 -> 14; matrix products, arithmetic and copies ran while one was open for 2% -> 2% of each run, Pallas kernels for 0% -> 0%
where the time goes in v3:
time: 160 us
  starting transfers between devices  49.2 us (31%)
  Pallas kernels  40.6 us (25%)
  blocking collectives  38.7 us (24%)
  waiting for transfers between devices  21.3 us (13%)
  other arithmetic  6.75 us (4%)
  local copies, waits for them, and re-layouts  2.26 us (1%)
    pallas_call x1, Pallas kernels, local_terms(): pl.pallas_call(functools.partial(local_kernel, sizes), name='local_terms'...  40.6 us
    all_to_all x2, blocking collectives, spread(): lax.all_to_all(jnp.broadcast_to(block[None], (count,) + block.shape), axi...  27.7 us
    all_to_all x1, blocking collectives, on_device(): got = lax.all_to_all(block.astype(BF).reshape(n_z, rows, ch), 'z', 0, 0)  11 us
    ppermute x4, starting transfers between devices, on_device(): others = [lax.ppermute(p, 'c', xor_perm(n_c, 1)) for p in pieces]  9.79 us
    ppermute x8, starting transfers between devices, on_device(): parts += [block, lax.ppermute(block, 'c', xor_perm(n_c, 1))]  8.64 us
    ppermute x6, starting transfers between devices, on_device(): block = held if s == 0 else lax.ppermute(held, 'y', xor_perm(n_y, s))  6.97 us
    ppermute x6, starting transfers between devices, gather_xor(): lax.ppermute(block, axis, xor_perm(count, s))  6.4 us
    ppermute x6, waiting for transfers between devices, gather_xor(): lax.ppermute(block, axis, xor_perm(count, s))  5.87 us
  transfers between devices with their start and end apart: 41, of which 14 were waited for; matrix products, arithmetic and copies ran while one was open for 2% of the time, Pallas kernels for 0%

profile of v3, /device:TPU:1, one launch (start us, length us, event | category | flops | bytes accessed | tf_op | source)
XLA Modules:
  0.0 159.9 jit_solution(3629018932185572269)
XLA Ops:
  0.7 0.9 copy-done
  1.6 16.6 %all_to_all.15.refs_0_ = bf16[8,32,256]{2,1,0:T(8,128)(2,1)S(1)} all-to-all(bf16[8,32,256]{2,1,0:T(8,128)(2,1)S(1)} %broadcast_in_dim.7), channel_id=1, replica_groups=mesh['xh'=2,'z'=8,'y'=4,'c'=2,'dp'=2] {'z'}, dimensions={0} | all-to-all | bytes 262144 | tf_op jit(solution)/shard_map/all_to_all | solution.py:51
  18.1 1.3 collective-permute-start.1
  19.4 2.6 %collective-permute-start.3 = (bf16[8,32,256]{2,1,0:T(8,128)(2,1)S(1)}, bf16[8,32,256]{2,1,0:T(8,128)(2,1)S(1)}, u32[]{:S(2)}, u32[]{:S(2)}) collective-permute-start(bf16[8,32,256]{2,1,0:T(8,128)(2,1)S(1)} %all_to_all.15.refs_0_), channel_id=1, source_target_pairs={{0,8},{4,12},{8,0},{12,4},{1,9},{5,13},{9,1},{13,5},{2,10},{6,14},... | collective-permute-start | bytes 393224 | tf_op jit(solution)/shard_map/ppermute | solution.py:332
  22.1 2.7 %collective-permute-start.7 = (bf16[8,32,256]{2,1,0:T(8,128)(2,1)S(1)}, bf16[8,32,256]{2,1,0:T(8,128)(2,1)S(1)}, u32[]{:S(2)}, u32[]{:S(2)}) collective-permute-start(bf16[8,32,256]{2,1,0:T(8,128)(2,1)S(1)} %all_to_all.15.refs_0_), channel_id=1, source_target_pairs={{0,128},{128,0},{1,129},{129,1},{2,130},{130,2},{3,131},{131,3},{4... | collective-permute-start | bytes 393224 | tf_op jit(solution)/shard_map/ppermute | solution.py:330
  24.8 3.1 %collective-permute-start = (bf16[8,32,256]{2,1,0:T(8,128)(2,1)S(1)}, bf16[8,32,256]{2,1,0:T(8,128)(2,1)S(1)}, u32[]{:S(2)}, u32[]{:S(2)}) collective-permute-start(bf16[8,32,256]{2,1,0:T(8,128)(2,1)S(1)} %all_to_all.15.refs_0_), channel_id=1, source_target_pairs={{0,2},{2,0},{1,3},{3,1},{4,6},{6,4},{5,7},{7,5},{8,10},{10,8},{9,1... | collective-permute-start | bytes 393224 | tf_op jit(solution)/shard_map/ppermute | solution.py:333
  27.9 0.2 collective-permute-start.2
  28.2 1.2 collective-permute-start.4
  29.3 3.0 %collective-permute-start.11 = (bf16[8,32,256]{2,1,0:T(8,128)(2,1)S(1)}, bf16[8,32,256]{2,1,0:T(8,128)(2,1)S(1)}, u32[]{:S(2)}, u32[]{:S(2)}) collective-permute-start(bf16[8,32,256]{2,1,0:T(8,128)(2,1)S(1)} %collective-permute-done.7.refs_8_), channel_id=1, source_target_pairs={{0,8},{4,12},{8,0},{12,4},{1,9},{5,13},{9,1},{13,5},{2,10},{6,14},... | collective-permute-start | bytes 393224 | tf_op jit(solution)/shard_map/ppermute | solution.py:332
  32.3 1.9 %collective-permute-done.5.refs_6_ = bf16[8,32,256]{2,1,0:T(8,128)(2,1)S(1)} collective-permute-done((bf16[8,32,256]{2,1,0:T(8,128)(2,1)S(1)}, bf16[8,32,256]{2,1,0:T(8,128)(2,1)S(1)}, u32[]{:S(2)}, u32[]{:S(2)}) %collective-permute-start.5) | collective-permute-done | bytes 131104 | tf_op jit(solution)/shard_map/ppermute | solution.py:332
  34.3 1.7 %collective-permute-start.8 = (bf16[8,32,256]{2,1,0:T(8,128)(2,1)S(1)}, bf16[8,32,256]{2,1,0:T(8,128)(2,1)S(1)}, u32[]{:S(2)}, u32[]{:S(2)}) collective-permute-start(bf16[8,32,256]{2,1,0:T(8,128)(2,1)S(1)} %collective-permute-done.7.refs_8_), channel_id=1, source_target_pairs={{0,2},{2,0},{1,3},{3,1},{4,6},{6,4},{5,7},{7,5},{8,10},{10,8},{9,1... | collective-permute-start | bytes 393224 | tf_op jit(solution)/shard_map/ppermute | solution.py:333
  36.1 0.1 collective-permute-start.6
  36.2 0.4 collective-permute-start.10
  36.6 1.8 %collective-permute-done.11.refs_12_ = bf16[8,32,256]{2,1,0:T(8,128)(2,1)S(1)} collective-permute-done((bf16[8,32,256]{2,1,0:T(8,128)(2,1)S(1)}, bf16[8,32,256]{2,1,0:T(8,128)(2,1)S(1)}, u32[]{:S(2)}, u32[]{:S(2)}) %collective-permute-start.11) | collective-permute-done | bytes 131104 | tf_op jit(solution)/shard_map/ppermute | solution.py:332
  38.5 1.2 collective-permute-start.12
  39.7 2.0 %collective-permute-done.13.refs_14_ = bf16[8,32,256]{2,1,0:T(8,128)(2,1)S(1)} collective-permute-done((bf16[8,32,256]{2,1,0:T(8,128)(2,1)S(1)}, bf16[8,32,256]{2,1,0:T(8,128)(2,1)S(1)}, u32[]{:S(2)}, u32[]{:S(2)}) %collective-permute-start.13) | collective-permute-done | bytes 131104 | tf_op jit(solution)/shard_map/ppermute | solution.py:332
  41.7 0.7 collective-permute-start.14
  42.4 0.6 stack.23.pos
  43.0 0.3 collective-permute-done.14.refs_15_
  43.5 0.2 copy-done.19
  43.8 0.2 copy-done.22
  44.0 40.6 %local_terms.1 = (bf16[384,256]{1,0:T(8,128)(2,1)}, bf16[384,256]{1,0:T(8,128)(2,1)}, bf16[384,256]{1,0:T(8,128)(2,1)}, bf16[384,256]{1,0:T(8,128)(2,1)}, bf16[3...) custom-call(s32[5]{0:T(128)} %stack.23.pos, ...), custom_call_target="tpu_custom_call" | custom-call | flops 24000000000 | bytes 12582912 | tf_op jit(solution)/shard_map/local_terms/pallas_call | solution.py:281
  84.7 0.4 collective-permute-start.20
  85.1 0.3 collective-permute-start.18
  85.4 0.2 collective-permute-start.16
  85.6 0.3 collective-permute-start.15
  85.9 0.5 collective-permute-done.20
  86.4 1.0 add_convert_fusion
  87.4 0.6 collective-permute-start.21
  88.0 1.0 add_convert_fusion.1
  89.0 0.3 collective-permute-start.19
  89.3 2.6 %collective-permute-start.17 = (bf16[384,256]{1,0:T(8,128)(2,1)S(1)}, bf16[384,256]{1,0:T(8,128)(2,1)S(1)}, u32[]{:S(2)}, u32[]{:S(2)}) collective-permute-start(bf16[384,256]{1,0:T(8,128)(2,1)S(1)} %add_convert_fusion.2), channel_id=1, source_target_pairs={{0,4},{4,0},{8,12},{12,8},{1,5},{5,1},{9,13},{13,9},{2,6},{6,2},{1... | collective-permute-start | bytes 589832 | tf_op jit(solution)/shard_map/ppermute | solution.py:353
  92.0 1.5 collective-permute-start.27
  93.4 0.8 collective-permute-start.26
  94.2 4.8 %collective-permute-done.21 = bf16[384,256]{1,0:T(8,128)(2,1)S(1)} collective-permute-done((bf16[384,256]{1,0:T(8,128)(2,1)S(1)}, bf16[384,256]{1,0:T(8,128)(2,1)S(1)}, u32[]{:S(2)}, u32[]{:S(2)}) %collective-permute-start.21) | collective-permute-done | bytes 196640 | tf_op jit(solution)/shard_map/ppermute | solution.py:353
  99.0 0.5 collective-permute-start.25
  99.5 1.0 collective-permute-done.17
  100.5 0.1 fusion.3
  100.6 1.6 collective-permute-start.24
  102.2 0.8 collective-permute-start.23
  102.9 1.0 collective-permute-start.22
  104.0 0.8 collective-permute-done.24
  104.8 1.8 %collective-permute-done.23 = bf16[96,256]{1,0:T(8,128)(2,1)S(1)} collective-permute-done((bf16[96,256]{1,0:T(8,128)(2,1)S(1)}, bf16[96,256]{1,0:T(8,128)(2,1)S(1)}, u32[]{:S(2)}, u32[]{:S(2)}) %collective-permute-start.23) | collective-permute-done | bytes 49184 | tf_op jit(solution)/shard_map/ppermute | solution.py:361
  106.8 11.0 %all_to_all.16 = bf16[8,44,256]{2,1,0:T(8,128)(2,1)S(1)} all-to-all(bf16[8,44,256]{2,1,0:T(8,128)(2,1)S(1)} %convert_element_type.123), channel_id=1, replica_groups=mesh['xh'=2,'z'=8,'y'=4,'c'=2,'dp'=2] {'z'}, dimensions={0} | all-to-all | bytes 360448 | tf_op jit(solution)/shard_map/all_to_all | solution.py:365
  117.9 11.1 %all_to_all.17 = bf16[8,44,256]{2,1,0:T(8,128)(2,1)S(1)} all-to-all(bf16[8,44,256]{2,1,0:T(8,128)(2,1)S(1)} %broadcast_in_dim.16), channel_id=1, replica_groups=mesh['xh'=2,'z'=8,'y'=4,'c'=2,'dp'=2] {'z'}, dimensions={0} | all-to-all | bytes 360448 | tf_op jit(solution)/shard_map/all_to_all | solution.py:51
  129.0 1.3 collective-permute-start.28
  130.3 0.9 collective-permute-start.29
  131.2 1.2 collective-permute-start.30
  132.4 1.2 collective-permute-done.28
  133.6 1.2 collective-permute-done.29
  134.8 1.5 collective-permute-start.39
  136.3 1.6 collective-permute-start.32
  137.9 2.3 %collective-permute-start.31 = (bf16[384,256]{1,0:T(8,128)(2,1)S(1)}, bf16[384,256]{1,0:T(8,128)(2,1)S(1)}, u32[]{:S(2)}, u32[]{:S(2)}) collective-permute-start(bf16[384,256]{1,0:T(8,128)(2,1)S(1)} %pad_maximum_fusion.1), channel_id=1, source_target_pairs={{0,12},{4,8},{8,4},{12,0},{1,13},{5,9},{9,5},{13,1},{2,14},{6,10},... | collective-permute-start | bytes 589832 | tf_op jit(solution)/shard_map/ppermute | solution.py:373
  140.2 1.5 collective-permute-start.38
  141.7 3.5 %collective-permute-done.38 = bf16[256,256]{1,0:T(8,128)(2,1)S(1)} collective-permute-done((bf16[256,256]{1,0:T(8,128)(2,1)S(1)}, bf16[256,256]{1,0:T(8,128)(2,1)S(1)}, u32[]{:S(2)}, u32[]{:S(2)}) %collective-permute-start.38) | collective-permute-done | bytes 131104 | tf_op jit(solution)/shard_map/ppermute | solution.py:46
  145.2 9.2 %collective-permute-start.37 = (bf16[384,256]{1,0:T(8,128)(2,1)S(1)}, bf16[384,256]{1,0:T(8,128)(2,1)S(1)}, u32[]{:S(2)}, u32[]{:S(2)}) collective-permute-start(bf16[384,256]{1,0:T(8,128)(2,1)S(1)} %pad_maximum_fusion.1), channel_id=1, source_target_pairs={{0,2},{2,0},{1,3},{3,1},{4,6},{6,4},{5,7},{7,5},{8,10},{10,8},{9,1... | collective-permute-start | bytes 589832 | tf_op jit(solution)/shard_map/ppermute | solution.py:374
  154.4 0.5 collective-permute-start.35
  155.0 1.0 select_convert_fusion
  156.1 0.3 collective-permute-done.34
  156.4 0.2 broadcast_select_fusion
  156.6 0.1 select_dynamic-update-slice_fusion.5
  156.7 0.1 select_dynamic-update-slice_fusion.4
  157.3 1.6 %convert.12 = f32[9,256,256]{2,1,0:T(8,128)} convert(bf16[9,256,256]{2,1,0:T(8,128)(2,1)S(1)} %bitcast.14) | non-fusion elementwise | flops 589824 | bytes 3538944 | tf_op jit(solution)/shard_map/reshape | solution.py:381
  158.9 0.9 convert.13
  (99 shorter events, 1.3 us)
Async XLA Ops:
  0.6 0.9 copy-start
  18.1 25.2 %copy-start.4 = (bf16[8,32,256]{2,1,0:T(8,128)(2,1)}, bf16[8,32,256]{2,1,0:T(8,128)(2,1)S(1)}, u32[]{:S(2)}) copy-start(bf16[8,32,256]{2,1,0:T(8,128)(2,1)S(1)} %all_to_all.15.refs_0_) | copy-start | bytes 393220
  18.1 9.8 %collective-permute-start.1 = (bf16[8,32,256]{2,1,0:T(8,128)(2,1)S(1)}, bf16[8,32,256]{2,1,0:T(8,128)(2,1)S(1)}, u32[]{:S(2)}, u32[]{:S(2)}) collective-permute-start(bf16[8,32,256]{2,1,0:T(8,128)(2,1)S(1)} %all_to_all.15.refs_0_), channel_id=1, source_target_pairs={{0,4},{4,0},{8,12},{12,8},{1,5},{5,1},{9,13},{13,9},{2,6},{6,2},{1... | collective-permute-start | bytes 393224 | tf_op jit(solution)/shard_map/ppermute | solution.py:332
  19.4 8.7 %collective-permute-start.3 = (bf16[8,32,256]{2,1,0:T(8,128)(2,1)S(1)}, bf16[8,32,256]{2,1,0:T(8,128)(2,1)S(1)}, u32[]{:S(2)}, u32[]{:S(2)}) collective-permute-start(bf16[8,32,256]{2,1,0:T(8,128)(2,1)S(1)} %all_to_all.15.refs_0_), channel_id=1, source_target_pairs={{0,8},{4,12},{8,0},{12,4},{1,9},{5,13},{9,1},{13,5},{2,10},{6,14},... | collective-permute-start | bytes 393224 | tf_op jit(solution)/shard_map/ppermute | solution.py:332
  22.1 7.3 %collective-permute-start.7 = (bf16[8,32,256]{2,1,0:T(8,128)(2,1)S(1)}, bf16[8,32,256]{2,1,0:T(8,128)(2,1)S(1)}, u32[]{:S(2)}, u32[]{:S(2)}) collective-permute-start(bf16[8,32,256]{2,1,0:T(8,128)(2,1)S(1)} %all_to_all.15.refs_0_), channel_id=1, source_target_pairs={{0,128},{128,0},{1,129},{129,1},{2,130},{130,2},{3,131},{131,3},{4... | collective-permute-start | bytes 393224 | tf_op jit(solution)/shard_map/ppermute | solution.py:330
  24.8 4.5 %collective-permute-start = (bf16[8,32,256]{2,1,0:T(8,128)(2,1)S(1)}, bf16[8,32,256]{2,1,0:T(8,128)(2,1)S(1)}, u32[]{:S(2)}, u32[]{:S(2)}) collective-permute-start(bf16[8,32,256]{2,1,0:T(8,128)(2,1)S(1)} %all_to_all.15.refs_0_), channel_id=1, source_target_pairs={{0,2},{2,0},{1,3},{3,1},{4,6},{6,4},{5,7},{7,5},{8,10},{10,8},{9,1... | collective-permute-start | bytes 393224 | tf_op jit(solution)/shard_map/ppermute | solution.py:333
  27.9 6.3 %collective-permute-start.5 = (bf16[8,32,256]{2,1,0:T(8,128)(2,1)S(1)}, bf16[8,32,256]{2,1,0:T(8,128)(2,1)S(1)}, u32[]{:S(2)}, u32[]{:S(2)}) collective-permute-start(bf16[8,32,256]{2,1,0:T(8,128)(2,1)S(1)} %all_to_all.15.refs_0_), channel_id=1, source_target_pairs={{0,12},{4,8},{8,4},{12,0},{1,13},{5,9},{9,5},{13,1},{2,14},{6,10},... | collective-permute-start | bytes 393224 | tf_op jit(solution)/shard_map/ppermute | solution.py:332
  27.9 15.4 %copy-start.5 = (bf16[8,32,256]{2,1,0:T(8,128)(2,1)}, bf16[8,32,256]{2,1,0:T(8,128)(2,1)S(1)}, u32[]{:S(2)}) copy-start(bf16[8,32,256]{2,1,0:T(8,128)(2,1)S(1)} %collective-permute-done.1.refs_2_) | copy-start | bytes 393220
  27.9 6.4 %collective-permute-start.2 = (bf16[8,32,256]{2,1,0:T(8,128)(2,1)S(1)}, bf16[8,32,256]{2,1,0:T(8,128)(2,1)S(1)}, u32[]{:S(2)}, u32[]{:S(2)}) collective-permute-start(bf16[8,32,256]{2,1,0:T(8,128)(2,1)S(1)} %collective-permute-done.1.refs_2_), channel_id=1, source_target_pairs={{0,2},{2,0},{1,3},{3,1},{4,6},{6,4},{5,7},{7,5},{8,10},{10,8},{9,1... | collective-permute-start | bytes 393224 | tf_op jit(solution)/shard_map/ppermute | solution.py:333
  28.2 15.2 %copy-start.6 = (bf16[8,32,256]{2,1,0:T(8,128)(2,1)}, bf16[8,32,256]{2,1,0:T(8,128)(2,1)S(1)}, u32[]{:S(2)}) copy-start(bf16[8,32,256]{2,1,0:T(8,128)(2,1)S(1)} %collective-permute-done.3.refs_4_) | copy-start | bytes 393220
  28.2 7.9 %collective-permute-start.4 = (bf16[8,32,256]{2,1,0:T(8,128)(2,1)S(1)}, bf16[8,32,256]{2,1,0:T(8,128)(2,1)S(1)}, u32[]{:S(2)}, u32[]{:S(2)}) collective-permute-start(bf16[8,32,256]{2,1,0:T(8,128)(2,1)S(1)} %collective-permute-done.3.refs_4_), channel_id=1, source_target_pairs={{0,2},{2,0},{1,3},{3,1},{4,6},{6,4},{5,7},{7,5},{8,10},{10,8},{9,1... | collective-permute-start | bytes 393224 | tf_op jit(solution)/shard_map/ppermute | solution.py:333
  29.3 14.1 %copy-start.7 = (bf16[8,32,256]{2,1,0:T(8,128)(2,1)}, bf16[8,32,256]{2,1,0:T(8,128)(2,1)S(1)}, u32[]{:S(2)}) copy-start(bf16[8,32,256]{2,1,0:T(8,128)(2,1)S(1)} %collective-permute-done.7.refs_8_) | copy-start | bytes 393220
  29.3 6.9 %collective-permute-start.9 = (bf16[8,32,256]{2,1,0:T(8,128)(2,1)S(1)}, bf16[8,32,256]{2,1,0:T(8,128)(2,1)S(1)}, u32[]{:S(2)}, u32[]{:S(2)}) collective-permute-start(bf16[8,32,256]{2,1,0:T(8,128)(2,1)S(1)} %collective-permute-done.7.refs_8_), channel_id=1, source_target_pairs={{0,4},{4,0},{8,12},{12,8},{1,5},{5,1},{9,13},{13,9},{2,6},{6,2},{1... | collective-permute-start | bytes 393224 | tf_op jit(solution)/shard_map/ppermute | solution.py:332
  29.3 14.1 %copy-start.8 = (bf16[8,32,256]{2,1,0:T(8,128)(2,1)}, bf16[8,32,256]{2,1,0:T(8,128)(2,1)S(1)}, u32[]{:S(2)}) copy-start(bf16[8,32,256]{2,1,0:T(8,128)(2,1)S(1)} %collective-permute-done.refs_1_) | copy-start | bytes 393220
  29.3 9.1 %collective-permute-start.11 = (bf16[8,32,256]{2,1,0:T(8,128)(2,1)S(1)}, bf16[8,32,256]{2,1,0:T(8,128)(2,1)S(1)}, u32[]{:S(2)}, u32[]{:S(2)}) collective-permute-start(bf16[8,32,256]{2,1,0:T(8,128)(2,1)S(1)} %collective-permute-done.7.refs_8_), channel_id=1, source_target_pairs={{0,8},{4,12},{8,0},{12,4},{1,9},{5,13},{9,1},{13,5},{2,10},{6,14},... | collective-permute-start | bytes 393224 | tf_op jit(solution)/shard_map/ppermute | solution.py:332
  34.3 9.1 %copy-start.9 = (bf16[8,32,256]{2,1,0:T(8,128)(2,1)}, bf16[8,32,256]{2,1,0:T(8,128)(2,1)S(1)}, u32[]{:S(2)}) copy-start(bf16[8,32,256]{2,1,0:T(8,128)(2,1)S(1)} %collective-permute-done.5.refs_6_) | copy-start | bytes 393220
  34.3 7.5 %collective-permute-start.13 = (bf16[8,32,256]{2,1,0:T(8,128)(2,1)S(1)}, bf16[8,32,256]{2,1,0:T(8,128)(2,1)S(1)}, u32[]{:S(2)}, u32[]{:S(2)}) collective-permute-start(bf16[8,32,256]{2,1,0:T(8,128)(2,1)S(1)} %collective-permute-done.7.refs_8_), channel_id=1, source_target_pairs={{0,12},{4,8},{8,4},{12,0},{1,13},{5,9},{9,5},{13,1},{2,14},{6,10},... | collective-permute-start | bytes 393224 | tf_op jit(solution)/shard_map/ppermute | solution.py:332
  34.3 9.1 %copy-start.11 = (bf16[8,32,256]{2,1,0:T(8,128)(2,1)}, bf16[8,32,256]{2,1,0:T(8,128)(2,1)S(1)}, u32[]{:S(2)}) copy-start(bf16[8,32,256]{2,1,0:T(8,128)(2,1)S(1)} %collective-permute-done.2.refs_3_) | copy-start | bytes 393220
  34.3 8.6 %collective-permute-start.8 = (bf16[8,32,256]{2,1,0:T(8,128)(2,1)S(1)}, bf16[8,32,256]{2,1,0:T(8,128)(2,1)S(1)}, u32[]{:S(2)}, u32[]{:S(2)}) collective-permute-start(bf16[8,32,256]{2,1,0:T(8,128)(2,1)S(1)} %collective-permute-done.7.refs_8_), channel_id=1, source_target_pairs={{0,2},{2,0},{1,3},{3,1},{4,6},{6,4},{5,7},{7,5},{8,10},{10,8},{9,1... | collective-permute-start | bytes 393224 | tf_op jit(solution)/shard_map/ppermute | solution.py:333
  36.1 7.3 %copy-start.13 = (bf16[8,32,256]{2,1,0:T(8,128)(2,1)}, bf16[8,32,256]{2,1,0:T(8,128)(2,1)S(1)}, u32[]{:S(2)}) copy-start(bf16[8,32,256]{2,1,0:T(8,128)(2,1)S(1)} %collective-permute-done.4.refs_5_) | copy-start | bytes 393220
  36.1 6.9 %collective-permute-start.6 = (bf16[8,32,256]{2,1,0:T(8,128)(2,1)S(1)}, bf16[8,32,256]{2,1,0:T(8,128)(2,1)S(1)}, u32[]{:S(2)}, u32[]{:S(2)}) collective-permute-start(bf16[8,32,256]{2,1,0:T(8,128)(2,1)S(1)} %collective-permute-done.5.refs_6_), channel_id=1, source_target_pairs={{0,2},{2,0},{1,3},{3,1},{4,6},{6,4},{5,7},{7,5},{8,10},{10,8},{9,1... | collective-permute-start | bytes 393224 | tf_op jit(solution)/shard_map/ppermute | solution.py:333
  36.2 7.2 %copy-start.15 = (bf16[8,32,256]{2,1,0:T(8,128)(2,1)}, bf16[8,32,256]{2,1,0:T(8,128)(2,1)S(1)}, u32[]{:S(2)}) copy-start(bf16[8,32,256]{2,1,0:T(8,128)(2,1)S(1)} %collective-permute-done.9.refs_10_) | copy-start | bytes 393220
  36.2 6.8 %collective-permute-start.10 = (bf16[8,32,256]{2,1,0:T(8,128)(2,1)S(1)}, bf16[8,32,256]{2,1,0:T(8,128)(2,1)S(1)}, u32[]{:S(2)}, u32[]{:S(2)}) collective-permute-start(bf16[8,32,256]{2,1,0:T(8,128)(2,1)S(1)} %collective-permute-done.9.refs_10_), channel_id=1, source_target_pairs={{0,2},{2,0},{1,3},{3,1},{4,6},{6,4},{5,7},{7,5},{8,10},{10,8},{9,1... | collective-permute-start | bytes 393224 | tf_op jit(solution)/shard_map/ppermute | solution.py:333
  38.5 5.0 %copy-start.16 = (bf16[8,32,256]{2,1,0:T(8,128)(2,1)}, bf16[8,32,256]{2,1,0:T(8,128)(2,1)S(1)}, u32[]{:S(2)}) copy-start(bf16[8,32,256]{2,1,0:T(8,128)(2,1)S(1)} %collective-permute-done.11.refs_12_) | copy-start | bytes 393220
  38.5 4.6 %collective-permute-start.12 = (bf16[8,32,256]{2,1,0:T(8,128)(2,1)S(1)}, bf16[8,32,256]{2,1,0:T(8,128)(2,1)S(1)}, u32[]{:S(2)}, u32[]{:S(2)}) collective-permute-start(bf16[8,32,256]{2,1,0:T(8,128)(2,1)S(1)} %collective-permute-done.11.refs_12_), channel_id=1, source_target_pairs={{0,2},{2,0},{1,3},{3,1},{4,6},{6,4},{5,7},{7,5},{8,10},{10,8},{9,1... | collective-permute-start | bytes 393224 | tf_op jit(solution)/shard_map/ppermute | solution.py:333
  41.7 1.7 %copy-start.17 = (bf16[8,32,256]{2,1,0:T(8,128)(2,1)}, bf16[8,32,256]{2,1,0:T(8,128)(2,1)S(1)}, u32[]{:S(2)}) copy-start(bf16[8,32,256]{2,1,0:T(8,128)(2,1)S(1)} %collective-permute-done.13.refs_14_) | copy-start | bytes 393220
  41.7 1.6 %collective-permute-start.14 = (bf16[8,32,256]{2,1,0:T(8,128)(2,1)S(1)}, bf16[8,32,256]{2,1,0:T(8,128)(2,1)S(1)}, u32[]{:S(2)}, u32[]{:S(2)}) collective-permute-start(bf16[8,32,256]{2,1,0:T(8,128)(2,1)S(1)} %collective-permute-done.13.refs_14_), channel_id=1, source_target_pairs={{0,2},{2,0},{1,3},{3,1},{4,6},{6,4},{5,7},{7,5},{8,10},{10,8},{9,1... | collective-permute-start | bytes 393224 | tf_op jit(solution)/shard_map/ppermute | solution.py:333
  43.0 0.7 copy-start.19
  43.0 0.7 copy-start.18
  43.0 0.7 copy-start.20
  43.0 0.7 copy-start.21
  43.4 0.7 copy-start.22
  84.6 4.7 %copy-start.2 = (bf16[384,256]{1,0:T(8,128)(2,1)S(1)}, bf16[384,256]{1,0:T(8,128)(2,1)}, u32[]{:S(2)}) copy-start(bf16[384,256]{1,0:T(8,128)(2,1)} %get-tuple-element.22) | copy-start | bytes 589828
  84.6 7.3 %copy-start.14 = (bf16[256,256]{1,0:T(8,128)(2,1)S(1)}, bf16[256,256]{1,0:T(8,128)(2,1)}, u32[]{:S(2)}) copy-start(bf16[256,256]{1,0:T(8,128)(2,1)} %get-tuple-element.31) | copy-start | bytes 393220
  84.6 8.8 %copy-start.12 = (bf16[256,256]{1,0:T(8,128)(2,1)S(1)}, bf16[256,256]{1,0:T(8,128)(2,1)}, u32[]{:S(2)}) copy-start(bf16[256,256]{1,0:T(8,128)(2,1)} %get-tuple-element.30) | copy-start | bytes 393220
  84.6 14.4 %copy-start.10 = (bf16[256,256]{1,0:T(8,128)(2,1)S(1)}, bf16[256,256]{1,0:T(8,128)(2,1)}, u32[]{:S(2)}) copy-start(bf16[256,256]{1,0:T(8,128)(2,1)} %get-tuple-element.29) | copy-start | bytes 393220
  84.7 15.8 %copy-start.1 = (bf16[384,256]{1,0:T(8,128)(2,1)S(1)}, bf16[384,256]{1,0:T(8,128)(2,1)}, u32[]{:S(2)}) copy-start(bf16[384,256]{1,0:T(8,128)(2,1)} %get-tuple-element.20) | copy-start | bytes 589828
  84.7 1.7 %collective-permute-start.20 = (bf16[384,256]{1,0:T(8,128)(2,1)}, bf16[384,256]{1,0:T(8,128)(2,1)S(1)}, u32[]{:S(2)}, u32[]{:S(2)}) collective-permute-start(bf16[384,256]{1,0:T(8,128)(2,1)} %get-tuple-element.27), channel_id=1, source_target_pairs={{0,2},{2,0},{1,3},{3,1},{4,6},{6,4},{5,7},{7,5},{8,10},{10,8},{9,1... | collective-permute-start | bytes 589832 | tf_op jit(solution)/shard_map/ppermute | solution.py:349
  85.1 2.8 %collective-permute-start.18 = (bf16[384,256]{1,0:T(8,128)(2,1)}, bf16[384,256]{1,0:T(8,128)(2,1)S(1)}, u32[]{:S(2)}, u32[]{:S(2)}) collective-permute-start(bf16[384,256]{1,0:T(8,128)(2,1)} %get-tuple-element.25), channel_id=1, source_target_pairs={{0,2},{2,0},{1,3},{3,1},{4,6},{6,4},{5,7},{7,5},{8,10},{10,8},{9,1... | collective-permute-start | bytes 589832 | tf_op jit(solution)/shard_map/ppermute | solution.py:349
  85.4 3.8 %collective-permute-start.16 = (bf16[384,256]{1,0:T(8,128)(2,1)}, bf16[384,256]{1,0:T(8,128)(2,1)S(1)}, u32[]{:S(2)}, u32[]{:S(2)}) collective-permute-start(bf16[384,256]{1,0:T(8,128)(2,1)} %get-tuple-element.23), channel_id=1, source_target_pairs={{0,2},{2,0},{1,3},{3,1},{4,6},{6,4},{5,7},{7,5},{8,10},{10,8},{9,1... | collective-permute-start | bytes 589832 | tf_op jit(solution)/shard_map/ppermute | solution.py:349
  85.6 7.8 %collective-permute-start.15 = (bf16[384,256]{1,0:T(8,128)(2,1)}, bf16[384,256]{1,0:T(8,128)(2,1)S(1)}, u32[]{:S(2)}, u32[]{:S(2)}) collective-permute-start(bf16[384,256]{1,0:T(8,128)(2,1)} %get-tuple-element.21), channel_id=1, source_target_pairs={{0,2},{2,0},{1,3},{3,1},{4,6},{6,4},{5,7},{7,5},{8,10},{10,8},{9,1... | collective-permute-start | bytes 589832 | tf_op jit(solution)/shard_map/ppermute | solution.py:349
  87.4 11.6 %collective-permute-start.21 = (bf16[384,256]{1,0:T(8,128)(2,1)S(1)}, bf16[384,256]{1,0:T(8,128)(2,1)S(1)}, u32[]{:S(2)}, u32[]{:S(2)}) collective-permute-start(bf16[384,256]{1,0:T(8,128)(2,1)S(1)} %add_convert_fusion), channel_id=1, source_target_pairs={{0,12},{4,8},{8,4},{12,0},{1,13},{5,9},{9,5},{13,1},{2,14},{6,10},... | collective-permute-start | bytes 589832 | tf_op jit(solution)/shard_map/ppermute | solution.py:353
  89.0 10.5 %collective-permute-start.19 = (bf16[384,256]{1,0:T(8,128)(2,1)S(1)}, bf16[384,256]{1,0:T(8,128)(2,1)S(1)}, u32[]{:S(2)}, u32[]{:S(2)}) collective-permute-start(bf16[384,256]{1,0:T(8,128)(2,1)S(1)} %add_convert_fusion.1), channel_id=1, source_target_pairs={{0,8},{4,12},{8,0},{12,4},{1,9},{5,13},{9,1},{13,5},{2,10},{6,14},... | collective-permute-start | bytes 589832 | tf_op jit(solution)/shard_map/ppermute | solution.py:353
  89.3 14.7 %copy-start.3 = (bf16[256,256]{1,0:T(8,128)(2,1)S(1)}, bf16[256,256]{1,0:T(8,128)(2,1)}, u32[]{:S(2)}) copy-start(bf16[256,256]{1,0:T(8,128)(2,1)} %get-tuple-element.28) | copy-start | bytes 393220
  89.3 11.1 %collective-permute-start.17 = (bf16[384,256]{1,0:T(8,128)(2,1)S(1)}, bf16[384,256]{1,0:T(8,128)(2,1)S(1)}, u32[]{:S(2)}, u32[]{:S(2)}) collective-permute-start(bf16[384,256]{1,0:T(8,128)(2,1)S(1)} %add_convert_fusion.2), channel_id=1, source_target_pairs={{0,4},{4,0},{8,12},{12,8},{1,5},{5,1},{9,13},{13,9},{2,6},{6,2},{1... | collective-permute-start | bytes 589832 | tf_op jit(solution)/shard_map/ppermute | solution.py:353
  92.0 11.0 %collective-permute-start.27 = (bf16[256,256]{1,0:T(8,128)(2,1)S(1)}, bf16[256,256]{1,0:T(8,128)(2,1)S(1)}, u32[]{:S(2)}, u32[]{:S(2)}) collective-permute-start(bf16[256,256]{1,0:T(8,128)(2,1)S(1)} %copy-done.14), channel_id=1, source_target_pairs={{0,129},{1,128},{128,1},{129,0},{2,131},{3,130},{130,3},{131,2},{4... | collective-permute-start | bytes 393224 | tf_op jit(solution)/shard_map/ppermute | solution.py:356
  93.4 10.5 %collective-permute-start.26 = (bf16[256,256]{1,0:T(8,128)(2,1)S(1)}, bf16[256,256]{1,0:T(8,128)(2,1)S(1)}, u32[]{:S(2)}, u32[]{:S(2)}) collective-permute-start(bf16[256,256]{1,0:T(8,128)(2,1)S(1)} %copy-done.12), channel_id=1, source_target_pairs={{0,128},{1,129},{128,0},{129,1},{2,130},{3,131},{130,2},{131,3},{4... | collective-permute-start | bytes 393224 | tf_op jit(solution)/shard_map/ppermute | solution.py:356
  99.0 4.9 %collective-permute-start.25 = (bf16[256,256]{1,0:T(8,128)(2,1)S(1)}, bf16[256,256]{1,0:T(8,128)(2,1)S(1)}, u32[]{:S(2)}, u32[]{:S(2)}) collective-permute-start(bf16[256,256]{1,0:T(8,128)(2,1)S(1)} %copy-done.10), channel_id=1, source_target_pairs={{0,1},{1,0},{128,129},{129,128},{2,3},{3,2},{130,131},{131,130},{4... | collective-permute-start | bytes 393224 | tf_op jit(solution)/shard_map/ppermute | solution.py:356
  100.6 4.2 %collective-permute-start.24 = (bf16[96,256]{1,0:T(8,128)(2,1)S(1)}, bf16[96,256]{1,0:T(8,128)(2,1)S(1)}, u32[]{:S(2)}, u32[]{:S(2)}) collective-permute-start(bf16[96,256]{1,0:T(8,128)(2,1)S(1)} %get-tuple-element.60), channel_id=1, source_target_pairs={{0,129},{1,128},{128,1},{129,0},{2,131},{3,130},{130,3},{131,2},{4... | collective-permute-start | bytes 147464 | tf_op jit(solution)/shard_map/ppermute | solution.py:361
  102.2 4.5 %collective-permute-start.23 = (bf16[96,256]{1,0:T(8,128)(2,1)S(1)}, bf16[96,256]{1,0:T(8,128)(2,1)S(1)}, u32[]{:S(2)}, u32[]{:S(2)}) collective-permute-start(bf16[96,256]{1,0:T(8,128)(2,1)S(1)} %get-tuple-element.61), channel_id=1, source_target_pairs={{0,128},{1,129},{128,0},{129,1},{2,130},{3,131},{130,2},{131,3},{4... | collective-permute-start | bytes 147464 | tf_op jit(solution)/shard_map/ppermute | solution.py:361
  102.9 3.7 %collective-permute-start.22 = (bf16[96,256]{1,0:T(8,128)(2,1)S(1)}, bf16[96,256]{1,0:T(8,128)(2,1)S(1)}, u32[]{:S(2)}, u32[]{:S(2)}) collective-permute-start(bf16[96,256]{1,0:T(8,128)(2,1)S(1)} %get-tuple-element.59), channel_id=1, source_target_pairs={{0,1},{1,0},{128,129},{129,128},{2,3},{3,2},{130,131},{131,130},{4... | collective-permute-start | bytes 147464 | tf_op jit(solution)/shard_map/ppermute | solution.py:361
  129.0 4.5 %collective-permute-start.28 = (bf16[96,256]{1,0:T(8,128)(2,1)S(1)}, bf16[96,256]{1,0:T(8,128)(2,1)S(1)}, u32[]{:S(2)}, u32[]{:S(2)}) collective-permute-start(bf16[96,256]{1,0:T(8,128)(2,1)S(1)} %slice.29), channel_id=1, source_target_pairs={{0,129},{1,128},{128,1},{129,0},{2,131},{3,130},{130,3},{131,2},{4... | collective-permute-start | bytes 147464 | tf_op jit(solution)/shard_map/ppermute | solution.py:46
  130.3 4.4 %collective-permute-start.29 = (bf16[96,256]{1,0:T(8,128)(2,1)S(1)}, bf16[96,256]{1,0:T(8,128)(2,1)S(1)}, u32[]{:S(2)}, u32[]{:S(2)}) collective-permute-start(bf16[96,256]{1,0:T(8,128)(2,1)S(1)} %slice.29), channel_id=1, source_target_pairs={{0,128},{1,129},{128,0},{129,1},{2,130},{3,131},{130,2},{131,3},{4... | collective-permute-start | bytes 147464 | tf_op jit(solution)/shard_map/ppermute | solution.py:46
  131.2 3.6 %collective-permute-start.30 = (bf16[96,256]{1,0:T(8,128)(2,1)S(1)}, bf16[96,256]{1,0:T(8,128)(2,1)S(1)}, u32[]{:S(2)}, u32[]{:S(2)}) collective-permute-start(bf16[96,256]{1,0:T(8,128)(2,1)S(1)} %slice.29), channel_id=1, source_target_pairs={{0,1},{1,0},{128,129},{129,128},{2,3},{3,2},{130,131},{131,130},{4... | collective-permute-start | bytes 147464 | tf_op jit(solution)/shard_map/ppermute | solution.py:46
  134.8 6.9 %collective-permute-start.39 = (bf16[256,256]{1,0:T(8,128)(2,1)S(1)}, bf16[256,256]{1,0:T(8,128)(2,1)S(1)}, u32[]{:S(2)}, u32[]{:S(2)}) collective-permute-start(bf16[256,256]{1,0:T(8,128)(2,1)S(1)} %slice.28), channel_id=1, source_target_pairs={{0,128},{1,129},{128,0},{129,1},{2,130},{3,131},{130,2},{131,3},{4... | collective-permute-start | bytes 393224 | tf_op jit(solution)/shard_map/ppermute | solution.py:46
  136.3 18.1 %collective-permute-start.33 = (bf16[384,256]{1,0:T(8,128)(2,1)S(1)}, bf16[384,256]{1,0:T(8,128)(2,1)S(1)}, u32[]{:S(2)}, u32[]{:S(2)}) collective-permute-start(bf16[384,256]{1,0:T(8,128)(2,1)S(1)} %pad_maximum_fusion.1), channel_id=1, source_target_pairs={{0,4},{4,0},{8,12},{12,8},{1,5},{5,1},{9,13},{13,9},{2,6},{6,2},{1... | collective-permute-start | bytes 589832 | tf_op jit(solution)/shard_map/ppermute | solution.py:373
  136.3 18.1 %collective-permute-start.32 = (bf16[384,256]{1,0:T(8,128)(2,1)S(1)}, bf16[384,256]{1,0:T(8,128)(2,1)S(1)}, u32[]{:S(2)}, u32[]{:S(2)}) collective-permute-start(bf16[384,256]{1,0:T(8,128)(2,1)S(1)} %pad_maximum_fusion.1), channel_id=1, source_target_pairs={{0,8},{4,12},{8,0},{12,4},{1,9},{5,13},{9,1},{13,5},{2,10},{6,14},... | collective-permute-start | bytes 589832 | tf_op jit(solution)/shard_map/ppermute | solution.py:373
  137.9 17.0 %collective-permute-start.31 = (bf16[384,256]{1,0:T(8,128)(2,1)S(1)}, bf16[384,256]{1,0:T(8,128)(2,1)S(1)}, u32[]{:S(2)}, u32[]{:S(2)}) collective-permute-start(bf16[384,256]{1,0:T(8,128)(2,1)S(1)} %pad_maximum_fusion.1), channel_id=1, source_target_pairs={{0,12},{4,8},{8,4},{12,0},{1,13},{5,9},{9,5},{13,1},{2,14},{6,10},... | collective-permute-start | bytes 589832 | tf_op jit(solution)/shard_map/ppermute | solution.py:373
  140.2 5.0 %collective-permute-start.38 = (bf16[256,256]{1,0:T(8,128)(2,1)S(1)}, bf16[256,256]{1,0:T(8,128)(2,1)S(1)}, u32[]{:S(2)}, u32[]{:S(2)}) collective-permute-start(bf16[256,256]{1,0:T(8,128)(2,1)S(1)} %slice.28), channel_id=1, source_target_pairs={{0,129},{1,128},{128,1},{129,0},{2,131},{3,130},{130,3},{131,2},{4... | collective-permute-start | bytes 393224 | tf_op jit(solution)/shard_map/ppermute | solution.py:46
  141.7 13.3 %collective-permute-start.40 = (bf16[256,256]{1,0:T(8,128)(2,1)S(1)}, bf16[256,256]{1,0:T(8,128)(2,1)S(1)}, u32[]{:S(2)}, u32[]{:S(2)}) collective-permute-start(bf16[256,256]{1,0:T(8,128)(2,1)S(1)} %slice.28), channel_id=1, source_target_pairs={{0,1},{1,0},{128,129},{129,128},{2,3},{3,2},{130,131},{131,130},{4... | collective-permute-start | bytes 393224 | tf_op jit(solution)/shard_map/ppermute | solution.py:46
  145.2 10.8 %collective-permute-start.37 = (bf16[384,256]{1,0:T(8,128)(2,1)S(1)}, bf16[384,256]{1,0:T(8,128)(2,1)S(1)}, u32[]{:S(2)}, u32[]{:S(2)}) collective-permute-start(bf16[384,256]{1,0:T(8,128)(2,1)S(1)} %pad_maximum_fusion.1), channel_id=1, source_target_pairs={{0,2},{2,0},{1,3},{3,1},{4,6},{6,4},{5,7},{7,5},{8,10},{10,8},{9,1... | collective-permute-start | bytes 589832 | tf_op jit(solution)/shard_map/ppermute | solution.py:374
  154.4 1.7 %collective-permute-start.36 = (bf16[384,256]{1,0:T(8,128)(2,1)S(1)}, bf16[384,256]{1,0:T(8,128)(2,1)S(1)}, u32[]{:S(2)}, u32[]{:S(2)}) collective-permute-start(bf16[384,256]{1,0:T(8,128)(2,1)S(1)} %collective-permute-done.33), channel_id=1, source_target_pairs={{0,2},{2,0},{1,3},{3,1},{4,6},{6,4},{5,7},{7,5},{8,10},{10,8},{9,1... | collective-permute-start | bytes 589832 | tf_op jit(solution)/shard_map/ppermute | solution.py:374
  154.4 1.7 %collective-permute-start.35 = (bf16[384,256]{1,0:T(8,128)(2,1)S(1)}, bf16[384,256]{1,0:T(8,128)(2,1)S(1)}, u32[]{:S(2)}, u32[]{:S(2)}) collective-permute-start(bf16[384,256]{1,0:T(8,128)(2,1)S(1)} %collective-permute-done.32), channel_id=1, source_target_pairs={{0,2},{2,0},{1,3},{3,1},{4,6},{6,4},{5,7},{7,5},{8,10},{10,8},{9,1... | collective-permute-start | bytes 589832 | tf_op jit(solution)/shard_map/ppermute | solution.py:374
  154.9 1.5 collective-permute-start.34

commit v4 on v3

--- a/solution.py
+++ b/solution.py
@@ -78,10 +78,10 @@
 ):
     n_xh, n_z, n_y, n_c, n_dp = dims
     n_x = n_xh * n_dp
-    n_parts = n_xh * n_y * n_c
+    n_parts = n_y * n_c
     parts = refs[:n_parts]
-    w_sp, w_t, w_q, w_k, w_v, w_o, up_ref = refs[n_parts : n_parts + 7]
-    outs = refs[n_parts + 7 : n_parts + 7 + 2 * n_y + n_x]
+    packed = refs[n_parts]
+    outs = refs[n_parts + 1 : n_parts + 1 + 2 * n_y + n_x]
     send_refs, keep_refs, head_refs = outs[:n_y], outs[n_y : 2 * n_y], outs[2 * n_y :]
     (
         cols,
@@ -100,16 +100,21 @@
         g_ref,
         att_ref,
         gq_ref,
-    ) = refs[n_parts + 7 + 2 * n_y + n_x :]
+    ) = refs[n_parts + 1 + 2 * n_y + n_x :]
+    tokens, ch = feat.shape
+    local = q_ref.shape[0]
+    rows = [9 * ch, 3 * ch, ch, ch, ch, q_ref.shape[1], local]
+    starts = [sum(rows[:k]) for k in range(len(rows))]
+    w_sp, w_t, w_q, w_k, w_v, w_o, up_ref = [
+        packed.at[pl.ds(a, n)] for a, n in zip(starts, rows)
+    ]
     my_xh, my_y, my_c, my_x = pos[0], pos[1], pos[2], pos[4]
-    first = pl.multiple_of(pos[3], up_ref.shape[0])
-    tokens, ch = feat.shape
-    local = up_ref.shape[0]
-    half = parts[0].shape[1]
+    first = pl.multiple_of(pos[3], local)
+    half = parts[0].shape[2]
     scale = HD ** (-0.5)
     n_head = n_y * n_c
-    own_ids = jnp.broadcast_to(ids_ref[:, pl.ds(first, local)].astype(F32), (SIDE, local))
-    own_ids = jnp.transpose(own_ids)[:, 0:1].astype(jnp.int32)
+    own_ids = jnp.broadcast_to(ids_ref[:, pl.ds(first, local)], (SIDE, local))
+    own_ids = jnp.transpose(own_ids)[:, 0:1]
 
     @pl.loop(0, n_z)
     def _(z):
@@ -118,7 +123,7 @@
                 for t in range(n_c):
                     frame = ((my_xh ^ u) * n_z + z) * n_y + (my_y ^ s)
                     row = pl.multiple_of(frame * FRAME + (my_c ^ t) * half, half)
-                    low = parts[(u * n_y + s) * n_c + t][z]
+                    low = parts[s * n_c + t][u, z]
                     wide = low.astype(F32)
                     cols[pl.ds(row, half), 0:ch] = roll_cols(wide, -1).astype(BF)
                     cols[pl.ds(row, half), ch : 2 * ch] = low
@@ -166,7 +171,7 @@
     q_ref[...] = dot(feat[pl.ds(first, local), :], w_q[...]).astype(BF)
     g_ref[...] = dot_t(up_ref[...], w_o[...]).astype(BF)
 
-    chunk = min(tokens, 2048)
+    chunk = min(tokens, 4096)
     n_chunk = tokens // chunk
     def fold(block, join):
         out = block[:, 0:HD]
@@ -215,7 +220,7 @@
         gq = lax.fori_loop(0, n_chunk, backward, zero)
         gq_ref[:, sel] = (gq * scale).astype(BF)
 
-    chunk = min(tokens, 1024)
+    chunk = min(tokens, 2048)
     n_chunk = tokens // chunk
     @pl.loop(0, n_chunk)
     def _(i):
@@ -276,7 +281,9 @@
     wide = weights[2].shape[1]
     block = 12 * ch // (n_c * n_y)
     vm = pl.BlockSpec(memory_space=pltpu.VMEM)
-    n_in = 1 + len(parts) + len(weights) + 1
+    packed = jnp.concatenate([*weights, up])
+    ids = ids.astype(F32)
+    n_in = 2 + len(parts)
     shapes = [(block, ch)] * (2 * n_y) + [(4 * ch // n_x, ch)] * n_x
     out = pl.pallas_call(
         functools.partial(local_kernel, sizes),
@@ -302,12 +309,52 @@
             pltpu.VMEM((local, wide), BF),
             pltpu.VMEM((local, wide), BF),
         ],
-        compiler_params=pltpu.CompilerParams(vmem_limit_bytes=58 * 2**20),
+        compiler_params=pltpu.CompilerParams(vmem_limit_bytes=42 * 2**20),
         cost_estimate=pl.CostEstimate(
             flops=24 * 10**9, transcendentals=2 * local * tokens, bytes_accessed=12 * 2**20
         ),
-    )(pos, ids, *parts, *weights, up)
+    )(pos, ids, *parts, packed)
     return out[:n_y], out[n_y : 2 * n_y], out[2 * n_y :]
+
+
+def place_kernel(pos, *refs):
+    *blocks, first_ref, second_ref = refs
+    n_y = len(blocks) // 2
+    rows = blocks[0].shape[0]
+    n_first = first_ref.shape[0] // rows
+    for k, ref in enumerate(blocks):
+        which = pos[2] if k < n_y else 1 - pos[2]
+        at = which * n_y + (pos[1] ^ (k % n_y))
+
+        @pl.when(at < n_first)
+        def _():
+            row = pl.multiple_of(at * rows, rows)
+            first_ref[pl.ds(row, rows), :] = ref[...].astype(F32)
+
+        @pl.when(at >= n_first)
+        def _():
+            row = pl.multiple_of((at - n_first) * rows, rows)
+            second_ref[pl.ds(row, rows), :] = ref[...].astype(F32)
+
+
+def place(pos, pieces, others, n_first):
+    rows, ch = pieces[0].shape
+    total = rows * 2 * len(pieces)
+    vm = pl.BlockSpec(memory_space=pltpu.VMEM)
+    return pl.pallas_call(
+        place_kernel,
+        name="place",
+        out_shape=(
+            jax.ShapeDtypeStruct((n_first, ch), F32),
+            jax.ShapeDtypeStruct((total - n_first, ch), F32),
+        ),
+        in_specs=[pl.BlockSpec(memory_space=pltpu.SMEM)] + [vm] * (2 * len(pieces)),
+        out_specs=(vm, vm),
+        compiler_params=pltpu.CompilerParams(vmem_limit_bytes=16 * 2**20),
+        cost_estimate=pl.CostEstimate(
+            flops=0, transcendentals=0, bytes_accessed=6 * total * ch
+        ),
+    )(pos, *pieces, *others)
 
 
 def on_device(sizes, clip, block_ids, w_spatial, w_temporal, w_query, w_key, w_value, w_out, cotangent):
@@ -325,12 +372,11 @@
     piece = local // n_head
     mine = lax.dynamic_slice_in_dim(own_clip, lax.axis_index(("y", "c")) * piece, piece)
     part = spread(mine, "z", n_z)
+    part = jnp.stack([part, lax.ppermute(part, "xh", xor_perm(n_xh, 1))])
     parts = []
-    for u in range(n_xh):
-        held = part if u == 0 else lax.ppermute(part, "xh", xor_perm(n_xh, u))
-        for s in range(n_y):
-            block = held if s == 0 else lax.ppermute(held, "y", xor_perm(n_y, s))
-            parts += [block, lax.ppermute(block, "c", xor_perm(n_c, 1))]
+    for s in range(n_y):
+        block = part if s == 0 else lax.ppermute(part, "y", xor_perm(n_y, s))
+        parts += [block, lax.ppermute(block, "c", xor_perm(n_c, 1))]
 
     first = lax.axis_index(("xh", "z")) * local
     pos = jnp.stack([i_xh, i_y, i_c, first, i_x]).astype(jnp.int32)
@@ -367,21 +413,13 @@
     done = (jnp.sum(got.astype(F32), axis=0) * factor).astype(BF)
 
     done = spread(done, "z", n_z).reshape(n_z * rows, ch)
-    piece = jnp.concatenate(gather_xor(done[:cut], x_axes, n_x, i_x))
-    own_head, piece = lax.optimization_barrier((done[cut:], piece))
-    g_heads = [part.astype(F32) for part in gather_xor(own_head, x_axes, n_x, i_x)]
+    done = gather_xor(done, x_axes, n_x, i_x)
+    g_heads = [part[cut:].astype(F32) for part in done]
+    piece = jnp.concatenate([part[:cut] for part in done])
     pieces = [piece] + [lax.ppermute(piece, "y", xor_perm(n_y, s)) for s in range(1, n_y)]
     others = [lax.ppermute(p, "c", xor_perm(n_c, 1)) for p in pieces]
-    pieces, others = unxor(pieces, i_y), unxor(others, i_y)
-    halves = []
-    for c in range(n_c):
-        halves += [jnp.where(i_c == c, p, o).astype(F32) for p, o in zip(pieces, others)]
-    n_ws = 9 * ch // halves[0].shape[0]
-    return (
-        jnp.concatenate(halves[:n_ws]).reshape(9, ch, ch),
-        jnp.concatenate(halves[n_ws:]).reshape(3, ch, ch),
-        *g_heads,
-    )
+    g_ws, g_wt = place(pos, pieces, others, 9 * ch)
+    return (g_ws.reshape(9, ch, ch), g_wt.reshape(3, ch, ch), *g_heads)
 
 
 def solution(mesh):

time: 160 us -> 158 us (0.988)
  starting transfers between devices: 49.2 us -> 56.1 us
  waiting for transfers between devices: 21.3 us -> 16.6 us
  other arithmetic: 6.75 us -> 2.18 us
    ppermute x8 -> x4, starting transfers between devices: 8.64 us -> 14.5 us  [on_device(): parts += [block, lax.ppermute(block, 'c', xor_perm(n_c, 1))]]
    ppermute x4, starting transfers between devices: 9.79 us -> 13.9 us  [on_device(): others = [lax.ppermute(p, 'c', xor_perm(n_c, 1)) for p in pieces]]
    pallas_call x1, Pallas kernels: 40.6 us -> 36.8 us  [local_terms(): pl.pallas_call(functools.partial(local_kernel, sizes), name='local_terms'...]
    ppermute x7 -> x4, waiting for transfers between devices: 5.83 us -> 2.1 us  [the longest x1 1.14 us: on_device(): part = jnp.stack([part, lax.ppermute(part, 'xh', xor_perm(n_xh, 1))])]
    ppermute x7 -> x4, starting transfers between devices: 9.71 us -> 6.75 us  [the longest x3 4.01 us: on_device(): block = part if s == 0 else lax.ppermute(part, 'y', xor_perm(n_y, s))]
    ppermute x6 -> x3, starting transfers between devices: 6.4 us -> 3.59 us  [gather_xor(): lax.ppermute(block, axis, xor_perm(count, s))]
    reshape x2 -> x0, other arithmetic: 2.57 us -> none  [the longest x1 1.63 us: on_device(): jnp.concatenate(halves[:n_ws]).reshape(9, ch, ch)]
    pallas_call x0 -> x1, Pallas kernels: none -> 2.51 us  [place(): pl.pallas_call(place_kernel, name='place', out_shape=(jax.ShapeDtypeStruc...]
  transfers between devices with their start and end apart: 41 -> 31, of which waited for: 14 -> 13; matrix products, arithmetic and copies ran while one was open for 2% -> 3% of each run, Pallas kernels for 0% -> 0%
where the time goes in v4:
time: 158 us; the launch traced here: 157 us
  starting transfers between devices  56.1 us (36%)
  Pallas kernels  39.3 us (25%)
  blocking collectives  38.8 us (25%)
  waiting for transfers between devices  16.6 us (11%)
  local copies, waits for them, and re-layouts  3.5 us (2%)
  other arithmetic  2.18 us (1%)
    pallas_call x1, Pallas kernels, local_terms(): pl.pallas_call(functools.partial(local_kernel, sizes), name='local_terms'...  36.8 us
    all_to_all x2, blocking collectives, spread(): lax.all_to_all(jnp.broadcast_to(block[None], (count,) + block.shape), axi...  27.7 us
    ppermute x4, starting transfers between devices, on_device(): parts += [block, lax.ppermute(block, 'c', xor_perm(n_c, 1))]  14.5 us
    ppermute x4, starting transfers between devices, on_device(): others = [lax.ppermute(p, 'c', xor_perm(n_c, 1)) for p in pieces]  13.9 us
    all_to_all x1, blocking collectives, on_device(): got = lax.all_to_all(block.astype(BF).reshape(n_z, rows, ch), 'z', 0, 0)  11.1 us
    ppermute x3, waiting for transfers between devices, gather_xor(): lax.ppermute(block, axis, xor_perm(count, s))  4.81 us
    ppermute x3, starting transfers between devices, on_device(): lax.ppermute(heads[r], x_axes, xor_perm(n_x, r)).astype(F32)  4.44 us
    ppermute x3, waiting for transfers between devices, on_device(): got = lax.ppermute(low[r * cut:(r + 1) * cut], x_axes, xor_perm(n_x, r))  4.35 us
  transfers between devices with their start and end apart: 31, of which 13 were waited for; matrix products, arithmetic and copies ran while one was open for 3% of the time, Pallas kernels for 0%

profile of v4, /device:TPU:1, one launch (start us, length us, event | category | flops | bytes accessed | tf_op | source)
XLA Modules:
  0.0 157.4 jit_solution(2619864754258005845)
XLA Ops:
  0.6 0.0 copy-start
  0.7 0.9 copy-done
  1.6 0.0 copy-start.4
  1.6 16.7 %all_to_all.15 = bf16[8,32,256]{2,1,0:T(8,128)(2,1)S(1)} all-to-all(bf16[8,32,256]{2,1,0:T(8,128)(2,1)S(1)} %broadcast_in_dim.7), channel_id=1, replica_groups=mesh['xh'=2,'z'=8,'y'=4,'c'=2,'dp'=2] {'z'}, dimensions={0} | all-to-all | bytes 262144 | tf_op jit(solution)/shard_map/all_to_all | solution.py:51
  18.3 2.7 %collective-permute-start = (bf16[8,32,256]{2,1,0:T(8,128)(2,1)S(1)}, bf16[8,32,256]{2,1,0:T(8,128)(2,1)S(1)}, u32[]{:S(2)}, u32[]{:S(2)}) collective-permute-start(bf16[8,32,256]{2,1,0:T(8,128)(2,1)S(1)} %all_to_all.15), channel_id=1, source_target_pairs={{0,128},{128,0},{1,129},{129,1},{2,130},{130,2},{3,131},{131,3},{4... | collective-permute-start | bytes 393224 | tf_op jit(solution)/shard_map/ppermute | solution.py:375
  21.0 1.4 constant_dynamic-update-slice_fusion.5
  22.5 1.1 collective-permute-done
  23.6 1.4 collective-permute-start.2
  25.0 2.6 %collective-permute-start.4 = (bf16[2,8,32,256]{3,2,1,0:T(8,128)(2,1)S(1)}, bf16[2,8,32,256]{3,2,1,0:T(8,128)(2,1)S(1)}, u32[]{:S(2)}, u32[]{:S(2)}) collective-permute-start(bf16[2,8,32,256]{3,2,1,0:T(8,128)(2,1)S(1)} %pad_maximum_fusion.refs_0_), channel_id=1, source_target_pairs={{0,8},{4,12},{8,0},{12,4},{1,9},{5,13},{9,1},{13,5},{2,10},{6,14},... | collective-permute-start | bytes 786440 | tf_op jit(solution)/shard_map/ppermute | solution.py:378
  27.6 0.0 collective-permute-start.6
  27.7 4.3 %collective-permute-start.1 = (bf16[2,8,32,256]{3,2,1,0:T(8,128)(2,1)S(1)}, bf16[2,8,32,256]{3,2,1,0:T(8,128)(2,1)}, u32[]{:S(2)}, u32[]{:S(2)}) collective-permute-start(bf16[2,8,32,256]{3,2,1,0:T(8,128)(2,1)S(1)} %pad_maximum_fusion.refs_0_), channel_id=1, source_target_pairs={{0,2},{2,0},{1,3},{3,1},{4,6},{6,4},{5,7},{7,5},{8,10},{10,8},{9,1... | collective-permute-start | bytes 786440 | tf_op jit(solution)/shard_map/ppermute | solution.py:379
  32.0 0.0 collective-permute-done.2.refs_2_
  32.0 3.3 %collective-permute-start.3 = (bf16[2,8,32,256]{3,2,1,0:T(8,128)(2,1)S(1)}, bf16[2,8,32,256]{3,2,1,0:T(8,128)(2,1)}, u32[]{:S(2)}, u32[]{:S(2)}) collective-permute-start(bf16[2,8,32,256]{3,2,1,0:T(8,128)(2,1)S(1)} %collective-permute-done.2.refs_2_), channel_id=1, source_target_pairs={{0,2},{2,0},{1,3},{3,1},{4,6},{6,4},{5,7},{7,5},{8,10},{10,8},{9,1... | collective-permute-start | bytes 786440 | tf_op jit(solution)/shard_map/ppermute | solution.py:379
  35.3 0.7 collective-permute-done.4.refs_4_
  36.0 4.7 %collective-permute-start.5 = (bf16[2,8,32,256]{3,2,1,0:T(8,128)(2,1)S(1)}, bf16[2,8,32,256]{3,2,1,0:T(8,128)(2,1)}, u32[]{:S(2)}, u32[]{:S(2)}) collective-permute-start(bf16[2,8,32,256]{3,2,1,0:T(8,128)(2,1)S(1)} %collective-permute-done.4.refs_4_), channel_id=1, source_target_pairs={{0,2},{2,0},{1,3},{3,1},{4,6},{6,4},{5,7},{7,5},{8,10},{10,8},{9,1... | collective-permute-start | bytes 786440 | tf_op jit(solution)/shard_map/ppermute | solution.py:379
  40.7 0.3 collective-permute-done.6.refs_6_
  41.0 2.2 %collective-permute-start.7 = (bf16[2,8,32,256]{3,2,1,0:T(8,128)(2,1)S(1)}, bf16[2,8,32,256]{3,2,1,0:T(8,128)(2,1)}, u32[]{:S(2)}, u32[]{:S(2)}) collective-permute-start(bf16[2,8,32,256]{3,2,1,0:T(8,128)(2,1)S(1)} %collective-permute-done.6.refs_6_), channel_id=1, source_target_pairs={{0,2},{2,0},{1,3},{3,1},{4,6},{6,4},{5,7},{7,5},{8,10},{10,8},{9,1... | collective-permute-start | bytes 786440 | tf_op jit(solution)/shard_map/ppermute | solution.py:379
  43.3 0.1 stack.32.pos
  43.3 0.9 bitcast_dynamic-update-slice_fusion.refs_8_
  44.3 0.0 collective-permute-done.1.refs_1_
  44.3 0.0 collective-permute-done.3.refs_3_
  44.3 0.2 collective-permute-done.7.refs_7_
  44.5 36.8 %local_terms.1 = (bf16[384,256]{1,0:T(8,128)(2,1)S(1)}, bf16[384,256]{1,0:T(8,128)(2,1)S(1)}, bf16[384,256]{1,0:T(8,128)(2,1)S(1)}, bf16[384,256]{1,0:T(8,128)(2...) custom-call(s32[5]{0:T(128)S(1)} %stack.32.pos, ...), custom_call_target="tpu_custom_call" | custom-call | flops 24000000000 | bytes 12582912 | tf_op jit(solution)/shard_map/local_terms/pallas_call | solution.py:288
  81.3 0.5 collective-permute-start.9
  81.7 0.1 collective-permute-start.11
  81.9 0.4 collective-permute-start.13
  82.2 0.1 collective-permute-start.8
  82.4 0.4 collective-permute-done.9
  82.8 0.1 collective-permute-start.10
  82.9 0.2 collective-permute-done.11
  83.2 1.0 collective-permute-start.12
  84.3 0.0 collective-permute-done.13
  84.3 2.8 %collective-permute-start.14 = (bf16[384,256]{1,0:T(8,128)(2,1)S(1)}, bf16[384,256]{1,0:T(8,128)(2,1)S(1)}, u32[]{:S(2)}, u32[]{:S(2)}) collective-permute-start(bf16[384,256]{1,0:T(8,128)(2,1)S(1)} %add_convert_fusion), channel_id=1, source_target_pairs={{0,12},{4,8},{8,4},{12,0},{1,13},{5,9},{9,5},{13,1},{2,14},{6,10},... | collective-permute-start | bytes 589832 | tf_op jit(solution)/shard_map/ppermute | solution.py:399
  87.1 1.2 collective-permute-start.18
  88.3 2.4 %collective-permute-start.19 = (bf16[256,256]{1,0:T(8,128)(2,1)S(1)}, bf16[256,256]{1,0:T(8,128)(2,1)S(1)}, u32[]{:S(2)}, u32[]{:S(2)}) collective-permute-start(bf16[256,256]{1,0:T(8,128)(2,1)S(1)} %get-tuple-element.30), channel_id=1, source_target_pairs={{0,128},{1,129},{128,0},{129,1},{2,130},{3,131},{130,2},{131,3},{4... | collective-permute-start | bytes 393224 | tf_op jit(solution)/shard_map/ppermute | solution.py:402
  90.7 0.8 collective-permute-start.20
  91.5 1.5 collective-permute-done.12
  93.0 2.7 %collective-permute-done.14 = bf16[384,256]{1,0:T(8,128)(2,1)S(1)} collective-permute-done((bf16[384,256]{1,0:T(8,128)(2,1)S(1)}, bf16[384,256]{1,0:T(8,128)(2,1)S(1)}, u32[]{:S(2)}, u32[]{:S(2)}) %collective-permute-start.14) | collective-permute-done | bytes 196640 | tf_op jit(solution)/shard_map/ppermute | solution.py:399
  95.8 0.1 fusion.3
  95.9 1.3 collective-permute-start.15
  97.2 2.4 %collective-permute-start.16 = (bf16[96,256]{1,0:T(8,128)(2,1)S(1)}, bf16[96,256]{1,0:T(8,128)(2,1)S(1)}, u32[]{:S(2)}, u32[]{:S(2)}) collective-permute-start(bf16[96,256]{1,0:T(8,128)(2,1)S(1)} %get-tuple-element.42), channel_id=1, source_target_pairs={{0,128},{1,129},{128,0},{129,1},{2,130},{3,131},{130,2},{131,3},{4... | collective-permute-start | bytes 147464 | tf_op jit(solution)/shard_map/ppermute | solution.py:407
  99.7 0.2 collective-permute-start.17
  99.9 0.1 add_convert_fusion.3
  100.0 1.7 %collective-permute-done.16 = bf16[96,256]{1,0:T(8,128)(2,1)S(1)} collective-permute-done((bf16[96,256]{1,0:T(8,128)(2,1)S(1)}, bf16[96,256]{1,0:T(8,128)(2,1)S(1)}, u32[]{:S(2)}, u32[]{:S(2)}) %collective-permute-start.16) | collective-permute-done | bytes 49184 | tf_op jit(solution)/shard_map/ppermute | solution.py:407
  101.7 2.6 %collective-permute-done.17 = bf16[96,256]{1,0:T(8,128)(2,1)S(1)} collective-permute-done((bf16[96,256]{1,0:T(8,128)(2,1)S(1)}, bf16[96,256]{1,0:T(8,128)(2,1)S(1)}, u32[]{:S(2)}, u32[]{:S(2)}) %collective-permute-start.17) | collective-permute-done | bytes 49184 | tf_op jit(solution)/shard_map/ppermute | solution.py:407
  104.4 11.1 %all_to_all.16 = bf16[8,44,256]{2,1,0:T(8,128)(2,1)S(1)} all-to-all(bf16[8,44,256]{2,1,0:T(8,128)(2,1)S(1)} %convert_element_type.119), channel_id=1, replica_groups=mesh['xh'=2,'z'=8,'y'=4,'c'=2,'dp'=2] {'z'}, dimensions={0} | all-to-all | bytes 360448 | tf_op jit(solution)/shard_map/all_to_all | solution.py:411
  115.5 11.0 %all_to_all.17 = bf16[8,44,256]{2,1,0:T(8,128)(2,1)S(1)} all-to-all(bf16[8,44,256]{2,1,0:T(8,128)(2,1)S(1)} %broadcast_in_dim.16), channel_id=1, replica_groups=mesh['xh'=2,'z'=8,'y'=4,'c'=2,'dp'=2] {'z'}, dimensions={0} | all-to-all | bytes 360448 | tf_op jit(solution)/shard_map/all_to_all | solution.py:51
  126.6 0.4 collective-permute-start.21
  127.0 0.1 collective-permute-start.22
  127.1 3.1 %collective-permute-start.23 = (bf16[352,256]{1,0:T(8,128)(2,1)S(1)}, bf16[352,256]{1,0:T(8,128)(2,1)S(1)}, u32[]{:S(2)}, u32[]{:S(2)}) collective-permute-start(bf16[352,256]{1,0:T(8,128)(2,1)S(1)} %reshape.38), channel_id=1, source_target_pairs={{0,1},{1,0},{128,129},{129,128},{2,3},{3,2},{130,131},{131,130},{4... | collective-permute-start | bytes 540680 | tf_op jit(solution)/shard_map/ppermute | solution.py:46
  130.2 4.2 %collective-permute-done.21 = bf16[352,256]{1,0:T(8,128)(2,1)S(1)} collective-permute-done((bf16[352,256]{1,0:T(8,128)(2,1)S(1)}, bf16[352,256]{1,0:T(8,128)(2,1)S(1)}, u32[]{:S(2)}, u32[]{:S(2)}) %collective-permute-start.21) | collective-permute-done | bytes 180256 | tf_op jit(solution)/shard_map/ppermute | solution.py:46
  134.4 0.6 collective-permute-done.23
  135.0 0.1 broadcast_select_fusion.7
  135.1 0.1 collective-permute-start.24
  135.2 3.8 %collective-permute-start.25 = (bf16[384,256]{1,0:T(8,128)(2,1)S(1)}, bf16[384,256]{1,0:T(8,128)(2,1)S(1)}, u32[]{:S(2)}, u32[]{:S(2)}) collective-permute-start(bf16[384,256]{1,0:T(8,128)(2,1)S(1)} %pad_maximum_fusion.1.refs_0_), channel_id=1, source_target_pairs={{0,8},{4,12},{8,0},{12,4},{1,9},{5,13},{9,1},{13,5},{2,10},{6,14},... | collective-permute-start | bytes 589832 | tf_op jit(solution)/shard_map/ppermute | solution.py:419
  139.1 0.0 collective-permute-start.26
  139.1 7.1 %collective-permute-start.27 = (bf16[384,256]{1,0:T(8,128)(2,1)S(1)}, bf16[384,256]{1,0:T(8,128)(2,1)S(1)}, u32[]{:S(2)}, u32[]{:S(2)}) collective-permute-start(bf16[384,256]{1,0:T(8,128)(2,1)S(1)} %pad_maximum_fusion.1.refs_0_), channel_id=1, source_target_pairs={{0,2},{2,0},{1,3},{3,1},{4,6},{6,4},{5,7},{7,5},{8,10},{10,8},{9,1... | collective-permute-start | bytes 589832 | tf_op jit(solution)/shard_map/ppermute | solution.py:420
  146.2 0.8 slice_convert_fusion
  147.1 0.1 collective-permute-start.28
  147.2 4.6 %collective-permute-start.29 = (bf16[384,256]{1,0:T(8,128)(2,1)S(1)}, bf16[384,256]{1,0:T(8,128)(2,1)S(1)}, u32[]{:S(2)}, u32[]{:S(2)}) collective-permute-start(bf16[384,256]{1,0:T(8,128)(2,1)S(1)} %collective-permute-done.25.refs_2_), channel_id=1, source_target_pairs={{0,2},{2,0},{1,3},{3,1},{4,6},{6,4},{5,7},{7,5},{8,10},{10,8},{9,1... | collective-permute-start | bytes 589832 | tf_op jit(solution)/shard_map/ppermute | solution.py:420
  151.8 2.0 %collective-permute-start.30 = (bf16[384,256]{1,0:T(8,128)(2,1)S(1)}, bf16[384,256]{1,0:T(8,128)(2,1)S(1)}, u32[]{:S(2)}, u32[]{:S(2)}) collective-permute-start(bf16[384,256]{1,0:T(8,128)(2,1)S(1)} %collective-permute-done.26.refs_3_), channel_id=1, source_target_pairs={{0,2},{2,0},{1,3},{3,1},{4,6},{6,4},{5,7},{7,5},{8,10},{10,8},{9,1... | collective-permute-start | bytes 589832 | tf_op jit(solution)/shard_map/ppermute | solution.py:420
  153.8 0.8 slice_convert_fusion.2
  154.6 0.2 collective-permute-done.30.refs_7_
  154.9 2.5 %place.1 = (f32[2304,256]{1,0:T(8,128)}, f32[768,256]{1,0:T(8,128)}) custom-call(s32[5]{0:T(128)S(1)} %stack.32.pos, bf16[384,256]{1,0:T(8,128)(2,1)S(1)} %pad_maximum_fusion.1.refs_0_, bf16[384,256]{1,0:T(8,128)(2,1)S(1)} %collective-permute-done.24.refs_1_, bf16[384,256]{1,0:T(8,128)(2,1)S(1)} %collective-permute-done.25.refs_2_, ...), custom_call_target="tpu_custom_call" | custom-call | bytes 4718592 | tf_op jit(solution)/shard_map/place/pallas_call | solution.py:344
  (50 shorter events, 0.5 us)
Async XLA Ops:
  0.6 0.9 copy-start
  0.6 21.8 %copy-start.1 = (bf16[3,256,256]{2,1,0:T(8,128)(2,1)S(1)}, bf16[3,256,256]{2,1,0:T(8,128)(2,1)}, u32[]{:S(2)}) copy-start(bf16[3,256,256]{2,1,0:T(8,128)(2,1)} %param.12) | copy-start | bytes 1179652
  1.5 26.1 %copy-start.2 = (bf16[256,256]{1,0:T(8,128)(2,1)S(1)}, bf16[256,256]{1,0:T(8,128)(2,1)}, u32[]{:S(2)}) copy-start(bf16[256,256]{1,0:T(8,128)(2,1)} %param.13) | copy-start | bytes 393220
  1.5 26.1 %copy-start.3 = (bf16[256,256]{1,0:T(8,128)(2,1)S(1)}, bf16[256,256]{1,0:T(8,128)(2,1)}, u32[]{:S(2)}) copy-start(bf16[256,256]{1,0:T(8,128)(2,1)} %param.14) | copy-start | bytes 393220
  1.6 26.1 %copy-start.4 = (bf16[256,256]{1,0:T(8,128)(2,1)S(1)}, bf16[256,256]{1,0:T(8,128)(2,1)}, u32[]{:S(2)}) copy-start(bf16[256,256]{1,0:T(8,128)(2,1)} %param.15) | copy-start | bytes 393220
  18.3 5.3 %collective-permute-start = (bf16[8,32,256]{2,1,0:T(8,128)(2,1)S(1)}, bf16[8,32,256]{2,1,0:T(8,128)(2,1)S(1)}, u32[]{:S(2)}, u32[]{:S(2)}) collective-permute-start(bf16[8,32,256]{2,1,0:T(8,128)(2,1)S(1)} %all_to_all.15), channel_id=1, source_target_pairs={{0,128},{128,0},{1,129},{129,1},{2,130},{130,2},{3,131},{131,3},{4... | collective-permute-start | bytes 393224 | tf_op jit(solution)/shard_map/ppermute | solution.py:375
  21.0 22.2 %copy-start.5 = (bf16[256,256]{1,0:T(8,128)(2,1)S(1)}, bf16[256,256]{1,0:T(8,128)(2,1)}, u32[]{:S(2)}) copy-start(bf16[256,256]{1,0:T(8,128)(2,1)} %param.16) | copy-start | bytes 393220
  21.0 22.2 %copy-start.6 = (s32[1,4096]{1,0:T(1,128)S(1)}, s32[1,4096]{1,0:T(1,128)}, u32[]{:S(2)}) copy-start(s32[1,4096]{1,0:T(1,128)} %param.10) | copy-start | bytes 49156
  23.6 8.4 %collective-permute-start.2 = (bf16[2,8,32,256]{3,2,1,0:T(8,128)(2,1)S(1)}, bf16[2,8,32,256]{3,2,1,0:T(8,128)(2,1)S(1)}, u32[]{:S(2)}, u32[]{:S(2)}) collective-permute-start(bf16[2,8,32,256]{3,2,1,0:T(8,128)(2,1)S(1)} %pad_maximum_fusion.refs_0_), channel_id=1, source_target_pairs={{0,4},{4,0},{8,12},{12,8},{1,5},{5,1},{9,13},{13,9},{2,6},{6,2},{1... | collective-permute-start | bytes 786440 | tf_op jit(solution)/shard_map/ppermute | solution.py:378
  25.0 10.9 %collective-permute-start.4 = (bf16[2,8,32,256]{3,2,1,0:T(8,128)(2,1)S(1)}, bf16[2,8,32,256]{3,2,1,0:T(8,128)(2,1)S(1)}, u32[]{:S(2)}, u32[]{:S(2)}) collective-permute-start(bf16[2,8,32,256]{3,2,1,0:T(8,128)(2,1)S(1)} %pad_maximum_fusion.refs_0_), channel_id=1, source_target_pairs={{0,8},{4,12},{8,0},{12,4},{1,9},{5,13},{9,1},{13,5},{2,10},{6,14},... | collective-permute-start | bytes 786440 | tf_op jit(solution)/shard_map/ppermute | solution.py:378
  27.6 13.3 %collective-permute-start.6 = (bf16[2,8,32,256]{3,2,1,0:T(8,128)(2,1)S(1)}, bf16[2,8,32,256]{3,2,1,0:T(8,128)(2,1)S(1)}, u32[]{:S(2)}, u32[]{:S(2)}) collective-permute-start(bf16[2,8,32,256]{3,2,1,0:T(8,128)(2,1)S(1)} %pad_maximum_fusion.refs_0_), channel_id=1, source_target_pairs={{0,12},{4,8},{8,4},{12,0},{1,13},{5,9},{9,5},{13,1},{2,14},{6,10},... | collective-permute-start | bytes 786440 | tf_op jit(solution)/shard_map/ppermute | solution.py:378
  27.7 16.5 %collective-permute-start.1 = (bf16[2,8,32,256]{3,2,1,0:T(8,128)(2,1)S(1)}, bf16[2,8,32,256]{3,2,1,0:T(8,128)(2,1)}, u32[]{:S(2)}, u32[]{:S(2)}) collective-permute-start(bf16[2,8,32,256]{3,2,1,0:T(8,128)(2,1)S(1)} %pad_maximum_fusion.refs_0_), channel_id=1, source_target_pairs={{0,2},{2,0},{1,3},{3,1},{4,6},{6,4},{5,7},{7,5},{8,10},{10,8},{9,1... | collective-permute-start | bytes 786440 | tf_op jit(solution)/shard_map/ppermute | solution.py:379
  32.0 12.3 %collective-permute-start.3 = (bf16[2,8,32,256]{3,2,1,0:T(8,128)(2,1)S(1)}, bf16[2,8,32,256]{3,2,1,0:T(8,128)(2,1)}, u32[]{:S(2)}, u32[]{:S(2)}) collective-permute-start(bf16[2,8,32,256]{3,2,1,0:T(8,128)(2,1)S(1)} %collective-permute-done.2.refs_2_), channel_id=1, source_target_pairs={{0,2},{2,0},{1,3},{3,1},{4,6},{6,4},{5,7},{7,5},{8,10},{10,8},{9,1... | collective-permute-start | bytes 786440 | tf_op jit(solution)/shard_map/ppermute | solution.py:379
  36.0 8.3 %collective-permute-start.5 = (bf16[2,8,32,256]{3,2,1,0:T(8,128)(2,1)S(1)}, bf16[2,8,32,256]{3,2,1,0:T(8,128)(2,1)}, u32[]{:S(2)}, u32[]{:S(2)}) collective-permute-start(bf16[2,8,32,256]{3,2,1,0:T(8,128)(2,1)S(1)} %collective-permute-done.4.refs_4_), channel_id=1, source_target_pairs={{0,2},{2,0},{1,3},{3,1},{4,6},{6,4},{5,7},{7,5},{8,10},{10,8},{9,1... | collective-permute-start | bytes 786440 | tf_op jit(solution)/shard_map/ppermute | solution.py:379
  41.0 3.5 %collective-permute-start.7 = (bf16[2,8,32,256]{3,2,1,0:T(8,128)(2,1)S(1)}, bf16[2,8,32,256]{3,2,1,0:T(8,128)(2,1)}, u32[]{:S(2)}, u32[]{:S(2)}) collective-permute-start(bf16[2,8,32,256]{3,2,1,0:T(8,128)(2,1)S(1)} %collective-permute-done.6.refs_6_), channel_id=1, source_target_pairs={{0,2},{2,0},{1,3},{3,1},{4,6},{6,4},{5,7},{7,5},{8,10},{10,8},{9,1... | collective-permute-start | bytes 786440 | tf_op jit(solution)/shard_map/ppermute | solution.py:379
  81.3 1.5 collective-permute-start.9
  81.7 1.4 collective-permute-start.11
  81.9 2.4 %collective-permute-start.13 = (bf16[384,256]{1,0:T(8,128)(2,1)S(1)}, bf16[384,256]{1,0:T(8,128)(2,1)S(1)}, u32[]{:S(2)}, u32[]{:S(2)}) collective-permute-start(bf16[384,256]{1,0:T(8,128)(2,1)S(1)} %get-tuple-element.27), channel_id=1, source_target_pairs={{0,2},{2,0},{1,3},{3,1},{4,6},{6,4},{5,7},{7,5},{8,10},{10,8},{9,1... | collective-permute-start | bytes 589832 | tf_op jit(solution)/shard_map/ppermute | solution.py:395
  82.2 6.1 %collective-permute-start.8 = (bf16[384,256]{1,0:T(8,128)(2,1)S(1)}, bf16[384,256]{1,0:T(8,128)(2,1)S(1)}, u32[]{:S(2)}, u32[]{:S(2)}) collective-permute-start(bf16[384,256]{1,0:T(8,128)(2,1)S(1)} %get-tuple-element.21), channel_id=1, source_target_pairs={{0,2},{2,0},{1,3},{3,1},{4,6},{6,4},{5,7},{7,5},{8,10},{10,8},{9,1... | collective-permute-start | bytes 589832 | tf_op jit(solution)/shard_map/ppermute | solution.py:395
  82.8 7.9 %collective-permute-start.10 = (bf16[384,256]{1,0:T(8,128)(2,1)S(1)}, bf16[384,256]{1,0:T(8,128)(2,1)S(1)}, u32[]{:S(2)}, u32[]{:S(2)}) collective-permute-start(bf16[384,256]{1,0:T(8,128)(2,1)S(1)} %add_convert_fusion.2), channel_id=1, source_target_pairs={{0,4},{4,0},{8,12},{12,8},{1,5},{5,1},{9,13},{13,9},{2,6},{6,2},{1... | collective-permute-start | bytes 589832 | tf_op jit(solution)/shard_map/ppermute | solution.py:399
  83.2 9.8 %collective-permute-start.12 = (bf16[384,256]{1,0:T(8,128)(2,1)S(1)}, bf16[384,256]{1,0:T(8,128)(2,1)S(1)}, u32[]{:S(2)}, u32[]{:S(2)}) collective-permute-start(bf16[384,256]{1,0:T(8,128)(2,1)S(1)} %add_convert_fusion.1), channel_id=1, source_target_pairs={{0,8},{4,12},{8,0},{12,4},{1,9},{5,13},{9,1},{13,5},{2,10},{6,14},... | collective-permute-start | bytes 589832 | tf_op jit(solution)/shard_map/ppermute | solution.py:399
  84.3 11.5 %collective-permute-start.14 = (bf16[384,256]{1,0:T(8,128)(2,1)S(1)}, bf16[384,256]{1,0:T(8,128)(2,1)S(1)}, u32[]{:S(2)}, u32[]{:S(2)}) collective-permute-start(bf16[384,256]{1,0:T(8,128)(2,1)S(1)} %add_convert_fusion), channel_id=1, source_target_pairs={{0,12},{4,8},{8,4},{12,0},{1,13},{5,9},{9,5},{13,1},{2,14},{6,10},... | collective-permute-start | bytes 589832 | tf_op jit(solution)/shard_map/ppermute | solution.py:399
  87.1 12.6 %collective-permute-start.18 = (bf16[256,256]{1,0:T(8,128)(2,1)S(1)}, bf16[256,256]{1,0:T(8,128)(2,1)S(1)}, u32[]{:S(2)}, u32[]{:S(2)}) collective-permute-start(bf16[256,256]{1,0:T(8,128)(2,1)S(1)} %get-tuple-element.29), channel_id=1, source_target_pairs={{0,1},{1,0},{128,129},{129,128},{2,3},{3,2},{130,131},{131,130},{4... | collective-permute-start | bytes 393224 | tf_op jit(solution)/shard_map/ppermute | solution.py:402
  88.3 11.6 %collective-permute-start.19 = (bf16[256,256]{1,0:T(8,128)(2,1)S(1)}, bf16[256,256]{1,0:T(8,128)(2,1)S(1)}, u32[]{:S(2)}, u32[]{:S(2)}) collective-permute-start(bf16[256,256]{1,0:T(8,128)(2,1)S(1)} %get-tuple-element.30), channel_id=1, source_target_pairs={{0,128},{1,129},{128,0},{129,1},{2,130},{3,131},{130,2},{131,3},{4... | collective-permute-start | bytes 393224 | tf_op jit(solution)/shard_map/ppermute | solution.py:402
  90.7 9.1 %collective-permute-start.20 = (bf16[256,256]{1,0:T(8,128)(2,1)S(1)}, bf16[256,256]{1,0:T(8,128)(2,1)S(1)}, u32[]{:S(2)}, u32[]{:S(2)}) collective-permute-start(bf16[256,256]{1,0:T(8,128)(2,1)S(1)} %get-tuple-element.31), channel_id=1, source_target_pairs={{0,129},{1,128},{128,1},{129,0},{2,131},{3,130},{130,3},{131,2},{4... | collective-permute-start | bytes 393224 | tf_op jit(solution)/shard_map/ppermute | solution.py:402
  95.9 4.0 %collective-permute-start.15 = (bf16[96,256]{1,0:T(8,128)(2,1)S(1)}, bf16[96,256]{1,0:T(8,128)(2,1)S(1)}, u32[]{:S(2)}, u32[]{:S(2)}) collective-permute-start(bf16[96,256]{1,0:T(8,128)(2,1)S(1)} %get-tuple-element.40), channel_id=1, source_target_pairs={{0,1},{1,0},{128,129},{129,128},{2,3},{3,2},{130,131},{131,130},{4... | collective-permute-start | bytes 147464 | tf_op jit(solution)/shard_map/ppermute | solution.py:407
  97.2 4.4 %collective-permute-start.16 = (bf16[96,256]{1,0:T(8,128)(2,1)S(1)}, bf16[96,256]{1,0:T(8,128)(2,1)S(1)}, u32[]{:S(2)}, u32[]{:S(2)}) collective-permute-start(bf16[96,256]{1,0:T(8,128)(2,1)S(1)} %get-tuple-element.42), channel_id=1, source_target_pairs={{0,128},{1,129},{128,0},{129,1},{2,130},{3,131},{130,2},{131,3},{4... | collective-permute-start | bytes 147464 | tf_op jit(solution)/shard_map/ppermute | solution.py:407
  99.7 4.6 %collective-permute-start.17 = (bf16[96,256]{1,0:T(8,128)(2,1)S(1)}, bf16[96,256]{1,0:T(8,128)(2,1)S(1)}, u32[]{:S(2)}, u32[]{:S(2)}) collective-permute-start(bf16[96,256]{1,0:T(8,128)(2,1)S(1)} %get-tuple-element.41), channel_id=1, source_target_pairs={{0,129},{1,128},{128,1},{129,0},{2,131},{3,130},{130,3},{131,2},{4... | collective-permute-start | bytes 147464 | tf_op jit(solution)/shard_map/ppermute | solution.py:407
  126.6 7.8 %collective-permute-start.21 = (bf16[352,256]{1,0:T(8,128)(2,1)S(1)}, bf16[352,256]{1,0:T(8,128)(2,1)S(1)}, u32[]{:S(2)}, u32[]{:S(2)}) collective-permute-start(bf16[352,256]{1,0:T(8,128)(2,1)S(1)} %reshape.38), channel_id=1, source_target_pairs={{0,129},{1,128},{128,1},{129,0},{2,131},{3,130},{130,3},{131,2},{4... | collective-permute-start | bytes 540680 | tf_op jit(solution)/shard_map/ppermute | solution.py:46
  127.0 7.5 %collective-permute-start.22 = (bf16[352,256]{1,0:T(8,128)(2,1)S(1)}, bf16[352,256]{1,0:T(8,128)(2,1)S(1)}, u32[]{:S(2)}, u32[]{:S(2)}) collective-permute-start(bf16[352,256]{1,0:T(8,128)(2,1)S(1)} %reshape.38), channel_id=1, source_target_pairs={{0,128},{1,129},{128,0},{129,1},{2,130},{3,131},{130,2},{131,3},{4... | collective-permute-start | bytes 540680 | tf_op jit(solution)/shard_map/ppermute | solution.py:46
  127.1 7.9 %collective-permute-start.23 = (bf16[352,256]{1,0:T(8,128)(2,1)S(1)}, bf16[352,256]{1,0:T(8,128)(2,1)S(1)}, u32[]{:S(2)}, u32[]{:S(2)}) collective-permute-start(bf16[352,256]{1,0:T(8,128)(2,1)S(1)} %reshape.38), channel_id=1, source_target_pairs={{0,1},{1,0},{128,129},{129,128},{2,3},{3,2},{130,131},{131,130},{4... | collective-permute-start | bytes 540680 | tf_op jit(solution)/shard_map/ppermute | solution.py:46
  135.1 11.9 %collective-permute-start.24 = (bf16[384,256]{1,0:T(8,128)(2,1)S(1)}, bf16[384,256]{1,0:T(8,128)(2,1)S(1)}, u32[]{:S(2)}, u32[]{:S(2)}) collective-permute-start(bf16[384,256]{1,0:T(8,128)(2,1)S(1)} %pad_maximum_fusion.1.refs_0_), channel_id=1, source_target_pairs={{0,4},{4,0},{8,12},{12,8},{1,5},{5,1},{9,13},{13,9},{2,6},{6,2},{1... | collective-permute-start | bytes 589832 | tf_op jit(solution)/shard_map/ppermute | solution.py:419
  135.2 12.0 %collective-permute-start.25 = (bf16[384,256]{1,0:T(8,128)(2,1)S(1)}, bf16[384,256]{1,0:T(8,128)(2,1)S(1)}, u32[]{:S(2)}, u32[]{:S(2)}) collective-permute-start(bf16[384,256]{1,0:T(8,128)(2,1)S(1)} %pad_maximum_fusion.1.refs_0_), channel_id=1, source_target_pairs={{0,8},{4,12},{8,0},{12,4},{1,9},{5,13},{9,1},{13,5},{2,10},{6,14},... | collective-permute-start | bytes 589832 | tf_op jit(solution)/shard_map/ppermute | solution.py:419
  139.1 12.7 %collective-permute-start.26 = (bf16[384,256]{1,0:T(8,128)(2,1)S(1)}, bf16[384,256]{1,0:T(8,128)(2,1)S(1)}, u32[]{:S(2)}, u32[]{:S(2)}) collective-permute-start(bf16[384,256]{1,0:T(8,128)(2,1)S(1)} %pad_maximum_fusion.1.refs_0_), channel_id=1, source_target_pairs={{0,12},{4,8},{8,4},{12,0},{1,13},{5,9},{9,5},{13,1},{2,14},{6,10},... | collective-permute-start | bytes 589832 | tf_op jit(solution)/shard_map/ppermute | solution.py:419
  139.1 15.5 %collective-permute-start.27 = (bf16[384,256]{1,0:T(8,128)(2,1)S(1)}, bf16[384,256]{1,0:T(8,128)(2,1)S(1)}, u32[]{:S(2)}, u32[]{:S(2)}) collective-permute-start(bf16[384,256]{1,0:T(8,128)(2,1)S(1)} %pad_maximum_fusion.1.refs_0_), channel_id=1, source_target_pairs={{0,2},{2,0},{1,3},{3,1},{4,6},{6,4},{5,7},{7,5},{8,10},{10,8},{9,1... | collective-permute-start | bytes 589832 | tf_op jit(solution)/shard_map/ppermute | solution.py:420
  147.1 7.6 %collective-permute-start.28 = (bf16[384,256]{1,0:T(8,128)(2,1)S(1)}, bf16[384,256]{1,0:T(8,128)(2,1)S(1)}, u32[]{:S(2)}, u32[]{:S(2)}) collective-permute-start(bf16[384,256]{1,0:T(8,128)(2,1)S(1)} %collective-permute-done.24.refs_1_), channel_id=1, source_target_pairs={{0,2},{2,0},{1,3},{3,1},{4,6},{6,4},{5,7},{7,5},{8,10},{10,8},{9,1... | collective-permute-start | bytes 589832 | tf_op jit(solution)/shard_map/ppermute | solution.py:420
  147.2 7.4 %collective-permute-start.29 = (bf16[384,256]{1,0:T(8,128)(2,1)S(1)}, bf16[384,256]{1,0:T(8,128)(2,1)S(1)}, u32[]{:S(2)}, u32[]{:S(2)}) collective-permute-start(bf16[384,256]{1,0:T(8,128)(2,1)S(1)} %collective-permute-done.25.refs_2_), channel_id=1, source_target_pairs={{0,2},{2,0},{1,3},{3,1},{4,6},{6,4},{5,7},{7,5},{8,10},{10,8},{9,1... | collective-permute-start | bytes 589832 | tf_op jit(solution)/shard_map/ppermute | solution.py:420
  151.8 3.1 %collective-permute-start.30 = (bf16[384,256]{1,0:T(8,128)(2,1)S(1)}, bf16[384,256]{1,0:T(8,128)(2,1)S(1)}, u32[]{:S(2)}, u32[]{:S(2)}) collective-permute-start(bf16[384,256]{1,0:T(8,128)(2,1)S(1)} %collective-permute-done.26.refs_3_), channel_id=1, source_target_pairs={{0,2},{2,0},{1,3},{3,1},{4,6},{6,4},{5,7},{7,5},{8,10},{10,8},{9,1... | collective-permute-start | bytes 589832 | tf_op jit(solution)/shard_map/ppermute | solution.py:420

commit v5 on v4

--- a/solution.py
+++ b/solution.py
@@ -154,7 +154,7 @@
         slope[pl.ds(row, chunk), :] = sigma * (1.0 + pre * (1.0 - sigma))
         hid[pl.ds(pl.multiple_of(row + FRAME, FRAME), chunk), :] = (pre * sigma).astype(BF)
 
-    chunk = min(tokens, 1024)
+    chunk = min(tokens, 2048)
     n_chunk = tokens // chunk
     @pl.loop(0, n_chunk)
     def _(i):

time: 158 us -> 157 us (level)
  no operation moved by 1% of the time
where the time goes in v5:
time: 157 us
  starting transfers between devices  55.8 us (36%)
  Pallas kernels  38.9 us (25%)
  blocking collectives  38.8 us (25%)
  waiting for transfers between devices  16.6 us (11%)
  local copies, waits for them, and re-layouts  3.5 us (2%)
  other arithmetic  2.18 us (1%)
    pallas_call x1, Pallas kernels, local_terms(): pl.pallas_call(functools.partial(local_kernel, sizes), name='local_terms'...  36.4 us
    all_to_all x2, blocking collectives, spread(): lax.all_to_all(jnp.broadcast_to(block[None], (count,) + block.shape), axi...  27.7 us
    ppermute x4, starting transfers between devices, on_device(): parts += [block, lax.ppermute(block, 'c', xor_perm(n_c, 1))]  14.5 us
    ppermute x4, starting transfers between devices, on_device(): others = [lax.ppermute(p, 'c', xor_perm(n_c, 1)) for p in pieces]  13.9 us
    all_to_all x1, blocking collectives, on_device(): got = lax.all_to_all(block.astype(BF).reshape(n_z, rows, ch), 'z', 0, 0)  11 us
    ppermute x3, waiting for transfers between devices, gather_xor(): lax.ppermute(block, axis, xor_perm(count, s))  4.81 us
    ppermute x3, starting transfers between devices, on_device(): lax.ppermute(heads[r], x_axes, xor_perm(n_x, r)).astype(F32)  4.44 us
    ppermute x3, waiting for transfers between devices, on_device(): got = lax.ppermute(low[r * cut:(r + 1) * cut], x_axes, xor_perm(n_x, r))  4.33 us
  transfers between devices with their start and end apart: 31, of which 13 were waited for; matrix products, arithmetic and copies ran while one was open for 3% of the time, Pallas kernels for 0%

profile of v5, /device:TPU:1, one launch (start us, length us, event | category | flops | bytes accessed | tf_op | source)
XLA Modules:
  0.0 156.8 jit_solution(13086777754679513142)
XLA Ops:
  0.6 0.0 copy-start
  0.7 0.9 copy-done
  1.6 0.0 copy-start.4
  1.6 16.7 %all_to_all.15 = bf16[8,32,256]{2,1,0:T(8,128)(2,1)S(1)} all-to-all(bf16[8,32,256]{2,1,0:T(8,128)(2,1)S(1)} %broadcast_in_dim.7), channel_id=1, replica_groups=mesh['xh'=2,'z'=8,'y'=4,'c'=2,'dp'=2] {'z'}, dimensions={0} | all-to-all | bytes 262144 | tf_op jit(solution)/shard_map/all_to_all | solution.py:51
  18.3 2.7 %collective-permute-start = (bf16[8,32,256]{2,1,0:T(8,128)(2,1)S(1)}, bf16[8,32,256]{2,1,0:T(8,128)(2,1)S(1)}, u32[]{:S(2)}, u32[]{:S(2)}) collective-permute-start(bf16[8,32,256]{2,1,0:T(8,128)(2,1)S(1)} %all_to_all.15), channel_id=1, source_target_pairs={{0,128},{128,0},{1,129},{129,1},{2,130},{130,2},{3,131},{131,3},{4... | collective-permute-start | bytes 393224 | tf_op jit(solution)/shard_map/ppermute | solution.py:375
  21.0 1.4 constant_dynamic-update-slice_fusion.5
  22.5 1.1 collective-permute-done
  23.6 1.4 collective-permute-start.2
  25.0 2.6 %collective-permute-start.4 = (bf16[2,8,32,256]{3,2,1,0:T(8,128)(2,1)S(1)}, bf16[2,8,32,256]{3,2,1,0:T(8,128)(2,1)S(1)}, u32[]{:S(2)}, u32[]{:S(2)}) collective-permute-start(bf16[2,8,32,256]{3,2,1,0:T(8,128)(2,1)S(1)} %pad_maximum_fusion.refs_0_), channel_id=1, source_target_pairs={{0,8},{4,12},{8,0},{12,4},{1,9},{5,13},{9,1},{13,5},{2,10},{6,14},... | collective-permute-start | bytes 786440 | tf_op jit(solution)/shard_map/ppermute | solution.py:378
  27.6 0.0 collective-permute-start.6
  27.7 4.3 %collective-permute-start.1 = (bf16[2,8,32,256]{3,2,1,0:T(8,128)(2,1)S(1)}, bf16[2,8,32,256]{3,2,1,0:T(8,128)(2,1)}, u32[]{:S(2)}, u32[]{:S(2)}) collective-permute-start(bf16[2,8,32,256]{3,2,1,0:T(8,128)(2,1)S(1)} %pad_maximum_fusion.refs_0_), channel_id=1, source_target_pairs={{0,2},{2,0},{1,3},{3,1},{4,6},{6,4},{5,7},{7,5},{8,10},{10,8},{9,1... | collective-permute-start | bytes 786440 | tf_op jit(solution)/shard_map/ppermute | solution.py:379
  32.0 0.0 collective-permute-done.2.refs_2_
  32.0 3.3 %collective-permute-start.3 = (bf16[2,8,32,256]{3,2,1,0:T(8,128)(2,1)S(1)}, bf16[2,8,32,256]{3,2,1,0:T(8,128)(2,1)}, u32[]{:S(2)}, u32[]{:S(2)}) collective-permute-start(bf16[2,8,32,256]{3,2,1,0:T(8,128)(2,1)S(1)} %collective-permute-done.2.refs_2_), channel_id=1, source_target_pairs={{0,2},{2,0},{1,3},{3,1},{4,6},{6,4},{5,7},{7,5},{8,10},{10,8},{9,1... | collective-permute-start | bytes 786440 | tf_op jit(solution)/shard_map/ppermute | solution.py:379
  35.3 0.7 collective-permute-done.4.refs_4_
  36.0 4.7 %collective-permute-start.5 = (bf16[2,8,32,256]{3,2,1,0:T(8,128)(2,1)S(1)}, bf16[2,8,32,256]{3,2,1,0:T(8,128)(2,1)}, u32[]{:S(2)}, u32[]{:S(2)}) collective-permute-start(bf16[2,8,32,256]{3,2,1,0:T(8,128)(2,1)S(1)} %collective-permute-done.4.refs_4_), channel_id=1, source_target_pairs={{0,2},{2,0},{1,3},{3,1},{4,6},{6,4},{5,7},{7,5},{8,10},{10,8},{9,1... | collective-permute-start | bytes 786440 | tf_op jit(solution)/shard_map/ppermute | solution.py:379
  40.7 0.3 collective-permute-done.6.refs_6_
  41.0 2.2 %collective-permute-start.7 = (bf16[2,8,32,256]{3,2,1,0:T(8,128)(2,1)S(1)}, bf16[2,8,32,256]{3,2,1,0:T(8,128)(2,1)}, u32[]{:S(2)}, u32[]{:S(2)}) collective-permute-start(bf16[2,8,32,256]{3,2,1,0:T(8,128)(2,1)S(1)} %collective-permute-done.6.refs_6_), channel_id=1, source_target_pairs={{0,2},{2,0},{1,3},{3,1},{4,6},{6,4},{5,7},{7,5},{8,10},{10,8},{9,1... | collective-permute-start | bytes 786440 | tf_op jit(solution)/shard_map/ppermute | solution.py:379
  43.3 0.1 stack.32.pos
  43.3 0.9 bitcast_dynamic-update-slice_fusion.refs_8_
  44.3 0.0 collective-permute-done.3.refs_3_
  44.3 0.0 collective-permute-done.5.refs_5_
  44.3 0.2 collective-permute-done.7.refs_7_
  44.5 36.4 %local_terms.1 = (bf16[384,256]{1,0:T(8,128)(2,1)S(1)}, bf16[384,256]{1,0:T(8,128)(2,1)S(1)}, bf16[384,256]{1,0:T(8,128)(2,1)S(1)}, bf16[384,256]{1,0:T(8,128)(2...) custom-call(s32[5]{0:T(128)S(1)} %stack.32.pos, ...), custom_call_target="tpu_custom_call" | custom-call | flops 24000000000 | bytes 12582912 | tf_op jit(solution)/shard_map/local_terms/pallas_call | solution.py:288
  80.9 0.5 collective-permute-start.9
  81.4 0.1 collective-permute-start.11
  81.5 0.4 collective-permute-start.13
  81.9 0.1 collective-permute-start.8
  82.0 0.4 collective-permute-done.9
  82.5 0.1 collective-permute-start.10
  82.6 0.2 collective-permute-done.11
  82.8 1.0 collective-permute-start.12
  83.9 0.0 collective-permute-done.13
  83.9 2.8 %collective-permute-start.14 = (bf16[384,256]{1,0:T(8,128)(2,1)S(1)}, bf16[384,256]{1,0:T(8,128)(2,1)S(1)}, u32[]{:S(2)}, u32[]{:S(2)}) collective-permute-start(bf16[384,256]{1,0:T(8,128)(2,1)S(1)} %add_convert_fusion), channel_id=1, source_target_pairs={{0,12},{4,8},{8,4},{12,0},{1,13},{5,9},{9,5},{13,1},{2,14},{6,10},... | collective-permute-start | bytes 589832 | tf_op jit(solution)/shard_map/ppermute | solution.py:399
  86.7 1.2 collective-permute-start.18
  87.9 2.4 %collective-permute-start.19 = (bf16[256,256]{1,0:T(8,128)(2,1)S(1)}, bf16[256,256]{1,0:T(8,128)(2,1)S(1)}, u32[]{:S(2)}, u32[]{:S(2)}) collective-permute-start(bf16[256,256]{1,0:T(8,128)(2,1)S(1)} %get-tuple-element.30), channel_id=1, source_target_pairs={{0,128},{1,129},{128,0},{129,1},{2,130},{3,131},{130,2},{131,3},{4... | collective-permute-start | bytes 393224 | tf_op jit(solution)/shard_map/ppermute | solution.py:402
  90.4 0.8 collective-permute-start.20
  91.2 1.5 collective-permute-done.12
  92.7 2.8 %collective-permute-done.14 = bf16[384,256]{1,0:T(8,128)(2,1)S(1)} collective-permute-done((bf16[384,256]{1,0:T(8,128)(2,1)S(1)}, bf16[384,256]{1,0:T(8,128)(2,1)S(1)}, u32[]{:S(2)}, u32[]{:S(2)}) %collective-permute-start.14) | collective-permute-done | bytes 196640 | tf_op jit(solution)/shard_map/ppermute | solution.py:399
  95.4 0.1 fusion.3
  95.6 1.3 collective-permute-start.15
  96.9 2.4 %collective-permute-start.16 = (bf16[96,256]{1,0:T(8,128)(2,1)S(1)}, bf16[96,256]{1,0:T(8,128)(2,1)S(1)}, u32[]{:S(2)}, u32[]{:S(2)}) collective-permute-start(bf16[96,256]{1,0:T(8,128)(2,1)S(1)} %get-tuple-element.42), channel_id=1, source_target_pairs={{0,128},{1,129},{128,0},{129,1},{2,130},{3,131},{130,2},{131,3},{4... | collective-permute-start | bytes 147464 | tf_op jit(solution)/shard_map/ppermute | solution.py:407
  99.3 0.2 collective-permute-start.17
  99.5 0.1 add_convert_fusion.3
  99.6 1.7 %collective-permute-done.16 = bf16[96,256]{1,0:T(8,128)(2,1)S(1)} collective-permute-done((bf16[96,256]{1,0:T(8,128)(2,1)S(1)}, bf16[96,256]{1,0:T(8,128)(2,1)S(1)}, u32[]{:S(2)}, u32[]{:S(2)}) %collective-permute-start.16) | collective-permute-done | bytes 49184 | tf_op jit(solution)/shard_map/ppermute | solution.py:407
  101.3 2.6 %collective-permute-done.17 = bf16[96,256]{1,0:T(8,128)(2,1)S(1)} collective-permute-done((bf16[96,256]{1,0:T(8,128)(2,1)S(1)}, bf16[96,256]{1,0:T(8,128)(2,1)S(1)}, u32[]{:S(2)}, u32[]{:S(2)}) %collective-permute-start.17) | collective-permute-done | bytes 49184 | tf_op jit(solution)/shard_map/ppermute | solution.py:407
  104.0 11.0 %all_to_all.16 = bf16[8,44,256]{2,1,0:T(8,128)(2,1)S(1)} all-to-all(bf16[8,44,256]{2,1,0:T(8,128)(2,1)S(1)} %convert_element_type.119), channel_id=1, replica_groups=mesh['xh'=2,'z'=8,'y'=4,'c'=2,'dp'=2] {'z'}, dimensions={0} | all-to-all | bytes 360448 | tf_op jit(solution)/shard_map/all_to_all | solution.py:411
  115.1 11.0 %all_to_all.17 = bf16[8,44,256]{2,1,0:T(8,128)(2,1)S(1)} all-to-all(bf16[8,44,256]{2,1,0:T(8,128)(2,1)S(1)} %broadcast_in_dim.16), channel_id=1, replica_groups=mesh['xh'=2,'z'=8,'y'=4,'c'=2,'dp'=2] {'z'}, dimensions={0} | all-to-all | bytes 360448 | tf_op jit(solution)/shard_map/all_to_all | solution.py:51
  126.2 0.1 collective-permute-start.21
  126.3 0.1 collective-permute-start.22
  126.5 3.1 %collective-permute-start.23 = (bf16[352,256]{1,0:T(8,128)(2,1)S(1)}, bf16[352,256]{1,0:T(8,128)(2,1)S(1)}, u32[]{:S(2)}, u32[]{:S(2)}) collective-permute-start(bf16[352,256]{1,0:T(8,128)(2,1)S(1)} %reshape.38), channel_id=1, source_target_pairs={{0,1},{1,0},{128,129},{129,128},{2,3},{3,2},{130,131},{131,130},{4... | collective-permute-start | bytes 540680 | tf_op jit(solution)/shard_map/ppermute | solution.py:46
  129.6 4.2 %collective-permute-done.21 = bf16[352,256]{1,0:T(8,128)(2,1)S(1)} collective-permute-done((bf16[352,256]{1,0:T(8,128)(2,1)S(1)}, bf16[352,256]{1,0:T(8,128)(2,1)S(1)}, u32[]{:S(2)}, u32[]{:S(2)}) %collective-permute-start.21) | collective-permute-done | bytes 180256 | tf_op jit(solution)/shard_map/ppermute | solution.py:46
  133.8 0.6 collective-permute-done.23
  134.4 0.1 broadcast_select_fusion.7
  134.5 0.1 collective-permute-start.24
  134.6 3.8 %collective-permute-start.25 = (bf16[384,256]{1,0:T(8,128)(2,1)S(1)}, bf16[384,256]{1,0:T(8,128)(2,1)S(1)}, u32[]{:S(2)}, u32[]{:S(2)}) collective-permute-start(bf16[384,256]{1,0:T(8,128)(2,1)S(1)} %pad_maximum_fusion.1.refs_0_), channel_id=1, source_target_pairs={{0,8},{4,12},{8,0},{12,4},{1,9},{5,13},{9,1},{13,5},{2,10},{6,14},... | collective-permute-start | bytes 589832 | tf_op jit(solution)/shard_map/ppermute | solution.py:419
  138.5 0.0 collective-permute-start.26
  138.5 7.1 %collective-permute-start.27 = (bf16[384,256]{1,0:T(8,128)(2,1)S(1)}, bf16[384,256]{1,0:T(8,128)(2,1)S(1)}, u32[]{:S(2)}, u32[]{:S(2)}) collective-permute-start(bf16[384,256]{1,0:T(8,128)(2,1)S(1)} %pad_maximum_fusion.1.refs_0_), channel_id=1, source_target_pairs={{0,2},{2,0},{1,3},{3,1},{4,6},{6,4},{5,7},{7,5},{8,10},{10,8},{9,1... | collective-permute-start | bytes 589832 | tf_op jit(solution)/shard_map/ppermute | solution.py:420
  145.6 0.8 slice_convert_fusion
  146.4 0.1 collective-permute-start.28
  146.6 4.6 %collective-permute-start.29 = (bf16[384,256]{1,0:T(8,128)(2,1)S(1)}, bf16[384,256]{1,0:T(8,128)(2,1)S(1)}, u32[]{:S(2)}, u32[]{:S(2)}) collective-permute-start(bf16[384,256]{1,0:T(8,128)(2,1)S(1)} %collective-permute-done.25.refs_2_), channel_id=1, source_target_pairs={{0,2},{2,0},{1,3},{3,1},{4,6},{6,4},{5,7},{7,5},{8,10},{10,8},{9,1... | collective-permute-start | bytes 589832 | tf_op jit(solution)/shard_map/ppermute | solution.py:420
  151.2 2.0 %collective-permute-start.30 = (bf16[384,256]{1,0:T(8,128)(2,1)S(1)}, bf16[384,256]{1,0:T(8,128)(2,1)S(1)}, u32[]{:S(2)}, u32[]{:S(2)}) collective-permute-start(bf16[384,256]{1,0:T(8,128)(2,1)S(1)} %collective-permute-done.26.refs_3_), channel_id=1, source_target_pairs={{0,2},{2,0},{1,3},{3,1},{4,6},{6,4},{5,7},{7,5},{8,10},{10,8},{9,1... | collective-permute-start | bytes 589832 | tf_op jit(solution)/shard_map/ppermute | solution.py:420
  153.2 0.8 slice_convert_fusion.2
  154.0 0.2 collective-permute-done.30.refs_7_
  154.2 2.5 %place.1 = (f32[2304,256]{1,0:T(8,128)}, f32[768,256]{1,0:T(8,128)}) custom-call(s32[5]{0:T(128)S(1)} %stack.32.pos, bf16[384,256]{1,0:T(8,128)(2,1)S(1)} %pad_maximum_fusion.1.refs_0_, bf16[384,256]{1,0:T(8,128)(2,1)S(1)} %collective-permute-done.24.refs_1_, bf16[384,256]{1,0:T(8,128)(2,1)S(1)} %collective-permute-done.25.refs_2_, ...), custom_call_target="tpu_custom_call" | custom-call | bytes 4718592 | tf_op jit(solution)/shard_map/place/pallas_call | solution.py:344
  (50 shorter events, 0.5 us)
Async XLA Ops:
  0.6 0.9 copy-start
  0.6 21.8 %copy-start.1 = (bf16[3,256,256]{2,1,0:T(8,128)(2,1)S(1)}, bf16[3,256,256]{2,1,0:T(8,128)(2,1)}, u32[]{:S(2)}) copy-start(bf16[3,256,256]{2,1,0:T(8,128)(2,1)} %param.12) | copy-start | bytes 1179652
  1.5 26.1 %copy-start.2 = (bf16[256,256]{1,0:T(8,128)(2,1)S(1)}, bf16[256,256]{1,0:T(8,128)(2,1)}, u32[]{:S(2)}) copy-start(bf16[256,256]{1,0:T(8,128)(2,1)} %param.13) | copy-start | bytes 393220
  1.5 26.1 %copy-start.3 = (bf16[256,256]{1,0:T(8,128)(2,1)S(1)}, bf16[256,256]{1,0:T(8,128)(2,1)}, u32[]{:S(2)}) copy-start(bf16[256,256]{1,0:T(8,128)(2,1)} %param.14) | copy-start | bytes 393220
  1.6 26.1 %copy-start.4 = (bf16[256,256]{1,0:T(8,128)(2,1)S(1)}, bf16[256,256]{1,0:T(8,128)(2,1)}, u32[]{:S(2)}) copy-start(bf16[256,256]{1,0:T(8,128)(2,1)} %param.15) | copy-start | bytes 393220
  18.3 5.3 %collective-permute-start = (bf16[8,32,256]{2,1,0:T(8,128)(2,1)S(1)}, bf16[8,32,256]{2,1,0:T(8,128)(2,1)S(1)}, u32[]{:S(2)}, u32[]{:S(2)}) collective-permute-start(bf16[8,32,256]{2,1,0:T(8,128)(2,1)S(1)} %all_to_all.15), channel_id=1, source_target_pairs={{0,128},{128,0},{1,129},{129,1},{2,130},{130,2},{3,131},{131,3},{4... | collective-permute-start | bytes 393224 | tf_op jit(solution)/shard_map/ppermute | solution.py:375
  21.0 22.2 %copy-start.5 = (bf16[256,256]{1,0:T(8,128)(2,1)S(1)}, bf16[256,256]{1,0:T(8,128)(2,1)}, u32[]{:S(2)}) copy-start(bf16[256,256]{1,0:T(8,128)(2,1)} %param.16) | copy-start | bytes 393220
  21.0 22.2 %copy-start.6 = (s32[1,4096]{1,0:T(1,128)S(1)}, s32[1,4096]{1,0:T(1,128)}, u32[]{:S(2)}) copy-start(s32[1,4096]{1,0:T(1,128)} %param.10) | copy-start | bytes 49156
  23.6 8.4 %collective-permute-start.2 = (bf16[2,8,32,256]{3,2,1,0:T(8,128)(2,1)S(1)}, bf16[2,8,32,256]{3,2,1,0:T(8,128)(2,1)S(1)}, u32[]{:S(2)}, u32[]{:S(2)}) collective-permute-start(bf16[2,8,32,256]{3,2,1,0:T(8,128)(2,1)S(1)} %pad_maximum_fusion.refs_0_), channel_id=1, source_target_pairs={{0,4},{4,0},{8,12},{12,8},{1,5},{5,1},{9,13},{13,9},{2,6},{6,2},{1... | collective-permute-start | bytes 786440 | tf_op jit(solution)/shard_map/ppermute | solution.py:378
  25.0 10.9 %collective-permute-start.4 = (bf16[2,8,32,256]{3,2,1,0:T(8,128)(2,1)S(1)}, bf16[2,8,32,256]{3,2,1,0:T(8,128)(2,1)S(1)}, u32[]{:S(2)}, u32[]{:S(2)}) collective-permute-start(bf16[2,8,32,256]{3,2,1,0:T(8,128)(2,1)S(1)} %pad_maximum_fusion.refs_0_), channel_id=1, source_target_pairs={{0,8},{4,12},{8,0},{12,4},{1,9},{5,13},{9,1},{13,5},{2,10},{6,14},... | collective-permute-start | bytes 786440 | tf_op jit(solution)/shard_map/ppermute | solution.py:378
  27.6 13.3 %collective-permute-start.6 = (bf16[2,8,32,256]{3,2,1,0:T(8,128)(2,1)S(1)}, bf16[2,8,32,256]{3,2,1,0:T(8,128)(2,1)S(1)}, u32[]{:S(2)}, u32[]{:S(2)}) collective-permute-start(bf16[2,8,32,256]{3,2,1,0:T(8,128)(2,1)S(1)} %pad_maximum_fusion.refs_0_), channel_id=1, source_target_pairs={{0,12},{4,8},{8,4},{12,0},{1,13},{5,9},{9,5},{13,1},{2,14},{6,10},... | collective-permute-start | bytes 786440 | tf_op jit(solution)/shard_map/ppermute | solution.py:378
  27.7 16.5 %collective-permute-start.1 = (bf16[2,8,32,256]{3,2,1,0:T(8,128)(2,1)S(1)}, bf16[2,8,32,256]{3,2,1,0:T(8,128)(2,1)}, u32[]{:S(2)}, u32[]{:S(2)}) collective-permute-start(bf16[2,8,32,256]{3,2,1,0:T(8,128)(2,1)S(1)} %pad_maximum_fusion.refs_0_), channel_id=1, source_target_pairs={{0,2},{2,0},{1,3},{3,1},{4,6},{6,4},{5,7},{7,5},{8,10},{10,8},{9,1... | collective-permute-start | bytes 786440 | tf_op jit(solution)/shard_map/ppermute | solution.py:379
  32.0 12.3 %collective-permute-start.3 = (bf16[2,8,32,256]{3,2,1,0:T(8,128)(2,1)S(1)}, bf16[2,8,32,256]{3,2,1,0:T(8,128)(2,1)}, u32[]{:S(2)}, u32[]{:S(2)}) collective-permute-start(bf16[2,8,32,256]{3,2,1,0:T(8,128)(2,1)S(1)} %collective-permute-done.2.refs_2_), channel_id=1, source_target_pairs={{0,2},{2,0},{1,3},{3,1},{4,6},{6,4},{5,7},{7,5},{8,10},{10,8},{9,1... | collective-permute-start | bytes 786440 | tf_op jit(solution)/shard_map/ppermute | solution.py:379
  36.0 8.3 %collective-permute-start.5 = (bf16[2,8,32,256]{3,2,1,0:T(8,128)(2,1)S(1)}, bf16[2,8,32,256]{3,2,1,0:T(8,128)(2,1)}, u32[]{:S(2)}, u32[]{:S(2)}) collective-permute-start(bf16[2,8,32,256]{3,2,1,0:T(8,128)(2,1)S(1)} %collective-permute-done.4.refs_4_), channel_id=1, source_target_pairs={{0,2},{2,0},{1,3},{3,1},{4,6},{6,4},{5,7},{7,5},{8,10},{10,8},{9,1... | collective-permute-start | bytes 786440 | tf_op jit(solution)/shard_map/ppermute | solution.py:379
  41.0 3.5 %collective-permute-start.7 = (bf16[2,8,32,256]{3,2,1,0:T(8,128)(2,1)S(1)}, bf16[2,8,32,256]{3,2,1,0:T(8,128)(2,1)}, u32[]{:S(2)}, u32[]{:S(2)}) collective-permute-start(bf16[2,8,32,256]{3,2,1,0:T(8,128)(2,1)S(1)} %collective-permute-done.6.refs_6_), channel_id=1, source_target_pairs={{0,2},{2,0},{1,3},{3,1},{4,6},{6,4},{5,7},{7,5},{8,10},{10,8},{9,1... | collective-permute-start | bytes 786440 | tf_op jit(solution)/shard_map/ppermute | solution.py:379
  80.9 1.5 collective-permute-start.9
  81.4 1.4 collective-permute-start.11
  81.5 2.4 %collective-permute-start.13 = (bf16[384,256]{1,0:T(8,128)(2,1)S(1)}, bf16[384,256]{1,0:T(8,128)(2,1)S(1)}, u32[]{:S(2)}, u32[]{:S(2)}) collective-permute-start(bf16[384,256]{1,0:T(8,128)(2,1)S(1)} %get-tuple-element.27), channel_id=1, source_target_pairs={{0,2},{2,0},{1,3},{3,1},{4,6},{6,4},{5,7},{7,5},{8,10},{10,8},{9,1... | collective-permute-start | bytes 589832 | tf_op jit(solution)/shard_map/ppermute | solution.py:395
  81.9 6.1 %collective-permute-start.8 = (bf16[384,256]{1,0:T(8,128)(2,1)S(1)}, bf16[384,256]{1,0:T(8,128)(2,1)S(1)}, u32[]{:S(2)}, u32[]{:S(2)}) collective-permute-start(bf16[384,256]{1,0:T(8,128)(2,1)S(1)} %get-tuple-element.21), channel_id=1, source_target_pairs={{0,2},{2,0},{1,3},{3,1},{4,6},{6,4},{5,7},{7,5},{8,10},{10,8},{9,1... | collective-permute-start | bytes 589832 | tf_op jit(solution)/shard_map/ppermute | solution.py:395
  82.5 7.9 %collective-permute-start.10 = (bf16[384,256]{1,0:T(8,128)(2,1)S(1)}, bf16[384,256]{1,0:T(8,128)(2,1)S(1)}, u32[]{:S(2)}, u32[]{:S(2)}) collective-permute-start(bf16[384,256]{1,0:T(8,128)(2,1)S(1)} %add_convert_fusion.2), channel_id=1, source_target_pairs={{0,4},{4,0},{8,12},{12,8},{1,5},{5,1},{9,13},{13,9},{2,6},{6,2},{1... | collective-permute-start | bytes 589832 | tf_op jit(solution)/shard_map/ppermute | solution.py:399
  82.8 9.8 %collective-permute-start.12 = (bf16[384,256]{1,0:T(8,128)(2,1)S(1)}, bf16[384,256]{1,0:T(8,128)(2,1)S(1)}, u32[]{:S(2)}, u32[]{:S(2)}) collective-permute-start(bf16[384,256]{1,0:T(8,128)(2,1)S(1)} %add_convert_fusion.1), channel_id=1, source_target_pairs={{0,8},{4,12},{8,0},{12,4},{1,9},{5,13},{9,1},{13,5},{2,10},{6,14},... | collective-permute-start | bytes 589832 | tf_op jit(solution)/shard_map/ppermute | solution.py:399
  83.9 11.5 %collective-permute-start.14 = (bf16[384,256]{1,0:T(8,128)(2,1)S(1)}, bf16[384,256]{1,0:T(8,128)(2,1)S(1)}, u32[]{:S(2)}, u32[]{:S(2)}) collective-permute-start(bf16[384,256]{1,0:T(8,128)(2,1)S(1)} %add_convert_fusion), channel_id=1, source_target_pairs={{0,12},{4,8},{8,4},{12,0},{1,13},{5,9},{9,5},{13,1},{2,14},{6,10},... | collective-permute-start | bytes 589832 | tf_op jit(solution)/shard_map/ppermute | solution.py:399
  86.7 12.6 %collective-permute-start.18 = (bf16[256,256]{1,0:T(8,128)(2,1)S(1)}, bf16[256,256]{1,0:T(8,128)(2,1)S(1)}, u32[]{:S(2)}, u32[]{:S(2)}) collective-permute-start(bf16[256,256]{1,0:T(8,128)(2,1)S(1)} %get-tuple-element.29), channel_id=1, source_target_pairs={{0,1},{1,0},{128,129},{129,128},{2,3},{3,2},{130,131},{131,130},{4... | collective-permute-start | bytes 393224 | tf_op jit(solution)/shard_map/ppermute | solution.py:402
  87.9 11.6 %collective-permute-start.19 = (bf16[256,256]{1,0:T(8,128)(2,1)S(1)}, bf16[256,256]{1,0:T(8,128)(2,1)S(1)}, u32[]{:S(2)}, u32[]{:S(2)}) collective-permute-start(bf16[256,256]{1,0:T(8,128)(2,1)S(1)} %get-tuple-element.30), channel_id=1, source_target_pairs={{0,128},{1,129},{128,0},{129,1},{2,130},{3,131},{130,2},{131,3},{4... | collective-permute-start | bytes 393224 | tf_op jit(solution)/shard_map/ppermute | solution.py:402
  90.4 9.1 %collective-permute-start.20 = (bf16[256,256]{1,0:T(8,128)(2,1)S(1)}, bf16[256,256]{1,0:T(8,128)(2,1)S(1)}, u32[]{:S(2)}, u32[]{:S(2)}) collective-permute-start(bf16[256,256]{1,0:T(8,128)(2,1)S(1)} %get-tuple-element.31), channel_id=1, source_target_pairs={{0,129},{1,128},{128,1},{129,0},{2,131},{3,130},{130,3},{131,2},{4... | collective-permute-start | bytes 393224 | tf_op jit(solution)/shard_map/ppermute | solution.py:402
  95.6 4.0 %collective-permute-start.15 = (bf16[96,256]{1,0:T(8,128)(2,1)S(1)}, bf16[96,256]{1,0:T(8,128)(2,1)S(1)}, u32[]{:S(2)}, u32[]{:S(2)}) collective-permute-start(bf16[96,256]{1,0:T(8,128)(2,1)S(1)} %get-tuple-element.40), channel_id=1, source_target_pairs={{0,1},{1,0},{128,129},{129,128},{2,3},{3,2},{130,131},{131,130},{4... | collective-permute-start | bytes 147464 | tf_op jit(solution)/shard_map/ppermute | solution.py:407
  96.9 4.4 %collective-permute-start.16 = (bf16[96,256]{1,0:T(8,128)(2,1)S(1)}, bf16[96,256]{1,0:T(8,128)(2,1)S(1)}, u32[]{:S(2)}, u32[]{:S(2)}) collective-permute-start(bf16[96,256]{1,0:T(8,128)(2,1)S(1)} %get-tuple-element.42), channel_id=1, source_target_pairs={{0,128},{1,129},{128,0},{129,1},{2,130},{3,131},{130,2},{131,3},{4... | collective-permute-start | bytes 147464 | tf_op jit(solution)/shard_map/ppermute | solution.py:407
  99.3 4.6 %collective-permute-start.17 = (bf16[96,256]{1,0:T(8,128)(2,1)S(1)}, bf16[96,256]{1,0:T(8,128)(2,1)S(1)}, u32[]{:S(2)}, u32[]{:S(2)}) collective-permute-start(bf16[96,256]{1,0:T(8,128)(2,1)S(1)} %get-tuple-element.41), channel_id=1, source_target_pairs={{0,129},{1,128},{128,1},{129,0},{2,131},{3,130},{130,3},{131,2},{4... | collective-permute-start | bytes 147464 | tf_op jit(solution)/shard_map/ppermute | solution.py:407
  126.2 7.6 %collective-permute-start.21 = (bf16[352,256]{1,0:T(8,128)(2,1)S(1)}, bf16[352,256]{1,0:T(8,128)(2,1)S(1)}, u32[]{:S(2)}, u32[]{:S(2)}) collective-permute-start(bf16[352,256]{1,0:T(8,128)(2,1)S(1)} %reshape.38), channel_id=1, source_target_pairs={{0,129},{1,128},{128,1},{129,0},{2,131},{3,130},{130,3},{131,2},{4... | collective-permute-start | bytes 540680 | tf_op jit(solution)/shard_map/ppermute | solution.py:46
  126.3 7.5 %collective-permute-start.22 = (bf16[352,256]{1,0:T(8,128)(2,1)S(1)}, bf16[352,256]{1,0:T(8,128)(2,1)S(1)}, u32[]{:S(2)}, u32[]{:S(2)}) collective-permute-start(bf16[352,256]{1,0:T(8,128)(2,1)S(1)} %reshape.38), channel_id=1, source_target_pairs={{0,128},{1,129},{128,0},{129,1},{2,130},{3,131},{130,2},{131,3},{4... | collective-permute-start | bytes 540680 | tf_op jit(solution)/shard_map/ppermute | solution.py:46
  126.5 7.9 %collective-permute-start.23 = (bf16[352,256]{1,0:T(8,128)(2,1)S(1)}, bf16[352,256]{1,0:T(8,128)(2,1)S(1)}, u32[]{:S(2)}, u32[]{:S(2)}) collective-permute-start(bf16[352,256]{1,0:T(8,128)(2,1)S(1)} %reshape.38), channel_id=1, source_target_pairs={{0,1},{1,0},{128,129},{129,128},{2,3},{3,2},{130,131},{131,130},{4... | collective-permute-start | bytes 540680 | tf_op jit(solution)/shard_map/ppermute | solution.py:46
  134.5 11.9 %collective-permute-start.24 = (bf16[384,256]{1,0:T(8,128)(2,1)S(1)}, bf16[384,256]{1,0:T(8,128)(2,1)S(1)}, u32[]{:S(2)}, u32[]{:S(2)}) collective-permute-start(bf16[384,256]{1,0:T(8,128)(2,1)S(1)} %pad_maximum_fusion.1.refs_0_), channel_id=1, source_target_pairs={{0,4},{4,0},{8,12},{12,8},{1,5},{5,1},{9,13},{13,9},{2,6},{6,2},{1... | collective-permute-start | bytes 589832 | tf_op jit(solution)/shard_map/ppermute | solution.py:419
  134.6 12.0 %collective-permute-start.25 = (bf16[384,256]{1,0:T(8,128)(2,1)S(1)}, bf16[384,256]{1,0:T(8,128)(2,1)S(1)}, u32[]{:S(2)}, u32[]{:S(2)}) collective-permute-start(bf16[384,256]{1,0:T(8,128)(2,1)S(1)} %pad_maximum_fusion.1.refs_0_), channel_id=1, source_target_pairs={{0,8},{4,12},{8,0},{12,4},{1,9},{5,13},{9,1},{13,5},{2,10},{6,14},... | collective-permute-start | bytes 589832 | tf_op jit(solution)/shard_map/ppermute | solution.py:419
  138.5 12.7 %collective-permute-start.26 = (bf16[384,256]{1,0:T(8,128)(2,1)S(1)}, bf16[384,256]{1,0:T(8,128)(2,1)S(1)}, u32[]{:S(2)}, u32[]{:S(2)}) collective-permute-start(bf16[384,256]{1,0:T(8,128)(2,1)S(1)} %pad_maximum_fusion.1.refs_0_), channel_id=1, source_target_pairs={{0,12},{4,8},{8,4},{12,0},{1,13},{5,9},{9,5},{13,1},{2,14},{6,10},... | collective-permute-start | bytes 589832 | tf_op jit(solution)/shard_map/ppermute | solution.py:419
  138.5 15.5 %collective-permute-start.27 = (bf16[384,256]{1,0:T(8,128)(2,1)S(1)}, bf16[384,256]{1,0:T(8,128)(2,1)S(1)}, u32[]{:S(2)}, u32[]{:S(2)}) collective-permute-start(bf16[384,256]{1,0:T(8,128)(2,1)S(1)} %pad_maximum_fusion.1.refs_0_), channel_id=1, source_target_pairs={{0,2},{2,0},{1,3},{3,1},{4,6},{6,4},{5,7},{7,5},{8,10},{10,8},{9,1... | collective-permute-start | bytes 589832 | tf_op jit(solution)/shard_map/ppermute | solution.py:420
  146.4 7.6 %collective-permute-start.28 = (bf16[384,256]{1,0:T(8,128)(2,1)S(1)}, bf16[384,256]{1,0:T(8,128)(2,1)S(1)}, u32[]{:S(2)}, u32[]{:S(2)}) collective-permute-start(bf16[384,256]{1,0:T(8,128)(2,1)S(1)} %collective-permute-done.24.refs_1_), channel_id=1, source_target_pairs={{0,2},{2,0},{1,3},{3,1},{4,6},{6,4},{5,7},{7,5},{8,10},{10,8},{9,1... | collective-permute-start | bytes 589832 | tf_op jit(solution)/shard_map/ppermute | solution.py:420
  146.6 7.4 %collective-permute-start.29 = (bf16[384,256]{1,0:T(8,128)(2,1)S(1)}, bf16[384,256]{1,0:T(8,128)(2,1)S(1)}, u32[]{:S(2)}, u32[]{:S(2)}) collective-permute-start(bf16[384,256]{1,0:T(8,128)(2,1)S(1)} %collective-permute-done.25.refs_2_), channel_id=1, source_target_pairs={{0,2},{2,0},{1,3},{3,1},{4,6},{6,4},{5,7},{7,5},{8,10},{10,8},{9,1... | collective-permute-start | bytes 589832 | tf_op jit(solution)/shard_map/ppermute | solution.py:420
  151.2 3.1 %collective-permute-start.30 = (bf16[384,256]{1,0:T(8,128)(2,1)S(1)}, bf16[384,256]{1,0:T(8,128)(2,1)S(1)}, u32[]{:S(2)}, u32[]{:S(2)}) collective-permute-start(bf16[384,256]{1,0:T(8,128)(2,1)S(1)} %collective-permute-done.26.refs_3_), channel_id=1, source_target_pairs={{0,2},{2,0},{1,3},{3,1},{4,6},{6,4},{5,7},{7,5},{8,10},{10,8},{9,1... | collective-permute-start | bytes 589832 | tf_op jit(solution)/shard_map/ppermute | solution.py:420
